TPU v7x, 32 devices: a whole 2x2x4 slice. The times are simulated.
32 devices in a mesh: groups: 2 (over y), pulse: 4 (over z), range: 2 (over x), sub: 2 (over core).
Axes of the slice: x: 2, y: 2, z: 4, core: 2. Of those that a mesh axis runs over, the one named last changes fastest.
Arguments:
- raw_echo: bfloat16 [2, 128, 16384], P(None, ('groups', 'pulse', 'sub'), 'range'), parts along dimension 1, may hold values from -6 to 6
- range_taps: bfloat16 [32, 512, 128], P('pulse'), may hold values from -0.25 to 0.25
- azim_taps: bfloat16 [128, 2048], P(('groups', 'pulse', 'sub')), parts along dimension 0, may hold values from -1 to 1
- tile_col: int32 [128, 1], P(('groups', 'pulse', 'sub')), parts along dimension 0, may hold values from 0 to 1; in each aligned block of 4 rows (0 to 3, 4 to 7, ...) at most 2 rows name the same one
Outputs:
- image: float32 [2, 8192, 4096], P(None, ('groups', 'pulse', 'range', 'sub')), parts along dimension 1
There are 2 independent parts, one for each index of `groups`. A program takes and returns all parts, laid end to end along the dimension named above; an argument that names none is the same for every part. Nothing has to cross between parts.
Inputs may be any that keep to these rules, and one draw needn't show every extreme that they name: `tile_col`: in each aligned block of 4 pulses no tile column is named by more than 2 pulses.
All inputs are finite; a program needn't handle non-finite values.
Results may differ from a plain program's by a relative error of at most 0.008.
Values may be sent and summed in bfloat16 or wider, within the bound.
No kernel may reach another device: no remote copies, remote signals or barrier semaphores. Data moves between devices by JAX's collectives and lax.ppermute only.
A program may use at most 64 MiB of HBM per device.

v0:
```python
import functools
import math

import jax
import jax.numpy as jnp
import numpy as np
from jax import lax
from jax.experimental import pallas as pl
from jax.experimental.pallas import tpu as pltpu
from jax.sharding import PartitionSpec as P


LANES = 128
F32 = jnp.float32
BF16 = jnp.bfloat16
VMEM = pl.BlockSpec(memory_space=pltpu.VMEM)
HELD = pl.BlockSpec(memory_space=pltpu.HBM)
NT = (((1,), (1,)), ((), ()))
NN = (((1,), (0,)), ((), ()))


def dot(a, b, dims=NN):
    return lax.dot_general(a, b, dims, preferred_element_type=F32)


def traded(block, axis, k):
    count = math.prod(lax.axis_size(a) for a in ((axis,) if isinstance(axis, str) else axis))
    return lax.ppermute(block, axis, [(i, i ^ k) for i in range(count)])


def near(*values):
    return [pltpu.with_memory_space_constraint(v, pltpu.VMEM) for v in values]


def far(*values):
    return [pltpu.with_memory_space_constraint(v, pltpu.HBM) for v in values]


def phasor(rows, cols, period, sign):
    turns = np.outer(rows, cols) % period
    angles = turns * (2.0 * math.pi / period)
    return np.cos(angles), sign * np.sin(angles)


def fourier(values, sign):
    count = len(values)
    if count == 1:
        return values
    even = fourier(values[0::2], sign)
    odd = fourier(values[1::2], sign)
    out = [None] * count
    for k in range(count // 2):
        er, ei = even[k]
        a, b = odd[k]
        angle = sign * 2.0 * math.pi * k / count
        if 4 * k == count:
            tr, ti = (-b, a) if sign > 0 else (b, -a)
        elif k == 0:
            tr, ti = a, b
        elif 8 * k == count:
            h = math.sqrt(0.5)
            tr, ti = ((a - b) * h, (a + b) * h) if sign > 0 else ((a + b) * h, (b - a) * h)
        elif 8 * k == 3 * count:
            h = math.sqrt(0.5)
            tr, ti = (-(a + b) * h, (a - b) * h) if sign > 0 else ((b - a) * h, -(a + b) * h)
        else:
            c, s = math.cos(angle), math.sin(angle)
            tr, ti = a * c - b * s, a * s + b * c
        out[k] = (er + tr, ei + ti)
        out[k + count // 2] = (er - tr, ei - ti)
    return out


def split_kernel(n_x, per, raw, taps, tile, *refs):
    outs = refs[:n_x]
    marked, held, lines, sent = refs[n_x:]
    my_x = lax.axis_index("range")
    copies = [pltpu.make_async_copy(raw.at[c], held.at[c], sent.at[c]) for c in range(2)]
    for copy in copies:
        copy.start()
    shard = raw.shape[1]
    tiles = raw.shape[2] // LANES
    width = taps.shape[1]
    row = lax.broadcasted_iota(jnp.int32, (per, LANES), 0)
    for k in range(n_x):
        rows = slice(k * per, (k + 1) * per)
        values = taps[:per, :].astype(F32)
        for x in range(1, n_x):
            pick = taps[x * per : (x + 1) * per, :].astype(F32)
            values = jnp.where((my_x ^ k) == x, pick, values)
        ids = jnp.zeros((per, LANES), jnp.int32)
        for p in range(per):
            ids = jnp.where(row == p, tile[0, (my_x ^ k) * per + p], ids)
        marked[rows, :width] = values.astype(BF16)
        marked[rows, width:] = ids.astype(F32).astype(BF16)
    for c in range(2):
        copies[c].wait()
        for t in range(tiles):
            lines[c, t * shard : (t + 1) * shard, :] = held[
                c, :, t * LANES : (t + 1) * LANES
            ].astype(F32)
        for k in range(n_x):
            for p in range(per):
                outs[k][c * tiles : (c + 1) * tiles, p * LANES : (p + 1) * LANES] = lines[
                    c, pl.ds((my_x ^ k) * per + p, tiles, stride=shard), :
                ].astype(BF16)


def ready_kernel(n_fixed, own, first, turn, *refs):
    fixed = refs[:n_fixed]
    part, rest, turned = refs[n_fixed : n_fixed + 3]
    brought = refs[n_fixed + 3 : 2 * n_fixed + 3]
    mine, sent = refs[2 * n_fixed + 3 :]
    my_x = lax.axis_index("range")
    copies = [
        pltpu.make_async_copy(first.at[my_x, 0], mine, sent.at[0]),
        pltpu.make_async_copy(first.at[my_x, pl.ds(1, rest.shape[0])], rest, sent.at[1]),
        pltpu.make_async_copy(turn.at[lax.axis_index("pulse")], turned, sent.at[2]),
    ]
    for i in range(n_fixed):
        copies.append(pltpu.make_async_copy(fixed[i], brought[i], sent.at[i + 3]))
    for copy in copies:
        copy.start()
    copies[0].wait()
    part[...] = dot(mine[...], own[...])
    for copy in copies[1:]:
        copy.wait()


def pulse_kernel(n_parts, n_z, per, *refs):
    parts = refs[: n_parts - 1]
    mixed, first, turn, second = refs[n_parts - 1 : n_parts + 3]
    outs = refs[n_parts + 3 :]
    my_z = lax.axis_index("pulse")
    mixed = mixed[...]
    for k, part in enumerate(parts):
        mixed = mixed + dot(first[k], part[...])
    half = mixed.shape[0] // 2
    band = LANES // n_z
    picks = []
    for k in range(n_z):
        for c in range(2):
            row = pl.multiple_of(c * LANES + (my_z ^ k) * band, band)
            picks.append(second[pl.ds(row, band), :])
    table = jnp.concatenate(picks, axis=0)
    tc, ts = turn[0], turn[1]
    for p in range(per):
        re = mixed[:half, p * LANES : (p + 1) * LANES]
        im = mixed[half:, p * LANES : (p + 1) * LANES]
        spun = jnp.concatenate([re * tc - im * ts, re * ts + im * tc], axis=1).astype(BF16)
        done = dot(table, spun, NT).astype(BF16)
        for k in range(n_z):
            outs[k][:, p * half : (p + 1) * half] = done[2 * band * k : 2 * band * (k + 1), :]


def line_kernel(n_z, per, blocks, quads, total_blocks, *refs):
    chunks = refs[:n_z]
    taps, turn, last = refs[n_z : n_z + 3]
    outs = refs[n_z + 3 : 2 * n_z + 3]
    bins, sums, rows = refs[2 * n_z + 3 :]
    my_z = lax.axis_index("pulse")
    band = blocks * quads
    pulses = n_z * per
    for k in range(n_z):
        for c in range(2):
            for p in range(per):
                at = ((c * n_z + k) * per + p) * band
                bins[at : at + band, :] = chunks[k][
                    c * band : (c + 1) * band, p * LANES : (p + 1) * LANES
                ].astype(F32)
    ky = []
    for b in range(blocks):
        lhs = jnp.concatenate(
            [bins[pl.ds(b * quads + q, 2 * pulses, stride=band), :].astype(BF16) for q in range(quads)],
            axis=1,
        )
        line = dot(lhs, taps[b])
        ky.append((line[:pulses], line[pulses:]))
    quarter = total_blocks // 4
    for y in range(quarter):
        classes = []
        for m in range(4):
            acc = None
            for b in range(m, blocks, 4):
                re, im = ky[b]
                angle = 2.0 * math.pi * (b * y % total_blocks) / total_blocks
                co, si = math.cos(angle), math.sin(angle)
                if b * y == 0:
                    term = (re, im)
                else:
                    term = (re * co - im * si, re * si + im * co)
                acc = term if acc is None else (acc[0] + term[0], acc[1] + term[1])
            if acc is None:
                acc = (jnp.zeros_like(ky[0][0]), jnp.zeros_like(ky[0][1]))
            classes.append(acc)
        for r, (re, im) in enumerate(fourier(classes, 1)):
            at = (y + r * quarter) * pulses
            sums[0, at : at + pulses, :] = re
            sums[1, at : at + pulses, :] = im
    fold = LANES // total_blocks
    tops = last.shape[0] // 2
    for m in range(pulses):
        gr = sums[0, pl.ds(m, total_blocks, stride=pulses), :]
        gi = sums[1, pl.ds(m, total_blocks, stride=pulses), :]
        spun = []
        for f in range(fold):
            tc = turn[0, f * total_blocks : (f + 1) * total_blocks, :]
            ts = turn[1, f * total_blocks : (f + 1) * total_blocks, :]
            spun.append(
                jnp.concatenate([gr * tc - gi * ts, gr * ts + gi * tc], axis=1).astype(BF16)
            )
        done = dot(last[...], jnp.concatenate(spun, axis=0), NT)
        for c in range(2):
            at = (c * pulses + m) * tops
            rows[at : at + tops, :] = done[c * tops : (c + 1) * tops, :]
    share = tops // n_z
    for k in range(n_z):
        for s in range(share):
            line = rows[pl.ds((my_z ^ k) * share + s, 2 * pulses, stride=tops), :]
            blocks_of = [
                line[c * pulses + (z ^ k) * per : c * pulses + (z ^ k) * per + per]
                for c in range(2)
                for z in range(n_z)
            ]
            outs[k][:, s * LANES : (s + 1) * LANES] = jnp.concatenate(blocks_of, axis=0).astype(BF16)


def fold_kernel(n_z, n_c, *refs):
    parts, outs, total = refs[:n_z], refs[n_z:-1], refs[-1]
    acc = parts[0][...].astype(F32)
    for part in parts[1:]:
        acc = acc + part[...].astype(F32)
    total[...] = acc.astype(BF16)
    mine = lax.axis_index("range") * n_c + lax.axis_index("sub")
    wide = outs[0].shape[1]
    for k, out in enumerate(outs):
        out[...] = total[:, pl.ds(pl.multiple_of((mine ^ k) * wide, wide), wide)]


def column_kernel(width, tile_cols, low, taps, table, turn, out, flipped, mixed):
    for t in range(taps.shape[1] // LANES):
        block = taps[:, t * LANES : (t + 1) * LANES].astype(F32)
        flipped[t * LANES : (t + 1) * LANES, :] = block.T
    tile = flipped[width : width + 1, :]
    highs = width // low
    high = table.shape[0] // 2
    for r in range(low):
        part = flipped[pl.ds(r, highs, stride=low), :]
        placed = [jnp.where(tile == float(s), part, 0.0) for s in range(tile_cols)]
        rhs = jnp.concatenate(placed, axis=0).astype(BF16)
        mixed[r] = dot(table[...], rhs)
    step = 16

    def rows(i, carry):
        y = pl.multiple_of(i * step, step)
        values = []
        tc = turn[0, pl.ds(y, step), :]
        ts = turn[1, pl.ds(y, step), :]
        for r in range(low):
            re = mixed[r, pl.ds(y, step), :]
            im = mixed[r, pl.ds(y + high, step), :]
            if r == 0:
                values.append((re, im))
                continue
            c, s = tc[:, r : r + 1], ts[:, r : r + 1]
            values.append((re * c - im * s, re * s + im * c))
        for d, (re, im) in enumerate(fourier(values, 1)):
            at = pl.multiple_of(d * high + y, step)
            out[pl.ds(at, step), :] = jnp.concatenate([re, im], axis=1).astype(BF16)
        return carry

    lax.fori_loop(0, high // step, rows, 0)


def factor(parts, n_z, n_x, n_c, per):
    pulses = n_z * per
    out = []
    for comp in range(2):
        for c in range(n_c):
            for z in range(n_z):
                for x in range(n_x):
                    at = comp * pulses + z * per
                    out.append(parts[x * n_c + c][at : at + per, :])
    return jnp.concatenate(out, axis=0)


def image_kernel(dims, step, *refs):
    n_z, n_x, n_c, per = dims
    count = n_x * n_c
    parts = [ref[...].astype(F32) for ref in refs[:count]]
    cols, out, held, sent = refs[count:]
    lines = factor(parts, n_z, n_x, n_c, per).T
    half = lines.shape[1] // 2
    re, im = lines[:, :half], lines[:, half:]
    rows = lines.shape[0]
    lhs = jnp.concatenate(
        [jnp.concatenate([re, -im], axis=1), jnp.concatenate([im, re], axis=1)], axis=0
    ).astype(BF16)
    copies = []
    for i in range(cols.shape[0] // step):
        done = dot(lhs, cols[i * step : (i + 1) * step, :], NT)
        at = pl.ds(i * step, step)
        held[0, :, at] = done[:rows]
        held[1, :, at] = done[rows:]
        copies.append(pltpu.make_async_copy(held.at[:, :, at], out.at[:, :, at], sent.at[i]))
        copies[-1].start()
    for copy in copies:
        copy.wait()


def image_plain(lhs, cols, out):
    rows = out.shape[1]
    done = dot(lhs[...], cols[...], NT)
    out[0] = done[:rows]
    out[1] = done[rows:]


def table_of(values, dtype=BF16):
    return jnp.asarray(np.asarray(values, np.float32), dtype)


def complex_left(c, s, scale=1.0):
    return np.block([[c, -s], [s, c]]) * scale


def program(raw_echo, range_taps, azim_taps, tile_col):
    n_x, n_z, n_c = lax.axis_size("range"), lax.axis_size("pulse"), lax.axis_size("sub")
    my_x, my_c = lax.axis_index("range"), lax.axis_index("sub")
    shard, part = raw_echo.shape[1:]
    per = shard // n_x
    samples = part * n_x
    blocks, block_bins, block_rows = range_taps.shape
    total_blocks = blocks * n_z
    grid = total_blocks * block_rows
    width = azim_taps.shape[1]
    tile_cols = grid // width
    quad = n_x * n_c
    out_rows = grid // (n_z * quad)
    pulses = n_z * per
    wide = out_rows % LANES == 0
    room = {}
    if wide:
        room = {"compiler_params": pltpu.CompilerParams(vmem_limit_bytes=24 << 20)}

    high = samples // LANES
    tiles = high // n_x
    n128 = np.arange(LANES)
    nh = np.arange(high)
    first = complex_left(*phasor(nh, nh, high, -1.0)).reshape(2 * high, 2, n_x, tiles)
    first = [first[:, :, [x ^ k for k in range(n_x)]].transpose(2, 0, 1, 3) for x in range(n_x)]
    first = table_of(np.stack(first).reshape(n_x, n_x, 2 * high, 2 * tiles))
    turn1 = table_of(np.stack(phasor(nh, n128, samples, -1.0)), F32)
    second = table_of(complex_left(*phasor(n128, n128, LANES, -1.0), 1.0 / math.sqrt(samples)))
    tops = grid // LANES
    shift = grid // n_z
    turn2 = np.stack([np.stack(phasor(n128, n128 + shift * z, grid, 1.0)) for z in range(n_z)])
    turn2 = table_of(turn2, F32)
    c, s = phasor(np.arange(tops), n128, tops, 1.0)
    last = table_of(complex_left(c, s, 1.0 / math.sqrt(grid)))
    low = 16
    tall = grid // low
    nt = np.arange(tall)
    c, s = phasor(nt, nt, tall, 1.0)
    table = table_of(np.concatenate([c, s], axis=0) / math.sqrt(grid))
    turn3 = table_of(np.stack(phasor(nt, np.arange(low), grid, 1.0)), F32)

    piece = pltpu.VMEM((2 * tiles, per * LANES), BF16)
    *pieces, marked = pl.pallas_call(
        functools.partial(split_kernel, n_x, per),
        in_specs=[HELD, VMEM, pl.BlockSpec(memory_space=pltpu.SMEM)],
        out_specs=[VMEM] * (n_x + 1),
        out_shape=[piece] * n_x + [pltpu.VMEM((shard, width + LANES), BF16)],
        scratch_shapes=[
            pltpu.VMEM(raw_echo.shape, BF16),
            pltpu.VMEM((2, tiles * shard, LANES), F32),
            pltpu.SemaphoreType.DMA((2,)),
        ],
        name="split",
        **room,
    )(*far(raw_echo, azim_taps), tile_col.T)
    parts = []
    for k in range(1, n_x):
        parts.append(traded(pieces[k], "range", k))

    everyone = marked
    for axis, count in (("pulse", n_z), ("sub", n_c)):
        k = 1
        while k < count:
            everyone = jnp.concatenate([everyone, traded(everyone, axis, k)], axis=0)
            k *= 2

    fixed = (turn1, second, last, range_taps, table, turn3)
    part1, rest, turn2, *brought = pl.pallas_call(
        functools.partial(ready_kernel, len(fixed)),
        in_specs=[VMEM] + [HELD] * (2 + len(fixed)),
        out_specs=[VMEM] * (3 + len(fixed)),
        out_shape=[
            pltpu.VMEM((2 * high, per * LANES), F32),
            pltpu.VMEM((max(n_x - 1, 1), 2 * high, 2 * tiles), BF16),
            pltpu.VMEM(turn2.shape[1:], F32),
        ]
        + [pltpu.VMEM(f.shape, f.dtype) for f in fixed],
        scratch_shapes=[
            pltpu.VMEM((2 * high, 2 * tiles), BF16),
            pltpu.SemaphoreType.DMA((3 + len(fixed),)),
        ],
        name="ready",
        **room,
    )(*near(pieces[0]), *far(first, turn2, *fixed))
    turn1, second, last, range_taps, table, turn3 = brought

    band = LANES // n_z
    chunk = pltpu.VMEM((2 * band, per * high), BF16)
    chunks = pl.pallas_call(
        functools.partial(pulse_kernel, n_x, n_z, per),
        in_specs=[VMEM] * (n_x + 3),
        out_specs=[VMEM] * n_z,
        out_shape=[chunk] * n_z,
        name="pulse_transform",
        **room,
    )(*near(*parts, part1, rest, turn1, second))
    moved = [chunks[0]]
    for k in range(1, n_z):
        moved.append(traded(chunks[k], "pulse", k))

    group = 64
    all_pulses = n_c * n_z * shard
    cuts = all_pulses // group
    scratch = [
        pltpu.VMEM((width + LANES, group), F32),
        pltpu.VMEM((low, 2 * tall, group), F32),
    ]
    make = functools.partial(column_kernel, width, tile_cols, low)
    if cuts == 1:
        cols = pl.pallas_call(
            make,
            in_specs=[VMEM] * 3,
            out_specs=VMEM,
            out_shape=pltpu.VMEM((grid, 2 * group), BF16),
            scratch_shapes=scratch,
            name="column_transform",
            **room,
        )(*near(everyone, table, turn3))
    else:
        cols = pl.pallas_call(
            make,
            grid=(cuts,),
            in_specs=[
                pl.BlockSpec((group, width + LANES), lambda i: (i, 0)),
                pl.BlockSpec((2 * tall, tall), lambda i: (0, 0)),
                pl.BlockSpec((2, tall, low), lambda i: (0, 0, 0)),
            ],
            out_specs=pl.BlockSpec((grid, 2 * group), lambda i: (0, i)),
            out_shape=jax.ShapeDtypeStruct((grid, 2 * all_pulses), BF16),
            scratch_shapes=scratch,
            name="column_transform",
        )(everyone, table, turn3)

    quads = block_bins // LANES
    lines = pl.pallas_call(
        functools.partial(line_kernel, n_z, per, blocks, quads, total_blocks),
        in_specs=[VMEM] * (n_z + 3),
        out_specs=[VMEM] * n_z,
        out_shape=[pltpu.VMEM((2 * pulses, grid // n_z), BF16)] * n_z,
        scratch_shapes=[
            pltpu.VMEM((2 * pulses * blocks * quads, LANES), F32),
            pltpu.VMEM((2, total_blocks * pulses, LANES), F32),
            pltpu.VMEM((2 * pulses * tops, LANES), F32),
        ],
        name="line_transform",
        **room,
    )(*near(*moved, range_taps, turn2, last))
    moved = [lines[0]]
    for k in range(1, n_z):
        moved.append(traded(lines[k], "pulse", k))
    if wide:
        pieces = pl.pallas_call(
            functools.partial(fold_kernel, n_z, n_c),
            in_specs=[VMEM] * n_z,
            out_specs=[VMEM] * quad,
            out_shape=[pltpu.VMEM((2 * pulses, out_rows), BF16)] * quad,
            scratch_shapes=[pltpu.VMEM((2 * pulses, grid // n_z), BF16)],
            name="fold",
            **room,
        )(*near(*moved))
    else:
        acc = sum(m.astype(F32) for m in moved).astype(BF16)
        mine = my_x * n_c + my_c
        pieces = [
            lax.dynamic_slice_in_dim(acc, (mine ^ k) * out_rows, out_rows, 1)
            for k in range(quad)
        ]
    parts = [pieces[0]]
    for k in range(1, quad):
        parts.append(traded(pieces[k], ("range", "sub"), k))

    wide_x = 512
    depth = 2 * all_pulses
    out_shape = jax.ShapeDtypeStruct((2, out_rows, grid), F32)
    if cuts == 1 and wide:
        return pl.pallas_call(
            functools.partial(image_kernel, (n_z, n_x, n_c, per), wide_x),
            in_specs=[VMEM] * (quad + 1),
            out_specs=HELD,
            out_shape=out_shape,
            scratch_shapes=[
                pltpu.VMEM((2, out_rows, grid), F32),
                pltpu.SemaphoreType.DMA((grid // wide_x,)),
            ],
            name="image",
            **room,
        )(*near(*parts, cols))
    lines = factor([p.astype(F32) for p in parts], n_z, n_x, n_c, per).T
    re = lines[:, :all_pulses].reshape(out_rows, cuts, 1, group)
    im = lines[:, all_pulses:].reshape(out_rows, cuts, 1, group)
    lhs = jnp.stack(
        [jnp.concatenate([re, -im], axis=2), jnp.concatenate([im, re], axis=2)]
    ).reshape(2 * out_rows, depth).astype(BF16)
    return pl.pallas_call(
        image_plain,
        grid=(grid // wide_x,),
        in_specs=[
            pl.BlockSpec(lhs.shape, lambda i: (0, 0)),
            pl.BlockSpec((wide_x, depth), lambda i: (i, 0)),
        ],
        out_specs=pl.BlockSpec((2, out_rows, wide_x), lambda i: (0, 0, i)),
        out_shape=out_shape,
        name="image",
    )(lhs, cols)


def solution(mesh):
    placed = (
        P(None, ("groups", "pulse", "sub"), "range"),
        P("pulse", None, None),
        P(("groups", "pulse", "sub"), None),
        P(("groups", "pulse", "sub"), None),
    )
    return jax.shard_map(
        program,
        mesh=mesh,
        in_specs=placed,
        out_specs=P(None, ("groups", "pulse", "range", "sub"), None),
        check_vma=False,
    )
```

profile of v0, /device:TPU:0, one launch (start us, length us, event | category | flops | bytes accessed | tf_op | source)
XLA Modules:
  0.0 48.3 jit_solution(8276947734568852193)
XLA Ops:
  0.0 0.7 %copy-done = s32[8,1]{0,1:T(1,128)S(1)} copy-done((s32[8,1]{0,1:T(1,128)S(1)}, s32[8,1]{0,1:T(1,128)}, u32[]{:S(2)}) %copy-start) | copy-done | bytes 56
  0.7 1.8 %split.1 = (bf16[128,512]{1,0:T(8,128)(2,1)S(1)}, bf16[128,512]{1,0:T(8,128)(2,1)S(1)}, bf16[8,2176]{1,0:T(8,128)(2,1)S(1)}) custom-call(bf16[2,8,8192]{2,1,0:T(8,128)(2,1)} %raw.1, bf16[8,2048]{1,0:T(8,128)(2,1)} %taps.1, s32[1,8]{1,0:T(1,128)S(1)} %bitcast.1), custom_call_target="tpu_custom_call" | custom-call | tf_op jit(solution)/shard_map/split/pallas_call | solution.py:368
  2.5 3.1 %collective-permute-start.10 = (bf16[8,2176]{1,0:T(8,128)(2,1)S(1)}, bf16[8,2176]{1,0:T(8,128)(2,1)S(1)}, u32[]{:S(2)}, u32[]{:S(2)}) collective-permute-start(bf16[8,2176]{1,0:T(8,128)(2,1)S(1)} %get-tuple-element.50), channel_id=1, source_target_pairs={{0,4},{4,0},{8,12},{12,8},{1,5},{5,1},{9,13},{13,9},{2,6},{6,2},{1... | collective-permute-start | bytes 104456 | tf_op jit(solution)/shard_map/ppermute | solution.py:28
  5.6 1.9 %collective-permute-done.10 = bf16[8,2176]{1,0:T(8,128)(2,1)S(1)} collective-permute-done((bf16[8,2176]{1,0:T(8,128)(2,1)S(1)}, bf16[8,2176]{1,0:T(8,128)(2,1)S(1)}, u32[]{:S(2)}, u32[]{:S(2)}) %collective-permute-start.10) | collective-permute-done | bytes 34848 | tf_op jit(solution)/shard_map/ppermute | solution.py:28
  7.6 3.0 %collective-permute-start.11 = (bf16[16,2176]{1,0:T(8,128)(2,1)S(1)}, bf16[16,2176]{1,0:T(8,128)(2,1)S(1)}, u32[]{:S(2)}, u32[]{:S(2)}) collective-permute-start(bf16[16,2176]{1,0:T(8,128)(2,1)S(1)} %pad_maximum_fusion.2), channel_id=1, source_target_pairs={{0,8},{4,12},{8,0},{12,4},{1,9},{5,13},{9,1},{13,5},{2,10},{6,14},... | collective-permute-start | bytes 208904 | tf_op jit(solution)/shard_map/ppermute | solution.py:28
  10.6 1.5 %collective-permute-start = (bf16[128,512]{1,0:T(8,128)(2,1)S(1)}, bf16[128,512]{1,0:T(8,128)(2,1)S(1)}, u32[]{:S(2)}, u32[]{:S(2)}) collective-permute-start(bf16[128,512]{1,0:T(8,128)(2,1)S(1)} %get-tuple-element.29), channel_id=1, source_target_pairs={{0,2},{2,0},{1,3},{3,1},{4,6},{6,4},{5,7},{7,5},{8,10},{10,8},{9,1... | collective-permute-start | bytes 393224 | tf_op jit(solution)/shard_map/ppermute | solution.py:28
  12.1 0.8 %collective-permute-done.11 = bf16[16,2176]{1,0:T(8,128)(2,1)S(1)} collective-permute-done((bf16[16,2176]{1,0:T(8,128)(2,1)S(1)}, bf16[16,2176]{1,0:T(8,128)(2,1)S(1)}, u32[]{:S(2)}, u32[]{:S(2)}) %collective-permute-start.11) | collective-permute-done | bytes 69664 | tf_op jit(solution)/shard_map/ppermute | solution.py:28
  12.9 0.1 collective-permute-start.12
  13.0 1.7 %ready.1 = (f32[256,512]{1,0:T(8,128)S(1)}, bf16[1,256,128]{2,1,0:T(8,128)(2,1)S(1)}, f32[2,128,128]{2,1,0:T(8,128)S(1)}, f32[2,128,128]{2,1,0:T(8,128)S(1)}, bf...) custom-call(bf16[128,512]{1,0:T(8,128)(2,1)S(1)} %get-tuple-element., ...), custom_call_target="tpu_custom_call" | custom-call | tf_op jit(solution)/shard_map/ready/pallas_call | solution.py:393
  14.7 0.9 %collective-permute-done.refs_0_ = bf16[128,512]{1,0:T(8,128)(2,1)S(1)} collective-permute-done((bf16[128,512]{1,0:T(8,128)(2,1)S(1)}, bf16[128,512]{1,0:T(8,128)(2,1)S(1)}, u32[]{:S(2)}, u32[]{:S(2)}) %collective-permute-start) | collective-permute-done | bytes 131104 | tf_op jit(solution)/shard_map/ppermute | solution.py:28
  15.6 0.5 %pulse_transform.1 = (bf16[64,512]{1,0:T(8,128)(2,1)S(1)}, bf16[64,512]{1,0:T(8,128)(2,1)S(1)}, bf16[64,512]{1,0:T(8,128)(2,1)S(1)}, bf16[64,512]{1,0:T(8,128)(2,1)S(1)}) custom-call(bf16[128,512]{1,0:T(8,128)(2,1)S(1)} %collective-permute-done.refs_0_, f32[256,512]{1,0:T(8,128)S(1)} %get-tuple-element.31.refs_1_, ...), custom_call_target="tpu_custom_call" | custom-call | tf_op jit(solution)/shard_map/pulse_transform/pallas_call | solution.py:414
  16.0 1.6 %collective-permute-start.1 = (bf16[64,512]{1,0:T(8,128)(2,1)S(1)}, bf16[64,512]{1,0:T(8,128)(2,1)S(1)}, u32[]{:S(2)}, u32[]{:S(2)}) collective-permute-start(bf16[64,512]{1,0:T(8,128)(2,1)S(1)} %get-tuple-element.36), channel_id=1, source_target_pairs={{0,4},{4,0},{8,12},{12,8},{1,5},{5,1},{9,13},{13,9},{2,6},{6,2},{1... | collective-permute-start | bytes 196616 | tf_op jit(solution)/shard_map/ppermute | solution.py:28
  17.7 2.7 %collective-permute-start.2 = (bf16[64,512]{1,0:T(8,128)(2,1)S(1)}, bf16[64,512]{1,0:T(8,128)(2,1)S(1)}, u32[]{:S(2)}, u32[]{:S(2)}) collective-permute-start(bf16[64,512]{1,0:T(8,128)(2,1)S(1)} %get-tuple-element.37), channel_id=1, source_target_pairs={{0,8},{4,12},{8,0},{12,4},{1,9},{5,13},{9,1},{13,5},{2,10},{6,14},... | collective-permute-start | bytes 196616 | tf_op jit(solution)/shard_map/ppermute | solution.py:28
  20.4 0.1 collective-permute-start.3
  20.5 0.0 collective-permute-done.1.refs_1_
  20.5 4.1 %collective-permute-done.2.refs_2_ = bf16[64,512]{1,0:T(8,128)(2,1)S(1)} collective-permute-done((bf16[64,512]{1,0:T(8,128)(2,1)S(1)}, bf16[64,512]{1,0:T(8,128)(2,1)S(1)}, u32[]{:S(2)}, u32[]{:S(2)}) %collective-permute-start.2) | collective-permute-done | bytes 65568 | tf_op jit(solution)/shard_map/ppermute | solution.py:28
  24.6 1.9 %collective-permute-done.3.refs_3_ = bf16[64,512]{1,0:T(8,128)(2,1)S(1)} collective-permute-done((bf16[64,512]{1,0:T(8,128)(2,1)S(1)}, bf16[64,512]{1,0:T(8,128)(2,1)S(1)}, u32[]{:S(2)}, u32[]{:S(2)}) %collective-permute-start.3) | collective-permute-done | bytes 65568 | tf_op jit(solution)/shard_map/ppermute | solution.py:28
  26.5 1.4 %line_transform.1 = (bf16[32,1024]{1,0:T(8,128)(2,1)S(1)}, bf16[32,1024]{1,0:T(8,128)(2,1)S(1)}, bf16[32,1024]{1,0:T(8,128)(2,1)S(1)}, bf16[32,1024]{1,0:T(8,128)(2,1)S(1)}) custom-call(bf16[64,512]{1,0:T(8,128)(2,1)S(1)} %get-tuple-element.35.refs_0_, bf16[64,512]{1,0:T(8,128)(2,1)S(1)} %collective-permute-done.1.refs_1_, ...), custom_call_target="tpu_custom_call" | custom-call | tf_op jit(solution)/shard_map/line_transform/pallas_call | solution.py:460
  27.9 1.2 %collective-permute-start.4 = (bf16[32,1024]{1,0:T(8,128)(2,1)S(1)}, bf16[32,1024]{1,0:T(8,128)(2,1)S(1)}, u32[]{:S(2)}, u32[]{:S(2)}) collective-permute-start(bf16[32,1024]{1,0:T(8,128)(2,1)S(1)} %get-tuple-element.43), channel_id=1, source_target_pairs={{0,4},{4,0},{8,12},{12,8},{1,5},{5,1},{9,13},{13,9},{2,6},{6,2},{1... | collective-permute-start | bytes 196616 | tf_op jit(solution)/shard_map/ppermute | solution.py:28
  29.1 1.5 %collective-permute-start.5 = (bf16[32,1024]{1,0:T(8,128)(2,1)S(1)}, bf16[32,1024]{1,0:T(8,128)(2,1)S(1)}, u32[]{:S(2)}, u32[]{:S(2)}) collective-permute-start(bf16[32,1024]{1,0:T(8,128)(2,1)S(1)} %get-tuple-element.44), channel_id=1, source_target_pairs={{0,8},{4,12},{8,0},{12,4},{1,9},{5,13},{9,1},{13,5},{2,10},{6,14},... | collective-permute-start | bytes 196616 | tf_op jit(solution)/shard_map/ppermute | solution.py:28
  30.7 1.7 %collective-permute-start.6 = (bf16[32,1024]{1,0:T(8,128)(2,1)S(1)}, bf16[32,1024]{1,0:T(8,128)(2,1)S(1)}, u32[]{:S(2)}, u32[]{:S(2)}) collective-permute-start(bf16[32,1024]{1,0:T(8,128)(2,1)S(1)} %get-tuple-element.45), channel_id=1, source_target_pairs={{0,12},{4,8},{8,4},{12,0},{1,13},{5,9},{9,5},{13,1},{2,14},{6,10},... | collective-permute-start | bytes 196616 | tf_op jit(solution)/shard_map/ppermute | solution.py:28
  32.4 4.7 %collective-permute-done.5.refs_2_ = bf16[32,1024]{1,0:T(8,128)(2,1)S(1)} collective-permute-done((bf16[32,1024]{1,0:T(8,128)(2,1)S(1)}, bf16[32,1024]{1,0:T(8,128)(2,1)S(1)}, u32[]{:S(2)}, u32[]{:S(2)}) %collective-permute-start.5) | collective-permute-done | bytes 65568 | tf_op jit(solution)/shard_map/ppermute | solution.py:28
  37.1 0.0 collective-permute-done.6.refs_3_
  37.1 0.1 fold.1
  37.1 0.1 collective-permute-start.7
  37.2 1.5 %collective-permute-start.8 = (bf16[32,256]{1,0:T(8,128)(2,1)S(1)}, bf16[32,256]{1,0:T(8,128)(2,1)S(1)}, u32[]{:S(2)}, u32[]{:S(2)}) collective-permute-start(bf16[32,256]{1,0:T(8,128)(2,1)S(1)} %get-tuple-element.48), channel_id=1, source_target_pairs={{0,2},{1,3},{2,0},{3,1},{4,6},{5,7},{6,4},{7,5},{8,10},{9,11},{10,... | collective-permute-start | bytes 49160 | tf_op jit(solution)/shard_map/ppermute | solution.py:28
  38.7 0.3 collective-permute-start.9
  39.0 0.0 collective-permute-done.12
  39.1 5.5 %column_transform.1.refs_4_ = bf16[4096,128]{1,0:T(8,128)(2,1)S(1)} custom-call(bf16[64,2176]{1,0:T(8,128)(2,1)S(1)} %pad_maximum_fusion.taps, bf16[512,256]{1,0:T(8,128)(2,1)S(1)} %get-tuple-element.51.table, f32[2,256,16]{2,1,0:T(8,128)S(1)} %get-tuple-element.52.turn), custom_call_target="tpu_custom_call" | custom-call | tf_op jit(solution)/shard_map/column_transform/pallas_call | solution.py:435
  44.6 0.0 collective-permute-done.7.refs_1_
  44.6 0.0 collective-permute-done.9.refs_3_
  44.6 3.7 %image.1 = f32[2,256,4096]{2,1,0:T(8,128)} custom-call(bf16[32,256]{1,0:T(8,128)(2,1)S(1)} %get-tuple-element.46.refs_0_, bf16[32,256]{1,0:T(8,128)(2,1)S(1)} %collective-permute-done.7.refs_1_, bf16[32,256]{1,0:T(8,128)(2,1)S(1)} %collective-permute-done.8.refs_2_, bf16[32,256]{1,0:T(8,128)(2,1)S(1)} %collective-permute-done.9.refs_3_, ...), custom_call_target="tpu_custom_call" | custom-call | tf_op jit(solution)/shard_map/image/pallas_call | solution.py:501
  (6 shorter events, 0.0 us)
Async XLA Ops:
  0.0 0.7 %copy-start = (s32[8,1]{0,1:T(1,128)S(1)}, s32[8,1]{0,1:T(1,128)}, u32[]{:S(2)}) copy-start(s32[8,1]{0,1:T(1,128)} %param.14) | copy-start | bytes 100
  2.5 5.0 %collective-permute-start.10 = (bf16[8,2176]{1,0:T(8,128)(2,1)S(1)}, bf16[8,2176]{1,0:T(8,128)(2,1)S(1)}, u32[]{:S(2)}, u32[]{:S(2)}) collective-permute-start(bf16[8,2176]{1,0:T(8,128)(2,1)S(1)} %get-tuple-element.50), channel_id=1, source_target_pairs={{0,4},{4,0},{8,12},{12,8},{1,5},{5,1},{9,13},{13,9},{2,6},{6,2},{1... | collective-permute-start | bytes 104456 | tf_op jit(solution)/shard_map/ppermute | solution.py:28
  7.6 5.3 %collective-permute-start.11 = (bf16[16,2176]{1,0:T(8,128)(2,1)S(1)}, bf16[16,2176]{1,0:T(8,128)(2,1)S(1)}, u32[]{:S(2)}, u32[]{:S(2)}) collective-permute-start(bf16[16,2176]{1,0:T(8,128)(2,1)S(1)} %pad_maximum_fusion.2), channel_id=1, source_target_pairs={{0,8},{4,12},{8,0},{12,4},{1,9},{5,13},{9,1},{13,5},{2,10},{6,14},... | collective-permute-start | bytes 208904 | tf_op jit(solution)/shard_map/ppermute | solution.py:28
  10.6 5.0 %collective-permute-start = (bf16[128,512]{1,0:T(8,128)(2,1)S(1)}, bf16[128,512]{1,0:T(8,128)(2,1)S(1)}, u32[]{:S(2)}, u32[]{:S(2)}) collective-permute-start(bf16[128,512]{1,0:T(8,128)(2,1)S(1)} %get-tuple-element.29), channel_id=1, source_target_pairs={{0,2},{2,0},{1,3},{3,1},{4,6},{6,4},{5,7},{7,5},{8,10},{10,8},{9,1... | collective-permute-start | bytes 393224 | tf_op jit(solution)/shard_map/ppermute | solution.py:28
  12.9 26.2 %collective-permute-start.12 = (bf16[32,2176]{1,0:T(8,128)(2,1)S(1)}, bf16[32,2176]{1,0:T(8,128)(2,1)S(1)}, u32[]{:S(2)}, u32[]{:S(2)}) collective-permute-start(bf16[32,2176]{1,0:T(8,128)(2,1)S(1)} %pad_maximum_fusion.1), channel_id=1, source_target_pairs={{0,1},{1,0},{2,3},{3,2},{4,5},{5,4},{6,7},{7,6},{8,9},{9,8},{10,11... | collective-permute-start | bytes 417800 | tf_op jit(solution)/shard_map/ppermute | solution.py:28
  16.0 4.5 %collective-permute-start.1 = (bf16[64,512]{1,0:T(8,128)(2,1)S(1)}, bf16[64,512]{1,0:T(8,128)(2,1)S(1)}, u32[]{:S(2)}, u32[]{:S(2)}) collective-permute-start(bf16[64,512]{1,0:T(8,128)(2,1)S(1)} %get-tuple-element.36), channel_id=1, source_target_pairs={{0,4},{4,0},{8,12},{12,8},{1,5},{5,1},{9,13},{13,9},{2,6},{6,2},{1... | collective-permute-start | bytes 196616 | tf_op jit(solution)/shard_map/ppermute | solution.py:28
  17.7 6.9 %collective-permute-start.2 = (bf16[64,512]{1,0:T(8,128)(2,1)S(1)}, bf16[64,512]{1,0:T(8,128)(2,1)S(1)}, u32[]{:S(2)}, u32[]{:S(2)}) collective-permute-start(bf16[64,512]{1,0:T(8,128)(2,1)S(1)} %get-tuple-element.37), channel_id=1, source_target_pairs={{0,8},{4,12},{8,0},{12,4},{1,9},{5,13},{9,1},{13,5},{2,10},{6,14},... | collective-permute-start | bytes 196616 | tf_op jit(solution)/shard_map/ppermute | solution.py:28
  20.4 6.1 %collective-permute-start.3 = (bf16[64,512]{1,0:T(8,128)(2,1)S(1)}, bf16[64,512]{1,0:T(8,128)(2,1)S(1)}, u32[]{:S(2)}, u32[]{:S(2)}) collective-permute-start(bf16[64,512]{1,0:T(8,128)(2,1)S(1)} %get-tuple-element.38), channel_id=1, source_target_pairs={{0,12},{4,8},{8,4},{12,0},{1,13},{5,9},{9,5},{13,1},{2,14},{6,10},... | collective-permute-start | bytes 196616 | tf_op jit(solution)/shard_map/ppermute | solution.py:28
  27.9 4.5 %collective-permute-start.4 = (bf16[32,1024]{1,0:T(8,128)(2,1)S(1)}, bf16[32,1024]{1,0:T(8,128)(2,1)S(1)}, u32[]{:S(2)}, u32[]{:S(2)}) collective-permute-start(bf16[32,1024]{1,0:T(8,128)(2,1)S(1)} %get-tuple-element.43), channel_id=1, source_target_pairs={{0,4},{4,0},{8,12},{12,8},{1,5},{5,1},{9,13},{13,9},{2,6},{6,2},{1... | collective-permute-start | bytes 196616 | tf_op jit(solution)/shard_map/ppermute | solution.py:28
  29.1 7.9 %collective-permute-start.5 = (bf16[32,1024]{1,0:T(8,128)(2,1)S(1)}, bf16[32,1024]{1,0:T(8,128)(2,1)S(1)}, u32[]{:S(2)}, u32[]{:S(2)}) collective-permute-start(bf16[32,1024]{1,0:T(8,128)(2,1)S(1)} %get-tuple-element.44), channel_id=1, source_target_pairs={{0,8},{4,12},{8,0},{12,4},{1,9},{5,13},{9,1},{13,5},{2,10},{6,14},... | collective-permute-start | bytes 196616 | tf_op jit(solution)/shard_map/ppermute | solution.py:28
  30.7 6.4 %collective-permute-start.6 = (bf16[32,1024]{1,0:T(8,128)(2,1)S(1)}, bf16[32,1024]{1,0:T(8,128)(2,1)S(1)}, u32[]{:S(2)}, u32[]{:S(2)}) collective-permute-start(bf16[32,1024]{1,0:T(8,128)(2,1)S(1)} %get-tuple-element.45), channel_id=1, source_target_pairs={{0,12},{4,8},{8,4},{12,0},{1,13},{5,9},{9,5},{13,1},{2,14},{6,10},... | collective-permute-start | bytes 196616 | tf_op jit(solution)/shard_map/ppermute | solution.py:28
  37.1 7.5 %collective-permute-start.7 = (bf16[32,256]{1,0:T(8,128)(2,1)S(1)}, bf16[32,256]{1,0:T(8,128)(2,1)S(1)}, u32[]{:S(2)}, u32[]{:S(2)}) collective-permute-start(bf16[32,256]{1,0:T(8,128)(2,1)S(1)} %get-tuple-element.47), channel_id=1, source_target_pairs={{0,1},{1,0},{2,3},{3,2},{4,5},{5,4},{6,7},{7,6},{8,9},{9,8},{10,11... | collective-permute-start | bytes 49160 | tf_op jit(solution)/shard_map/ppermute | solution.py:28
  37.2 7.4 %collective-permute-start.8 = (bf16[32,256]{1,0:T(8,128)(2,1)S(1)}, bf16[32,256]{1,0:T(8,128)(2,1)S(1)}, u32[]{:S(2)}, u32[]{:S(2)}) collective-permute-start(bf16[32,256]{1,0:T(8,128)(2,1)S(1)} %get-tuple-element.48), channel_id=1, source_target_pairs={{0,2},{1,3},{2,0},{3,1},{4,6},{5,7},{6,4},{7,5},{8,10},{9,11},{10,... | collective-permute-start | bytes 49160 | tf_op jit(solution)/shard_map/ppermute | solution.py:28
  38.7 5.9 %collective-permute-start.9 = (bf16[32,256]{1,0:T(8,128)(2,1)S(1)}, bf16[32,256]{1,0:T(8,128)(2,1)S(1)}, u32[]{:S(2)}, u32[]{:S(2)}) collective-permute-start(bf16[32,256]{1,0:T(8,128)(2,1)S(1)} %get-tuple-element.49), channel_id=1, source_target_pairs={{0,3},{1,2},{2,1},{3,0},{4,7},{5,6},{6,5},{7,4},{8,11},{9,10},{10,... | collective-permute-start | bytes 49160 | tf_op jit(solution)/shard_map/ppermute | solution.py:28
where the time goes:
time: 48.6 us; the launch traced here: 48.3 us
  starting transfers between devices  18.5 us (38%)
  Pallas kernels  14.8 us (30%)
  waiting for transfers between devices  14.2 us (29%)
  local copies, waits for them, and re-layouts  0.65 us (1%)
    ppermute x13, starting transfers between devices, traded(): return lax.ppermute(block, axis, [(i, i ^ k) for i in range(count)])  18.5 us
    ppermute x13, waiting for transfers between devices, traded(): return lax.ppermute(block, axis, [(i, i ^ k) for i in range(count)])  14.2 us
    pallas_call x1, Pallas kernels, program(): pl.pallas_call(make, in_specs=[VMEM] * 3, out_specs=VMEM, out_shape=pltpu...  5.51 us
    pallas_call x1, Pallas kernels, program(): pl.pallas_call(functools.partial(image_kernel, (n_z, n_x, n_c, per), wide...  3.71 us
    pallas_call x1, Pallas kernels, program(): pl.pallas_call(functools.partial(split_kernel, n_x, per), in_specs=[HELD,...  1.85 us
    pallas_call x1, Pallas kernels, program(): pl.pallas_call(functools.partial(ready_kernel, len(fixed)), in_specs=[VME...  1.72 us
    pallas_call x1, Pallas kernels, program(): pl.pallas_call(functools.partial(line_kernel, n_z, per, blocks, quads, to...  1.44 us
  transfers between devices with their start and end apart: 13, of which 6 were waited for; matrix products, arithmetic and copies ran while one was open for 0% of the time, Pallas kernels for 19%

commit v1 on v0

--- a/solution.py
+++ b/solution.py
@@ -40,6 +40,18 @@
     turns = np.outer(rows, cols) % period
     angles = turns * (2.0 * math.pi / period)
     return np.cos(angles), sign * np.sin(angles)
+
+
+def add(a, b):
+    return b if a is None else a if b is None else a + b
+
+
+def sub(a, b):
+    return a if b is None else -b if a is None else a - b
+
+
+def scaled(a, factor):
+    return None if a is None else a * factor
 
 
 def fourier(values, sign):
@@ -52,35 +64,42 @@
     for k in range(count // 2):
         er, ei = even[k]
         a, b = odd[k]
-        angle = sign * 2.0 * math.pi * k / count
         if 4 * k == count:
-            tr, ti = (-b, a) if sign > 0 else (b, -a)
+            tr, ti = (sub(None, b), a) if sign > 0 else (b, sub(None, a))
         elif k == 0:
             tr, ti = a, b
-        elif 8 * k == count:
+        elif 8 * k in (count, 3 * count):
             h = math.sqrt(0.5)
-            tr, ti = ((a - b) * h, (a + b) * h) if sign > 0 else ((a + b) * h, (b - a) * h)
-        elif 8 * k == 3 * count:
-            h = math.sqrt(0.5)
-            tr, ti = (-(a + b) * h, (a - b) * h) if sign > 0 else ((b - a) * h, -(a + b) * h)
+            c = h if 8 * k == count else -h
+            if sign < 0:
+                b, a, c = a, b, c
+                tr, ti = (sub(scaled(b, c), scaled(a, -h)), sub(scaled(a, c), scaled(b, h)))
+            else:
+                tr, ti = (sub(scaled(a, c), scaled(b, h)), add(scaled(a, h), scaled(b, c)))
         else:
+            angle = sign * 2.0 * math.pi * k / count
             c, s = math.cos(angle), math.sin(angle)
-            tr, ti = a * c - b * s, a * s + b * c
-        out[k] = (er + tr, ei + ti)
-        out[k + count // 2] = (er - tr, ei - ti)
+            tr = sub(scaled(a, c), scaled(b, s))
+            ti = add(scaled(a, s), scaled(b, c))
+        out[k] = (add(er, tr), add(ei, ti))
+        out[k + count // 2] = (sub(er, tr), sub(ei, ti))
     return out
 
 
-def split_kernel(n_x, per, raw, taps, tile, *refs):
+def split_kernel(n_x, per, raw, taps_in, tile_in, *refs):
     outs = refs[:n_x]
-    marked, held, lines, sent = refs[n_x:]
+    marked, held, taps, tile, lines, sent = refs[n_x:]
     my_x = lax.axis_index("range")
     copies = [pltpu.make_async_copy(raw.at[c], held.at[c], sent.at[c]) for c in range(2)]
+    copies.append(pltpu.make_async_copy(taps_in, taps, sent.at[2]))
+    copies.append(pltpu.make_async_copy(tile_in, tile, sent.at[3]))
     for copy in copies:
         copy.start()
     shard = raw.shape[1]
     tiles = raw.shape[2] // LANES
     width = taps.shape[1]
+    copies[2].wait()
+    copies[3].wait()
     row = lax.broadcasted_iota(jnp.int32, (per, LANES), 0)
     for k in range(n_x):
         rows = slice(k * per, (k + 1) * per)
@@ -237,39 +256,39 @@
         out[...] = total[:, pl.ds(pl.multiple_of((mine ^ k) * wide, wide), wide)]
 
 
-def column_kernel(width, tile_cols, low, taps, table, turn, out, flipped, mixed):
-    for t in range(taps.shape[1] // LANES):
-        block = taps[:, t * LANES : (t + 1) * LANES].astype(F32)
-        flipped[t * LANES : (t + 1) * LANES, :] = block.T
-    tile = flipped[width : width + 1, :]
-    highs = width // low
-    high = table.shape[0] // 2
-    for r in range(low):
-        part = flipped[pl.ds(r, highs, stride=low), :]
-        placed = [jnp.where(tile == float(s), part, 0.0) for s in range(tile_cols)]
-        rhs = jnp.concatenate(placed, axis=0).astype(BF16)
-        mixed[r] = dot(table[...], rhs)
+def column_kernel(width, tile_cols, taps, table, turn, out, mixed, spread):
+    pulses = taps.shape[0]
+    low = mixed.shape[0]
+    high = out.shape[0] // low
+    steps = width // high
     step = 16
-
-    def rows(i, carry):
-        y = pl.multiple_of(i * step, step)
-        values = []
-        tc = turn[0, pl.ds(y, step), :]
-        ts = turn[1, pl.ds(y, step), :]
-        for r in range(low):
-            re = mixed[r, pl.ds(y, step), :]
-            im = mixed[r, pl.ds(y + high, step), :]
-            if r == 0:
-                values.append((re, im))
-                continue
-            c, s = tc[:, r : r + 1], ts[:, r : r + 1]
-            values.append((re * c - im * s, re * s + im * c))
-        for d, (re, im) in enumerate(fourier(values, 1)):
-            at = pl.multiple_of(d * high + y, step)
-            out[pl.ds(at, step), :] = jnp.concatenate([re, im], axis=1).astype(BF16)
-        return carry
-
-    lax.fori_loop(0, high // step, rows, 0)
+    for v in range(high // LANES):
+        for r in range(0, pulses, step):
+            tile = taps[r : r + step, width:].astype(F32)
+            inside = [tile == float(t) for t in range(tile_cols)]
+            values = []
+            for t in range(tile_cols):
+                for i in range(steps):
+                    at = i * high + v * LANES
+                    value = taps[r : r + step, at : at + LANES].astype(F32)
+                    values.append((jnp.where(inside[t], value, 0.0), None))
+            left, right = slice(v * LANES, (v + 1) * LANES), slice(high + v * LANES, high + (v + 1) * LANES)
+            for d, (re, im) in enumerate(fourier(values, 1)):
+                tc, ts = turn[0, d : d + 1, left], turn[1, d : d + 1, left]
+                if im is None:
+                    re, im = re * tc, re * ts
+                else:
+                    re, im = re * tc - im * ts, re * ts + im * tc
+                mixed[d, r : r + step, left] = re.astype(BF16)
+                mixed[d, r : r + step, right] = (-im).astype(BF16)
+                mixed[d, pulses + r : pulses + r + step, left] = im.astype(BF16)
+                mixed[d, pulses + r : pulses + r + step, right] = re.astype(BF16)
+    for d in range(0, low, 2):
+        both = jnp.concatenate([mixed[d], mixed[d + 1]], axis=0)
+        done = dot(table[...], both, NT)
+        spread[pl.ds(d, high, stride=low), :] = done[:, : 2 * pulses]
+        spread[pl.ds(d + 1, high, stride=low), :] = done[:, 2 * pulses :]
+    out[...] = spread[...].astype(BF16)
 
 
 def factor(parts, n_z, n_x, n_c, per):
@@ -361,23 +380,25 @@
     tall = grid // low
     nt = np.arange(tall)
     c, s = phasor(nt, nt, tall, 1.0)
-    table = table_of(np.concatenate([c, s], axis=0) / math.sqrt(grid))
-    turn3 = table_of(np.stack(phasor(nt, np.arange(low), grid, 1.0)), F32)
+    table = table_of(np.concatenate([c, s], axis=1) / math.sqrt(grid))
+    turn3 = table_of(np.stack(phasor(np.arange(low), nt, grid, 1.0)), F32)
 
     piece = pltpu.VMEM((2 * tiles, per * LANES), BF16)
     *pieces, marked = pl.pallas_call(
         functools.partial(split_kernel, n_x, per),
-        in_specs=[HELD, VMEM, pl.BlockSpec(memory_space=pltpu.SMEM)],
+        in_specs=[HELD] * 3,
         out_specs=[VMEM] * (n_x + 1),
         out_shape=[piece] * n_x + [pltpu.VMEM((shard, width + LANES), BF16)],
         scratch_shapes=[
             pltpu.VMEM(raw_echo.shape, BF16),
+            pltpu.VMEM(azim_taps.shape, BF16),
+            pltpu.SMEM((1, shard), jnp.int32),
             pltpu.VMEM((2, tiles * shard, LANES), F32),
-            pltpu.SemaphoreType.DMA((2,)),
+            pltpu.SemaphoreType.DMA((4,)),
         ],
         name="split",
         **room,
-    )(*far(raw_echo, azim_taps), tile_col.T)
+    )(*far(raw_echo, azim_taps, tile_col.T))
     parts = []
     for k in range(1, n_x):
         parts.append(traded(pieces[k], "range", k))
@@ -427,10 +448,10 @@
     all_pulses = n_c * n_z * shard
     cuts = all_pulses // group
     scratch = [
-        pltpu.VMEM((width + LANES, group), F32),
-        pltpu.VMEM((low, 2 * tall, group), F32),
+        pltpu.VMEM((low, 2 * group, 2 * tall), BF16),
+        pltpu.VMEM((grid, 2 * group), F32),
     ]
-    make = functools.partial(column_kernel, width, tile_cols, low)
+    make = functools.partial(column_kernel, width, tile_cols)
     if cuts == 1:
         cols = pl.pallas_call(
             make,
@@ -447,8 +468,8 @@
             grid=(cuts,),
             in_specs=[
                 pl.BlockSpec((group, width + LANES), lambda i: (i, 0)),
-                pl.BlockSpec((2 * tall, tall), lambda i: (0, 0)),
-                pl.BlockSpec((2, tall, low), lambda i: (0, 0, 0)),
+                pl.BlockSpec((tall, 2 * tall), lambda i: (0, 0)),
+                pl.BlockSpec((2, low, tall), lambda i: (0, 0, 0)),
             ],
             out_specs=pl.BlockSpec((grid, 2 * group), lambda i: (0, i)),
             out_shape=jax.ShapeDtypeStruct((grid, 2 * all_pulses), BF16),

time: 48.6 us -> 44.3 us (0.912)
  Pallas kernels: 14.8 us -> 10.1 us
  waiting for transfers between devices: 14.2 us -> 15.4 us
  local copies, waits for them, and re-layouts: 0.65 us -> 0 us
    pallas_call x1, Pallas kernels: 5.51 us -> 1.69 us  [program(): pl.pallas_call(make, in_specs=[VMEM] * 3, out_specs=VMEM, out_shape=pltpu...]
    ppermute x13, waiting for transfers between devices: 14.2 us -> 15.4 us  [traded(): return lax.ppermute(block, axis, [(i, i ^ k) for i in range(count)])]
    pallas_call x1, Pallas kernels: 1.85 us -> 1.11 us  [program(): pl.pallas_call(functools.partial(split_kernel, n_x, per), in_specs=[HELD]...]
    unnamed x2 -> x0, local copies, waits for them, and re-layouts: 0.65 us -> none
  transfers between devices with their start and end apart: 13 -> 13, of which waited for: 6 -> 9; matrix products, arithmetic and copies ran while one was open for 0% -> 0% of each run, Pallas kernels for 19% -> 12%
where the time goes in v1:
time: 44.3 us; the launch traced here: 44.2 us
  starting transfers between devices  18.5 us (42%)
  waiting for transfers between devices  15.4 us (35%)
  Pallas kernels  10.1 us (23%)
    ppermute x13, starting transfers between devices, traded(): return lax.ppermute(block, axis, [(i, i ^ k) for i in range(count)])  18.5 us
    ppermute x13, waiting for transfers between devices, traded(): return lax.ppermute(block, axis, [(i, i ^ k) for i in range(count)])  15.4 us
    pallas_call x1, Pallas kernels, program(): pl.pallas_call(functools.partial(image_kernel, (n_z, n_x, n_c, per), wide...  3.71 us
    pallas_call x1, Pallas kernels, program(): pl.pallas_call(make, in_specs=[VMEM] * 3, out_specs=VMEM, out_shape=pltpu...  1.69 us
    pallas_call x1, Pallas kernels, program(): pl.pallas_call(functools.partial(ready_kernel, len(fixed)), in_specs=[VME...  1.64 us
    pallas_call x1, Pallas kernels, program(): pl.pallas_call(functools.partial(line_kernel, n_z, per, blocks, quads, to...  1.44 us
    pallas_call x1, Pallas kernels, program(): pl.pallas_call(functools.partial(split_kernel, n_x, per), in_specs=[HELD]...  1.11 us
  transfers between devices with their start and end apart: 13, of which 9 were waited for; matrix products, arithmetic and copies ran while one was open for 0% of the time, Pallas kernels for 12%

profile of v1, /device:TPU:0, one launch (start us, length us, event | category | flops | bytes accessed | tf_op | source)
XLA Modules:
  0.0 44.2 jit_solution(6847521857748084487)
XLA Ops:
  0.0 1.1 %split.1 = (bf16[128,512]{1,0:T(8,128)(2,1)S(1)}, bf16[128,512]{1,0:T(8,128)(2,1)S(1)}, bf16[8,2176]{1,0:T(8,128)(2,1)S(1)}) custom-call(bf16[2,8,8192]{2,1,0:T(8,128)(2,1)} %raw.1, bf16[8,2048]{1,0:T(8,128)(2,1)} %taps_in.1, s32[1,8]{1,0:T(1,128)} %bitcast.1), custom_call_target="tpu_custom_call" | custom-call | tf_op jit(solution)/shard_map/split/pallas_call | solution.py:387
  1.1 3.1 %collective-permute-start.10 = (bf16[8,2176]{1,0:T(8,128)(2,1)S(1)}, bf16[8,2176]{1,0:T(8,128)(2,1)S(1)}, u32[]{:S(2)}, u32[]{:S(2)}) collective-permute-start(bf16[8,2176]{1,0:T(8,128)(2,1)S(1)} %get-tuple-element.50), channel_id=1, source_target_pairs={{0,4},{4,0},{8,12},{12,8},{1,5},{5,1},{9,13},{13,9},{2,6},{6,2},{1... | collective-permute-start | bytes 104456 | tf_op jit(solution)/shard_map/ppermute | solution.py:28
  4.2 1.9 %collective-permute-done.10 = bf16[8,2176]{1,0:T(8,128)(2,1)S(1)} collective-permute-done((bf16[8,2176]{1,0:T(8,128)(2,1)S(1)}, bf16[8,2176]{1,0:T(8,128)(2,1)S(1)}, u32[]{:S(2)}, u32[]{:S(2)}) %collective-permute-start.10) | collective-permute-done | bytes 34848 | tf_op jit(solution)/shard_map/ppermute | solution.py:28
  6.2 3.0 %collective-permute-start.11 = (bf16[16,2176]{1,0:T(8,128)(2,1)S(1)}, bf16[16,2176]{1,0:T(8,128)(2,1)S(1)}, u32[]{:S(2)}, u32[]{:S(2)}) collective-permute-start(bf16[16,2176]{1,0:T(8,128)(2,1)S(1)} %pad_maximum_fusion.2), channel_id=1, source_target_pairs={{0,8},{4,12},{8,0},{12,4},{1,9},{5,13},{9,1},{13,5},{2,10},{6,14},... | collective-permute-start | bytes 208904 | tf_op jit(solution)/shard_map/ppermute | solution.py:28
  9.2 1.5 %collective-permute-start = (bf16[128,512]{1,0:T(8,128)(2,1)S(1)}, bf16[128,512]{1,0:T(8,128)(2,1)S(1)}, u32[]{:S(2)}, u32[]{:S(2)}) collective-permute-start(bf16[128,512]{1,0:T(8,128)(2,1)S(1)} %get-tuple-element.29), channel_id=1, source_target_pairs={{0,2},{2,0},{1,3},{3,1},{4,6},{6,4},{5,7},{7,5},{8,10},{10,8},{9,1... | collective-permute-start | bytes 393224 | tf_op jit(solution)/shard_map/ppermute | solution.py:28
  10.7 0.8 %collective-permute-done.11 = bf16[16,2176]{1,0:T(8,128)(2,1)S(1)} collective-permute-done((bf16[16,2176]{1,0:T(8,128)(2,1)S(1)}, bf16[16,2176]{1,0:T(8,128)(2,1)S(1)}, u32[]{:S(2)}, u32[]{:S(2)}) %collective-permute-start.11) | collective-permute-done | bytes 69664 | tf_op jit(solution)/shard_map/ppermute | solution.py:28
  11.5 0.1 collective-permute-start.12
  11.6 1.6 %ready.1 = (f32[256,512]{1,0:T(8,128)S(1)}, bf16[1,256,128]{2,1,0:T(8,128)(2,1)S(1)}, f32[2,128,128]{2,1,0:T(8,128)S(1)}, f32[2,128,128]{2,1,0:T(8,128)S(1)}, bf...) custom-call(bf16[128,512]{1,0:T(8,128)(2,1)S(1)} %get-tuple-element., ...), custom_call_target="tpu_custom_call" | custom-call | tf_op jit(solution)/shard_map/ready/pallas_call | solution.py:414
  13.2 0.9 %collective-permute-done.refs_0_ = bf16[128,512]{1,0:T(8,128)(2,1)S(1)} collective-permute-done((bf16[128,512]{1,0:T(8,128)(2,1)S(1)}, bf16[128,512]{1,0:T(8,128)(2,1)S(1)}, u32[]{:S(2)}, u32[]{:S(2)}) %collective-permute-start) | collective-permute-done | bytes 131104 | tf_op jit(solution)/shard_map/ppermute | solution.py:28
  14.2 0.5 %pulse_transform.1 = (bf16[64,512]{1,0:T(8,128)(2,1)S(1)}, bf16[64,512]{1,0:T(8,128)(2,1)S(1)}, bf16[64,512]{1,0:T(8,128)(2,1)S(1)}, bf16[64,512]{1,0:T(8,128)(2,1)S(1)}) custom-call(bf16[128,512]{1,0:T(8,128)(2,1)S(1)} %collective-permute-done.refs_0_, f32[256,512]{1,0:T(8,128)S(1)} %get-tuple-element.31.refs_1_, ...), custom_call_target="tpu_custom_call" | custom-call | tf_op jit(solution)/shard_map/pulse_transform/pallas_call | solution.py:435
  14.6 1.6 %collective-permute-start.1 = (bf16[64,512]{1,0:T(8,128)(2,1)S(1)}, bf16[64,512]{1,0:T(8,128)(2,1)S(1)}, u32[]{:S(2)}, u32[]{:S(2)}) collective-permute-start(bf16[64,512]{1,0:T(8,128)(2,1)S(1)} %get-tuple-element.36), channel_id=1, source_target_pairs={{0,4},{4,0},{8,12},{12,8},{1,5},{5,1},{9,13},{13,9},{2,6},{6,2},{1... | collective-permute-start | bytes 196616 | tf_op jit(solution)/shard_map/ppermute | solution.py:28
  16.3 2.6 %collective-permute-start.2 = (bf16[64,512]{1,0:T(8,128)(2,1)S(1)}, bf16[64,512]{1,0:T(8,128)(2,1)S(1)}, u32[]{:S(2)}, u32[]{:S(2)}) collective-permute-start(bf16[64,512]{1,0:T(8,128)(2,1)S(1)} %get-tuple-element.37), channel_id=1, source_target_pairs={{0,8},{4,12},{8,0},{12,4},{1,9},{5,13},{9,1},{13,5},{2,10},{6,14},... | collective-permute-start | bytes 196616 | tf_op jit(solution)/shard_map/ppermute | solution.py:28
  18.9 0.2 collective-permute-start.3
  19.1 4.2 %collective-permute-done.2.refs_2_ = bf16[64,512]{1,0:T(8,128)(2,1)S(1)} collective-permute-done((bf16[64,512]{1,0:T(8,128)(2,1)S(1)}, bf16[64,512]{1,0:T(8,128)(2,1)S(1)}, u32[]{:S(2)}, u32[]{:S(2)}) %collective-permute-start.2) | collective-permute-done | bytes 65568 | tf_op jit(solution)/shard_map/ppermute | solution.py:28
  23.3 1.7 %collective-permute-done.3.refs_3_ = bf16[64,512]{1,0:T(8,128)(2,1)S(1)} collective-permute-done((bf16[64,512]{1,0:T(8,128)(2,1)S(1)}, bf16[64,512]{1,0:T(8,128)(2,1)S(1)}, u32[]{:S(2)}, u32[]{:S(2)}) %collective-permute-start.3) | collective-permute-done | bytes 65568 | tf_op jit(solution)/shard_map/ppermute | solution.py:28
  25.0 1.4 %line_transform.1 = (bf16[32,1024]{1,0:T(8,128)(2,1)S(1)}, bf16[32,1024]{1,0:T(8,128)(2,1)S(1)}, bf16[32,1024]{1,0:T(8,128)(2,1)S(1)}, bf16[32,1024]{1,0:T(8,128)(2,1)S(1)}) custom-call(bf16[64,512]{1,0:T(8,128)(2,1)S(1)} %get-tuple-element.35.refs_0_, bf16[64,512]{1,0:T(8,128)(2,1)S(1)} %collective-permute-done.1.refs_1_, ...), custom_call_target="tpu_custom_call" | custom-call | tf_op jit(solution)/shard_map/line_transform/pallas_call | solution.py:481
  26.4 1.3 %collective-permute-start.4 = (bf16[32,1024]{1,0:T(8,128)(2,1)S(1)}, bf16[32,1024]{1,0:T(8,128)(2,1)S(1)}, u32[]{:S(2)}, u32[]{:S(2)}) collective-permute-start(bf16[32,1024]{1,0:T(8,128)(2,1)S(1)} %get-tuple-element.43), channel_id=1, source_target_pairs={{0,4},{4,0},{8,12},{12,8},{1,5},{5,1},{9,13},{13,9},{2,6},{6,2},{1... | collective-permute-start | bytes 196616 | tf_op jit(solution)/shard_map/ppermute | solution.py:28
  27.7 1.5 %collective-permute-start.5 = (bf16[32,1024]{1,0:T(8,128)(2,1)S(1)}, bf16[32,1024]{1,0:T(8,128)(2,1)S(1)}, u32[]{:S(2)}, u32[]{:S(2)}) collective-permute-start(bf16[32,1024]{1,0:T(8,128)(2,1)S(1)} %get-tuple-element.44), channel_id=1, source_target_pairs={{0,8},{4,12},{8,0},{12,4},{1,9},{5,13},{9,1},{13,5},{2,10},{6,14},... | collective-permute-start | bytes 196616 | tf_op jit(solution)/shard_map/ppermute | solution.py:28
  29.2 1.7 %collective-permute-start.6 = (bf16[32,1024]{1,0:T(8,128)(2,1)S(1)}, bf16[32,1024]{1,0:T(8,128)(2,1)S(1)}, u32[]{:S(2)}, u32[]{:S(2)}) collective-permute-start(bf16[32,1024]{1,0:T(8,128)(2,1)S(1)} %get-tuple-element.45), channel_id=1, source_target_pairs={{0,12},{4,8},{8,4},{12,0},{1,13},{5,9},{9,5},{13,1},{2,14},{6,10},... | collective-permute-start | bytes 196616 | tf_op jit(solution)/shard_map/ppermute | solution.py:28
  30.9 0.3 collective-permute-done.4.refs_1_
  31.2 4.4 %collective-permute-done.5.refs_2_ = bf16[32,1024]{1,0:T(8,128)(2,1)S(1)} collective-permute-done((bf16[32,1024]{1,0:T(8,128)(2,1)S(1)}, bf16[32,1024]{1,0:T(8,128)(2,1)S(1)}, u32[]{:S(2)}, u32[]{:S(2)}) %collective-permute-start.5) | collective-permute-done | bytes 65568 | tf_op jit(solution)/shard_map/ppermute | solution.py:28
  35.6 0.0 collective-permute-done.6.refs_3_
  35.6 0.1 fold.1
  35.6 0.1 collective-permute-start.7
  35.7 1.6 %collective-permute-start.8 = (bf16[32,256]{1,0:T(8,128)(2,1)S(1)}, bf16[32,256]{1,0:T(8,128)(2,1)S(1)}, u32[]{:S(2)}, u32[]{:S(2)}) collective-permute-start(bf16[32,256]{1,0:T(8,128)(2,1)S(1)} %get-tuple-element.48), channel_id=1, source_target_pairs={{0,2},{1,3},{2,0},{3,1},{4,6},{5,7},{6,4},{7,5},{8,10},{9,11},{10,... | collective-permute-start | bytes 49160 | tf_op jit(solution)/shard_map/ppermute | solution.py:28
  37.3 0.3 collective-permute-start.9
  37.6 0.0 collective-permute-done.12
  37.6 1.7 %column_transform.1.refs_4_ = bf16[4096,128]{1,0:T(8,128)(2,1)S(1)} custom-call(bf16[64,2176]{1,0:T(8,128)(2,1)S(1)} %pad_maximum_fusion.taps, bf16[256,512]{1,0:T(8,128)(2,1)S(1)} %get-tuple-element.51.table, f32[2,16,256]{2,1,0:T(8,128)S(1)} %get-tuple-element.52.turn), custom_call_target="tpu_custom_call" | custom-call | tf_op jit(solution)/shard_map/column_transform/pallas_call | solution.py:456
  39.3 0.0 collective-permute-done.7.refs_1_
  39.3 0.2 collective-permute-done.8.refs_2_
  39.5 0.9 %collective-permute-done.9.refs_3_ = bf16[32,256]{1,0:T(8,128)(2,1)S(1)} collective-permute-done((bf16[32,256]{1,0:T(8,128)(2,1)S(1)}, bf16[32,256]{1,0:T(8,128)(2,1)S(1)}, u32[]{:S(2)}, u32[]{:S(2)}) %collective-permute-start.9) | collective-permute-done | bytes 16416 | tf_op jit(solution)/shard_map/ppermute | solution.py:28
  40.4 3.7 %image.1 = f32[2,256,4096]{2,1,0:T(8,128)} custom-call(bf16[32,256]{1,0:T(8,128)(2,1)S(1)} %get-tuple-element.46.refs_0_, bf16[32,256]{1,0:T(8,128)(2,1)S(1)} %collective-permute-done.7.refs_1_, bf16[32,256]{1,0:T(8,128)(2,1)S(1)} %collective-permute-done.8.refs_2_, bf16[32,256]{1,0:T(8,128)(2,1)S(1)} %collective-permute-done.9.refs_3_, ...), custom_call_target="tpu_custom_call" | custom-call | tf_op jit(solution)/shard_map/image/pallas_call | solution.py:522
  (4 shorter events, 0.0 us)
Async XLA Ops:
  1.1 5.0 %collective-permute-start.10 = (bf16[8,2176]{1,0:T(8,128)(2,1)S(1)}, bf16[8,2176]{1,0:T(8,128)(2,1)S(1)}, u32[]{:S(2)}, u32[]{:S(2)}) collective-permute-start(bf16[8,2176]{1,0:T(8,128)(2,1)S(1)} %get-tuple-element.50), channel_id=1, source_target_pairs={{0,4},{4,0},{8,12},{12,8},{1,5},{5,1},{9,13},{13,9},{2,6},{6,2},{1... | collective-permute-start | bytes 104456 | tf_op jit(solution)/shard_map/ppermute | solution.py:28
  6.2 5.3 %collective-permute-start.11 = (bf16[16,2176]{1,0:T(8,128)(2,1)S(1)}, bf16[16,2176]{1,0:T(8,128)(2,1)S(1)}, u32[]{:S(2)}, u32[]{:S(2)}) collective-permute-start(bf16[16,2176]{1,0:T(8,128)(2,1)S(1)} %pad_maximum_fusion.2), channel_id=1, source_target_pairs={{0,8},{4,12},{8,0},{12,4},{1,9},{5,13},{9,1},{13,5},{2,10},{6,14},... | collective-permute-start | bytes 208904 | tf_op jit(solution)/shard_map/ppermute | solution.py:28
  9.2 5.0 %collective-permute-start = (bf16[128,512]{1,0:T(8,128)(2,1)S(1)}, bf16[128,512]{1,0:T(8,128)(2,1)S(1)}, u32[]{:S(2)}, u32[]{:S(2)}) collective-permute-start(bf16[128,512]{1,0:T(8,128)(2,1)S(1)} %get-tuple-element.29), channel_id=1, source_target_pairs={{0,2},{2,0},{1,3},{3,1},{4,6},{6,4},{5,7},{7,5},{8,10},{10,8},{9,1... | collective-permute-start | bytes 393224 | tf_op jit(solution)/shard_map/ppermute | solution.py:28
  11.5 26.1 %collective-permute-start.12 = (bf16[32,2176]{1,0:T(8,128)(2,1)S(1)}, bf16[32,2176]{1,0:T(8,128)(2,1)S(1)}, u32[]{:S(2)}, u32[]{:S(2)}) collective-permute-start(bf16[32,2176]{1,0:T(8,128)(2,1)S(1)} %pad_maximum_fusion.1), channel_id=1, source_target_pairs={{0,1},{1,0},{2,3},{3,2},{4,5},{5,4},{6,7},{7,6},{8,9},{9,8},{10,11... | collective-permute-start | bytes 417800 | tf_op jit(solution)/shard_map/ppermute | solution.py:28
  14.6 4.5 %collective-permute-start.1 = (bf16[64,512]{1,0:T(8,128)(2,1)S(1)}, bf16[64,512]{1,0:T(8,128)(2,1)S(1)}, u32[]{:S(2)}, u32[]{:S(2)}) collective-permute-start(bf16[64,512]{1,0:T(8,128)(2,1)S(1)} %get-tuple-element.36), channel_id=1, source_target_pairs={{0,4},{4,0},{8,12},{12,8},{1,5},{5,1},{9,13},{13,9},{2,6},{6,2},{1... | collective-permute-start | bytes 196616 | tf_op jit(solution)/shard_map/ppermute | solution.py:28
  16.3 7.0 %collective-permute-start.2 = (bf16[64,512]{1,0:T(8,128)(2,1)S(1)}, bf16[64,512]{1,0:T(8,128)(2,1)S(1)}, u32[]{:S(2)}, u32[]{:S(2)}) collective-permute-start(bf16[64,512]{1,0:T(8,128)(2,1)S(1)} %get-tuple-element.37), channel_id=1, source_target_pairs={{0,8},{4,12},{8,0},{12,4},{1,9},{5,13},{9,1},{13,5},{2,10},{6,14},... | collective-permute-start | bytes 196616 | tf_op jit(solution)/shard_map/ppermute | solution.py:28
  18.9 6.1 %collective-permute-start.3 = (bf16[64,512]{1,0:T(8,128)(2,1)S(1)}, bf16[64,512]{1,0:T(8,128)(2,1)S(1)}, u32[]{:S(2)}, u32[]{:S(2)}) collective-permute-start(bf16[64,512]{1,0:T(8,128)(2,1)S(1)} %get-tuple-element.38), channel_id=1, source_target_pairs={{0,12},{4,8},{8,4},{12,0},{1,13},{5,9},{9,5},{13,1},{2,14},{6,10},... | collective-permute-start | bytes 196616 | tf_op jit(solution)/shard_map/ppermute | solution.py:28
  26.4 4.7 %collective-permute-start.4 = (bf16[32,1024]{1,0:T(8,128)(2,1)S(1)}, bf16[32,1024]{1,0:T(8,128)(2,1)S(1)}, u32[]{:S(2)}, u32[]{:S(2)}) collective-permute-start(bf16[32,1024]{1,0:T(8,128)(2,1)S(1)} %get-tuple-element.43), channel_id=1, source_target_pairs={{0,4},{4,0},{8,12},{12,8},{1,5},{5,1},{9,13},{13,9},{2,6},{6,2},{1... | collective-permute-start | bytes 196616 | tf_op jit(solution)/shard_map/ppermute | solution.py:28
  27.7 7.8 %collective-permute-start.5 = (bf16[32,1024]{1,0:T(8,128)(2,1)S(1)}, bf16[32,1024]{1,0:T(8,128)(2,1)S(1)}, u32[]{:S(2)}, u32[]{:S(2)}) collective-permute-start(bf16[32,1024]{1,0:T(8,128)(2,1)S(1)} %get-tuple-element.44), channel_id=1, source_target_pairs={{0,8},{4,12},{8,0},{12,4},{1,9},{5,13},{9,1},{13,5},{2,10},{6,14},... | collective-permute-start | bytes 196616 | tf_op jit(solution)/shard_map/ppermute | solution.py:28
  29.2 6.4 %collective-permute-start.6 = (bf16[32,1024]{1,0:T(8,128)(2,1)S(1)}, bf16[32,1024]{1,0:T(8,128)(2,1)S(1)}, u32[]{:S(2)}, u32[]{:S(2)}) collective-permute-start(bf16[32,1024]{1,0:T(8,128)(2,1)S(1)} %get-tuple-element.45), channel_id=1, source_target_pairs={{0,12},{4,8},{8,4},{12,0},{1,13},{5,9},{9,5},{13,1},{2,14},{6,10},... | collective-permute-start | bytes 196616 | tf_op jit(solution)/shard_map/ppermute | solution.py:28
  35.6 3.7 %collective-permute-start.7 = (bf16[32,256]{1,0:T(8,128)(2,1)S(1)}, bf16[32,256]{1,0:T(8,128)(2,1)S(1)}, u32[]{:S(2)}, u32[]{:S(2)}) collective-permute-start(bf16[32,256]{1,0:T(8,128)(2,1)S(1)} %get-tuple-element.47), channel_id=1, source_target_pairs={{0,1},{1,0},{2,3},{3,2},{4,5},{5,4},{6,7},{7,6},{8,9},{9,8},{10,11... | collective-permute-start | bytes 49160 | tf_op jit(solution)/shard_map/ppermute | solution.py:28
  35.7 3.8 %collective-permute-start.8 = (bf16[32,256]{1,0:T(8,128)(2,1)S(1)}, bf16[32,256]{1,0:T(8,128)(2,1)S(1)}, u32[]{:S(2)}, u32[]{:S(2)}) collective-permute-start(bf16[32,256]{1,0:T(8,128)(2,1)S(1)} %get-tuple-element.48), channel_id=1, source_target_pairs={{0,2},{1,3},{2,0},{3,1},{4,6},{5,7},{6,4},{7,5},{8,10},{9,11},{10,... | collective-permute-start | bytes 49160 | tf_op jit(solution)/shard_map/ppermute | solution.py:28
  37.3 3.2 %collective-permute-start.9 = (bf16[32,256]{1,0:T(8,128)(2,1)S(1)}, bf16[32,256]{1,0:T(8,128)(2,1)S(1)}, u32[]{:S(2)}, u32[]{:S(2)}) collective-permute-start(bf16[32,256]{1,0:T(8,128)(2,1)S(1)} %get-tuple-element.49), channel_id=1, source_target_pairs={{0,3},{1,2},{2,1},{3,0},{4,7},{5,6},{6,5},{7,4},{8,11},{9,10},{10,... | collective-permute-start | bytes 49160 | tf_op jit(solution)/shard_map/ppermute | solution.py:28

commit v2 on v1

--- a/solution.py
+++ b/solution.py
@@ -125,24 +125,34 @@
                 ].astype(BF16)
 
 
-def ready_kernel(n_fixed, own, first, turn, *refs):
+def ready_kernel(n_fixed, own, first, *refs):
     fixed = refs[:n_fixed]
-    part, rest, turned = refs[n_fixed : n_fixed + 3]
-    brought = refs[n_fixed + 3 : 2 * n_fixed + 3]
-    mine, sent = refs[2 * n_fixed + 3 :]
+    part, rest = refs[n_fixed : n_fixed + 2]
+    brought = refs[n_fixed + 2 : 2 * n_fixed + 2]
+    mine, sent = refs[2 * n_fixed + 2 :]
     my_x = lax.axis_index("range")
     copies = [
         pltpu.make_async_copy(first.at[my_x, 0], mine, sent.at[0]),
         pltpu.make_async_copy(first.at[my_x, pl.ds(1, rest.shape[0])], rest, sent.at[1]),
-        pltpu.make_async_copy(turn.at[lax.axis_index("pulse")], turned, sent.at[2]),
     ]
     for i in range(n_fixed):
-        copies.append(pltpu.make_async_copy(fixed[i], brought[i], sent.at[i + 3]))
+        copies.append(pltpu.make_async_copy(fixed[i], brought[i], sent.at[i + 2]))
     for copy in copies:
         copy.start()
     copies[0].wait()
     part[...] = dot(mine[...], own[...])
     for copy in copies[1:]:
+        copy.wait()
+
+
+def bring_kernel(n_fixed, turn, *refs):
+    fixed, turned_in, brought, sent = refs[:n_fixed], refs[n_fixed], refs[n_fixed + 1 : -1], refs[-1]
+    copies = [pltpu.make_async_copy(turn.at[lax.axis_index("pulse")], turned_in, sent.at[n_fixed])]
+    for i in range(n_fixed):
+        copies.append(pltpu.make_async_copy(fixed[i], brought[i], sent.at[i]))
+    for copy in copies:
+        copy.start()
+    for copy in copies:
         copy.wait()
 
 
@@ -291,12 +301,19 @@
     out[...] = spread[...].astype(BF16)
 
 
+def turned(count):
+    order, k = [0], count // 2
+    while k > 0:
+        order, k = order + [o ^ k for o in order], k // 2
+    return order
+
+
 def factor(parts, n_z, n_x, n_c, per):
     pulses = n_z * per
     out = []
     for comp in range(2):
-        for c in range(n_c):
-            for z in range(n_z):
+        for c in turned(n_c):
+            for z in turned(n_z):
                 for x in range(n_x):
                     at = comp * pulses + z * per
                     out.append(parts[x * n_c + c][at : at + per, :])
@@ -405,30 +422,39 @@
 
     everyone = marked
     for axis, count in (("pulse", n_z), ("sub", n_c)):
-        k = 1
-        while k < count:
+        k = count // 2
+        while k > 0:
             everyone = jnp.concatenate([everyone, traded(everyone, axis, k)], axis=0)
-            k *= 2
-
-    fixed = (turn1, second, last, range_taps, table, turn3)
-    part1, rest, turn2, *brought = pl.pallas_call(
+            k //= 2
+
+    fixed = (turn1, second)
+    part1, rest, turn1, second = pl.pallas_call(
         functools.partial(ready_kernel, len(fixed)),
-        in_specs=[VMEM] + [HELD] * (2 + len(fixed)),
-        out_specs=[VMEM] * (3 + len(fixed)),
+        in_specs=[VMEM] + [HELD] * (1 + len(fixed)),
+        out_specs=[VMEM] * (2 + len(fixed)),
         out_shape=[
             pltpu.VMEM((2 * high, per * LANES), F32),
             pltpu.VMEM((max(n_x - 1, 1), 2 * high, 2 * tiles), BF16),
-            pltpu.VMEM(turn2.shape[1:], F32),
         ]
         + [pltpu.VMEM(f.shape, f.dtype) for f in fixed],
         scratch_shapes=[
             pltpu.VMEM((2 * high, 2 * tiles), BF16),
-            pltpu.SemaphoreType.DMA((3 + len(fixed),)),
+            pltpu.SemaphoreType.DMA((2 + len(fixed),)),
         ],
         name="ready",
         **room,
-    )(*near(pieces[0]), *far(first, turn2, *fixed))
-    turn1, second, last, range_taps, table, turn3 = brought
+    )(*near(pieces[0]), *far(first, *fixed))
+    fixed = (last, range_taps, table, turn3)
+    turn2, last, range_taps, table, turn3 = pl.pallas_call(
+        functools.partial(bring_kernel, len(fixed)),
+        in_specs=[HELD] * (1 + len(fixed)),
+        out_specs=[VMEM] * (1 + len(fixed)),
+        out_shape=[pltpu.VMEM(turn2.shape[1:], F32)]
+        + [pltpu.VMEM(f.shape, f.dtype) for f in fixed],
+        scratch_shapes=[pltpu.SemaphoreType.DMA((1 + len(fixed),))],
+        name="bring",
+        **room,
+    )(*far(turn2, *fixed))
 
     band = LANES // n_z
     chunk = pltpu.VMEM((2 * band, per * high), BF16)

time: 44.3 us -> 43.4 us (0.980)
  waiting for transfers between devices: 15.4 us -> 14.1 us
  Pallas kernels: 10.1 us -> 11 us
  starting transfers between devices: 18.5 us -> 18 us
    pallas_call x0 -> x1, Pallas kernels: none -> 1.4 us  [program(): pl.pallas_call(functools.partial(bring_kernel, len(fixed)), in_specs=[HEL...]
    ppermute x13, waiting for transfers between devices: 15.4 us -> 14.1 us  [traded(): return lax.ppermute(block, axis, [(i, i ^ k) for i in range(count)])]
    pallas_call x1, Pallas kernels: 1.64 us -> 1.11 us  [program(): pl.pallas_call(functools.partial(ready_kernel, len(fixed)), in_specs=[VME...]
    ppermute x13, starting transfers between devices: 18.5 us -> 18 us  [traded(): return lax.ppermute(block, axis, [(i, i ^ k) for i in range(count)])]
  transfers between devices with their start and end apart: 13 -> 13, of which waited for: 9 -> 9; matrix products, arithmetic and copies ran while one was open for 0% -> 0% of each run, Pallas kernels for 12% -> 14%
where the time goes in v2:
time: 43.4 us; the launch traced here: 43.2 us
  starting transfers between devices  18 us (41%)
  waiting for transfers between devices  14.1 us (32%)
  Pallas kernels  11 us (25%)
    ppermute x13, starting transfers between devices, traded(): return lax.ppermute(block, axis, [(i, i ^ k) for i in range(count)])  18 us
    ppermute x13, waiting for transfers between devices, traded(): return lax.ppermute(block, axis, [(i, i ^ k) for i in range(count)])  14.1 us
    pallas_call x1, Pallas kernels, program(): pl.pallas_call(functools.partial(image_kernel, (n_z, n_x, n_c, per), wide...  3.71 us
    pallas_call x1, Pallas kernels, program(): pl.pallas_call(make, in_specs=[VMEM] * 3, out_specs=VMEM, out_shape=pltpu...  1.69 us
    pallas_call x1, Pallas kernels, program(): pl.pallas_call(functools.partial(line_kernel, n_z, per, blocks, quads, to...  1.43 us
    pallas_call x1, Pallas kernels, program(): pl.pallas_call(functools.partial(bring_kernel, len(fixed)), in_specs=[HEL...  1.4 us
    pallas_call x1, Pallas kernels, program(): pl.pallas_call(functools.partial(ready_kernel, len(fixed)), in_specs=[VME...  1.11 us
    pallas_call x1, Pallas kernels, program(): pl.pallas_call(functools.partial(split_kernel, n_x, per), in_specs=[HELD]...  1.11 us
  transfers between devices with their start and end apart: 13, of which 9 were waited for; matrix products, arithmetic and copies ran while one was open for 0% of the time, Pallas kernels for 14%

profile of v2, /device:TPU:0, one launch (start us, length us, event | category | flops | bytes accessed | tf_op | source)
XLA Modules:
  0.0 43.2 jit_solution(8248458631026345893)
XLA Ops:
  0.0 1.1 %split.1 = (bf16[128,512]{1,0:T(8,128)(2,1)S(1)}, bf16[128,512]{1,0:T(8,128)(2,1)S(1)}, bf16[8,2176]{1,0:T(8,128)(2,1)S(1)}) custom-call(bf16[2,8,8192]{2,1,0:T(8,128)(2,1)} %raw.1, bf16[8,2048]{1,0:T(8,128)(2,1)} %taps_in.1, s32[1,8]{1,0:T(1,128)} %bitcast.1), custom_call_target="tpu_custom_call" | custom-call | tf_op jit(solution)/shard_map/split/pallas_call | solution.py:404
  1.1 4.1 %collective-permute-start.10 = (bf16[8,2176]{1,0:T(8,128)(2,1)S(1)}, bf16[8,2176]{1,0:T(8,128)(2,1)S(1)}, u32[]{:S(2)}, u32[]{:S(2)}) collective-permute-start(bf16[8,2176]{1,0:T(8,128)(2,1)S(1)} %get-tuple-element.50), channel_id=1, source_target_pairs={{0,8},{4,12},{8,0},{12,4},{1,9},{5,13},{9,1},{13,5},{2,10},{6,14},... | collective-permute-start | bytes 104456 | tf_op jit(solution)/shard_map/ppermute | solution.py:28
  5.2 2.3 %collective-permute-done.10 = bf16[8,2176]{1,0:T(8,128)(2,1)S(1)} collective-permute-done((bf16[8,2176]{1,0:T(8,128)(2,1)S(1)}, bf16[8,2176]{1,0:T(8,128)(2,1)S(1)}, u32[]{:S(2)}, u32[]{:S(2)}) %collective-permute-start.10) | collective-permute-done | bytes 34848 | tf_op jit(solution)/shard_map/ppermute | solution.py:28
  7.5 1.5 %collective-permute-start.11 = (bf16[16,2176]{1,0:T(8,128)(2,1)S(1)}, bf16[16,2176]{1,0:T(8,128)(2,1)S(1)}, u32[]{:S(2)}, u32[]{:S(2)}) collective-permute-start(bf16[16,2176]{1,0:T(8,128)(2,1)S(1)} %pad_maximum_fusion.2), channel_id=1, source_target_pairs={{0,4},{4,0},{8,12},{12,8},{1,5},{5,1},{9,13},{13,9},{2,6},{6,2},{1... | collective-permute-start | bytes 208904 | tf_op jit(solution)/shard_map/ppermute | solution.py:28
  9.1 1.5 %collective-permute-start = (bf16[128,512]{1,0:T(8,128)(2,1)S(1)}, bf16[128,512]{1,0:T(8,128)(2,1)S(1)}, u32[]{:S(2)}, u32[]{:S(2)}) collective-permute-start(bf16[128,512]{1,0:T(8,128)(2,1)S(1)} %get-tuple-element.29), channel_id=1, source_target_pairs={{0,2},{2,0},{1,3},{3,1},{4,6},{6,4},{5,7},{7,5},{8,10},{10,8},{9,1... | collective-permute-start | bytes 393224 | tf_op jit(solution)/shard_map/ppermute | solution.py:28
  10.6 1.3 %collective-permute-done.11 = bf16[16,2176]{1,0:T(8,128)(2,1)S(1)} collective-permute-done((bf16[16,2176]{1,0:T(8,128)(2,1)S(1)}, bf16[16,2176]{1,0:T(8,128)(2,1)S(1)}, u32[]{:S(2)}, u32[]{:S(2)}) %collective-permute-start.11) | collective-permute-done | bytes 69664 | tf_op jit(solution)/shard_map/ppermute | solution.py:28
  11.9 0.1 collective-permute-start.12
  11.9 1.1 %ready.1 = (f32[256,512]{1,0:T(8,128)S(1)}, bf16[1,256,128]{2,1,0:T(8,128)(2,1)S(1)}, f32[2,128,128]{2,1,0:T(8,128)S(1)}, bf16[256,256]{1,0:T(8,128)(2,1)S(1)}) custom-call(bf16[128,512]{1,0:T(8,128)(2,1)S(1)} %get-tuple-element.30.own, bf16[2,2,256,128]{3,2,1,0:T(8,128)(2,1)} %constant.14.clone.first, f32[2,128,128]{2,1,0:T(8,128)} %constant.15.clone.refs_0_, ...), custom_call_target="tpu_custom_call" | custom-call | tf_op jit(solution)/shard_map/ready/pallas_call | solution.py:431
  13.1 1.0 %collective-permute-done.refs_0_ = bf16[128,512]{1,0:T(8,128)(2,1)S(1)} collective-permute-done((bf16[128,512]{1,0:T(8,128)(2,1)S(1)}, bf16[128,512]{1,0:T(8,128)(2,1)S(1)}, u32[]{:S(2)}, u32[]{:S(2)}) %collective-permute-start) | collective-permute-done | bytes 131104 | tf_op jit(solution)/shard_map/ppermute | solution.py:28
  14.0 0.5 %pulse_transform.1 = (bf16[64,512]{1,0:T(8,128)(2,1)S(1)}, bf16[64,512]{1,0:T(8,128)(2,1)S(1)}, bf16[64,512]{1,0:T(8,128)(2,1)S(1)}, bf16[64,512]{1,0:T(8,128)(2,1)S(1)}) custom-call(bf16[128,512]{1,0:T(8,128)(2,1)S(1)} %collective-permute-done.refs_0_, f32[256,512]{1,0:T(8,128)S(1)} %get-tuple-element.31.refs_1_, ...), custom_call_target="tpu_custom_call" | custom-call | tf_op jit(solution)/shard_map/pulse_transform/pallas_call | solution.py:461
  14.5 0.6 %collective-permute-start.1 = (bf16[64,512]{1,0:T(8,128)(2,1)S(1)}, bf16[64,512]{1,0:T(8,128)(2,1)S(1)}, u32[]{:S(2)}, u32[]{:S(2)}) collective-permute-start(bf16[64,512]{1,0:T(8,128)(2,1)S(1)} %get-tuple-element.36), channel_id=1, source_target_pairs={{0,4},{4,0},{8,12},{12,8},{1,5},{5,1},{9,13},{13,9},{2,6},{6,2},{1... | collective-permute-start | bytes 196616 | tf_op jit(solution)/shard_map/ppermute | solution.py:28
  15.2 2.8 %collective-permute-start.2 = (bf16[64,512]{1,0:T(8,128)(2,1)S(1)}, bf16[64,512]{1,0:T(8,128)(2,1)S(1)}, u32[]{:S(2)}, u32[]{:S(2)}) collective-permute-start(bf16[64,512]{1,0:T(8,128)(2,1)S(1)} %get-tuple-element.37), channel_id=1, source_target_pairs={{0,8},{4,12},{8,0},{12,4},{1,9},{5,13},{9,1},{13,5},{2,10},{6,14},... | collective-permute-start | bytes 196616 | tf_op jit(solution)/shard_map/ppermute | solution.py:28
  18.0 1.0 %collective-permute-start.3 = (bf16[64,512]{1,0:T(8,128)(2,1)S(1)}, bf16[64,512]{1,0:T(8,128)(2,1)S(1)}, u32[]{:S(2)}, u32[]{:S(2)}) collective-permute-start(bf16[64,512]{1,0:T(8,128)(2,1)S(1)} %get-tuple-element.38), channel_id=1, source_target_pairs={{0,12},{4,8},{8,4},{12,0},{1,13},{5,9},{9,5},{13,1},{2,14},{6,10},... | collective-permute-start | bytes 196616 | tf_op jit(solution)/shard_map/ppermute | solution.py:28
  19.0 1.4 %bring.1 = (f32[2,128,128]{2,1,0:T(8,128)S(1)}, bf16[64,256]{1,0:T(8,128)(2,1)S(1)}, bf16[8,512,128]{2,1,0:T(8,128)(2,1)S(1)}, bf16[256,512]{1,0:T(8,128)(2,1)S(1)}, f32[2,16,256]{2,1,0:T(8,128)S(1)}) custom-call(f32[4,2,128,128]{3,2,1,0:T(8,128)} %constant.17.clone.turn, bf16[64,256]{1,0:T(8,128)(2,1)} %constant.18.clone.refs_0_, ...), custom_call_target="tpu_custom_call" | custom-call | tf_op jit(solution)/shard_map/bring/pallas_call | solution.py:448
  20.4 0.0 collective-permute-done.1.refs_1_
  20.4 2.7 %collective-permute-done.2.refs_2_ = bf16[64,512]{1,0:T(8,128)(2,1)S(1)} collective-permute-done((bf16[64,512]{1,0:T(8,128)(2,1)S(1)}, bf16[64,512]{1,0:T(8,128)(2,1)S(1)}, u32[]{:S(2)}, u32[]{:S(2)}) %collective-permute-start.2) | collective-permute-done | bytes 65568 | tf_op jit(solution)/shard_map/ppermute | solution.py:28
  23.1 1.0 %collective-permute-done.3.refs_3_ = bf16[64,512]{1,0:T(8,128)(2,1)S(1)} collective-permute-done((bf16[64,512]{1,0:T(8,128)(2,1)S(1)}, bf16[64,512]{1,0:T(8,128)(2,1)S(1)}, u32[]{:S(2)}, u32[]{:S(2)}) %collective-permute-start.3) | collective-permute-done | bytes 65568 | tf_op jit(solution)/shard_map/ppermute | solution.py:28
  24.1 1.4 %line_transform.1 = (bf16[32,1024]{1,0:T(8,128)(2,1)S(1)}, bf16[32,1024]{1,0:T(8,128)(2,1)S(1)}, bf16[32,1024]{1,0:T(8,128)(2,1)S(1)}, bf16[32,1024]{1,0:T(8,128)(2,1)S(1)}) custom-call(bf16[64,512]{1,0:T(8,128)(2,1)S(1)} %get-tuple-element.35.refs_0_, bf16[64,512]{1,0:T(8,128)(2,1)S(1)} %collective-permute-done.1.refs_1_, ...), custom_call_target="tpu_custom_call" | custom-call | tf_op jit(solution)/shard_map/line_transform/pallas_call | solution.py:507
  25.5 1.2 %collective-permute-start.4 = (bf16[32,1024]{1,0:T(8,128)(2,1)S(1)}, bf16[32,1024]{1,0:T(8,128)(2,1)S(1)}, u32[]{:S(2)}, u32[]{:S(2)}) collective-permute-start(bf16[32,1024]{1,0:T(8,128)(2,1)S(1)} %get-tuple-element.43), channel_id=1, source_target_pairs={{0,4},{4,0},{8,12},{12,8},{1,5},{5,1},{9,13},{13,9},{2,6},{6,2},{1... | collective-permute-start | bytes 196616 | tf_op jit(solution)/shard_map/ppermute | solution.py:28
  26.8 1.7 %collective-permute-start.5 = (bf16[32,1024]{1,0:T(8,128)(2,1)S(1)}, bf16[32,1024]{1,0:T(8,128)(2,1)S(1)}, u32[]{:S(2)}, u32[]{:S(2)}) collective-permute-start(bf16[32,1024]{1,0:T(8,128)(2,1)S(1)} %get-tuple-element.44), channel_id=1, source_target_pairs={{0,8},{4,12},{8,0},{12,4},{1,9},{5,13},{9,1},{13,5},{2,10},{6,14},... | collective-permute-start | bytes 196616 | tf_op jit(solution)/shard_map/ppermute | solution.py:28
  28.5 1.5 %collective-permute-start.6 = (bf16[32,1024]{1,0:T(8,128)(2,1)S(1)}, bf16[32,1024]{1,0:T(8,128)(2,1)S(1)}, u32[]{:S(2)}, u32[]{:S(2)}) collective-permute-start(bf16[32,1024]{1,0:T(8,128)(2,1)S(1)} %get-tuple-element.45), channel_id=1, source_target_pairs={{0,12},{4,8},{8,4},{12,0},{1,13},{5,9},{9,5},{13,1},{2,14},{6,10},... | collective-permute-start | bytes 196616 | tf_op jit(solution)/shard_map/ppermute | solution.py:28
  30.0 3.6 %collective-permute-done.5.refs_2_ = bf16[32,1024]{1,0:T(8,128)(2,1)S(1)} collective-permute-done((bf16[32,1024]{1,0:T(8,128)(2,1)S(1)}, bf16[32,1024]{1,0:T(8,128)(2,1)S(1)}, u32[]{:S(2)}, u32[]{:S(2)}) %collective-permute-start.5) | collective-permute-done | bytes 65568 | tf_op jit(solution)/shard_map/ppermute | solution.py:28
  33.6 1.1 %collective-permute-done.6.refs_3_ = bf16[32,1024]{1,0:T(8,128)(2,1)S(1)} collective-permute-done((bf16[32,1024]{1,0:T(8,128)(2,1)S(1)}, bf16[32,1024]{1,0:T(8,128)(2,1)S(1)}, u32[]{:S(2)}, u32[]{:S(2)}) %collective-permute-start.6) | collective-permute-done | bytes 65568 | tf_op jit(solution)/shard_map/ppermute | solution.py:28
  34.7 0.1 fold.1
  34.7 0.1 collective-permute-start.7
  34.8 1.6 %collective-permute-start.8 = (bf16[32,256]{1,0:T(8,128)(2,1)S(1)}, bf16[32,256]{1,0:T(8,128)(2,1)S(1)}, u32[]{:S(2)}, u32[]{:S(2)}) collective-permute-start(bf16[32,256]{1,0:T(8,128)(2,1)S(1)} %get-tuple-element.48), channel_id=1, source_target_pairs={{0,2},{1,3},{2,0},{3,1},{4,6},{5,7},{6,4},{7,5},{8,10},{9,11},{10,... | collective-permute-start | bytes 49160 | tf_op jit(solution)/shard_map/ppermute | solution.py:28
  36.3 0.3 collective-permute-start.9
  36.6 0.0 collective-permute-done.12
  36.7 1.7 %column_transform.1.refs_4_ = bf16[4096,128]{1,0:T(8,128)(2,1)S(1)} custom-call(bf16[64,2176]{1,0:T(8,128)(2,1)S(1)} %pad_maximum_fusion.taps, bf16[256,512]{1,0:T(8,128)(2,1)S(1)} %get-tuple-element.51.table, f32[2,16,256]{2,1,0:T(8,128)S(1)} %get-tuple-element.52.turn), custom_call_target="tpu_custom_call" | custom-call | tf_op jit(solution)/shard_map/column_transform/pallas_call | solution.py:482
  38.4 0.2 collective-permute-done.8.refs_2_
  38.6 0.9 %collective-permute-done.9.refs_3_ = bf16[32,256]{1,0:T(8,128)(2,1)S(1)} collective-permute-done((bf16[32,256]{1,0:T(8,128)(2,1)S(1)}, bf16[32,256]{1,0:T(8,128)(2,1)S(1)}, u32[]{:S(2)}, u32[]{:S(2)}) %collective-permute-start.9) | collective-permute-done | bytes 16416 | tf_op jit(solution)/shard_map/ppermute | solution.py:28
  39.5 3.7 %image.1 = f32[2,256,4096]{2,1,0:T(8,128)} custom-call(bf16[32,256]{1,0:T(8,128)(2,1)S(1)} %get-tuple-element.46.refs_0_, bf16[32,256]{1,0:T(8,128)(2,1)S(1)} %collective-permute-done.7.refs_1_, bf16[32,256]{1,0:T(8,128)(2,1)S(1)} %collective-permute-done.8.refs_2_, bf16[32,256]{1,0:T(8,128)(2,1)S(1)} %collective-permute-done.9.refs_3_, ...), custom_call_target="tpu_custom_call" | custom-call | tf_op jit(solution)/shard_map/image/pallas_call | solution.py:548
  (5 shorter events, 0.0 us)
Async XLA Ops:
  1.1 6.4 %collective-permute-start.10 = (bf16[8,2176]{1,0:T(8,128)(2,1)S(1)}, bf16[8,2176]{1,0:T(8,128)(2,1)S(1)}, u32[]{:S(2)}, u32[]{:S(2)}) collective-permute-start(bf16[8,2176]{1,0:T(8,128)(2,1)S(1)} %get-tuple-element.50), channel_id=1, source_target_pairs={{0,8},{4,12},{8,0},{12,4},{1,9},{5,13},{9,1},{13,5},{2,10},{6,14},... | collective-permute-start | bytes 104456 | tf_op jit(solution)/shard_map/ppermute | solution.py:28
  7.5 4.3 %collective-permute-start.11 = (bf16[16,2176]{1,0:T(8,128)(2,1)S(1)}, bf16[16,2176]{1,0:T(8,128)(2,1)S(1)}, u32[]{:S(2)}, u32[]{:S(2)}) collective-permute-start(bf16[16,2176]{1,0:T(8,128)(2,1)S(1)} %pad_maximum_fusion.2), channel_id=1, source_target_pairs={{0,4},{4,0},{8,12},{12,8},{1,5},{5,1},{9,13},{13,9},{2,6},{6,2},{1... | collective-permute-start | bytes 208904 | tf_op jit(solution)/shard_map/ppermute | solution.py:28
  9.1 5.0 %collective-permute-start = (bf16[128,512]{1,0:T(8,128)(2,1)S(1)}, bf16[128,512]{1,0:T(8,128)(2,1)S(1)}, u32[]{:S(2)}, u32[]{:S(2)}) collective-permute-start(bf16[128,512]{1,0:T(8,128)(2,1)S(1)} %get-tuple-element.29), channel_id=1, source_target_pairs={{0,2},{2,0},{1,3},{3,1},{4,6},{6,4},{5,7},{7,5},{8,10},{10,8},{9,1... | collective-permute-start | bytes 393224 | tf_op jit(solution)/shard_map/ppermute | solution.py:28
  11.9 24.8 %collective-permute-start.12 = (bf16[32,2176]{1,0:T(8,128)(2,1)S(1)}, bf16[32,2176]{1,0:T(8,128)(2,1)S(1)}, u32[]{:S(2)}, u32[]{:S(2)}) collective-permute-start(bf16[32,2176]{1,0:T(8,128)(2,1)S(1)} %pad_maximum_fusion.1), channel_id=1, source_target_pairs={{0,1},{1,0},{2,3},{3,2},{4,5},{5,4},{6,7},{7,6},{8,9},{9,8},{10,11... | collective-permute-start | bytes 417800 | tf_op jit(solution)/shard_map/ppermute | solution.py:28
  14.5 5.9 %collective-permute-start.1 = (bf16[64,512]{1,0:T(8,128)(2,1)S(1)}, bf16[64,512]{1,0:T(8,128)(2,1)S(1)}, u32[]{:S(2)}, u32[]{:S(2)}) collective-permute-start(bf16[64,512]{1,0:T(8,128)(2,1)S(1)} %get-tuple-element.36), channel_id=1, source_target_pairs={{0,4},{4,0},{8,12},{12,8},{1,5},{5,1},{9,13},{13,9},{2,6},{6,2},{1... | collective-permute-start | bytes 196616 | tf_op jit(solution)/shard_map/ppermute | solution.py:28
  15.2 7.9 %collective-permute-start.2 = (bf16[64,512]{1,0:T(8,128)(2,1)S(1)}, bf16[64,512]{1,0:T(8,128)(2,1)S(1)}, u32[]{:S(2)}, u32[]{:S(2)}) collective-permute-start(bf16[64,512]{1,0:T(8,128)(2,1)S(1)} %get-tuple-element.37), channel_id=1, source_target_pairs={{0,8},{4,12},{8,0},{12,4},{1,9},{5,13},{9,1},{13,5},{2,10},{6,14},... | collective-permute-start | bytes 196616 | tf_op jit(solution)/shard_map/ppermute | solution.py:28
  18.0 6.1 %collective-permute-start.3 = (bf16[64,512]{1,0:T(8,128)(2,1)S(1)}, bf16[64,512]{1,0:T(8,128)(2,1)S(1)}, u32[]{:S(2)}, u32[]{:S(2)}) collective-permute-start(bf16[64,512]{1,0:T(8,128)(2,1)S(1)} %get-tuple-element.38), channel_id=1, source_target_pairs={{0,12},{4,8},{8,4},{12,0},{1,13},{5,9},{9,5},{13,1},{2,14},{6,10},... | collective-permute-start | bytes 196616 | tf_op jit(solution)/shard_map/ppermute | solution.py:28
  25.5 4.5 %collective-permute-start.4 = (bf16[32,1024]{1,0:T(8,128)(2,1)S(1)}, bf16[32,1024]{1,0:T(8,128)(2,1)S(1)}, u32[]{:S(2)}, u32[]{:S(2)}) collective-permute-start(bf16[32,1024]{1,0:T(8,128)(2,1)S(1)} %get-tuple-element.43), channel_id=1, source_target_pairs={{0,4},{4,0},{8,12},{12,8},{1,5},{5,1},{9,13},{13,9},{2,6},{6,2},{1... | collective-permute-start | bytes 196616 | tf_op jit(solution)/shard_map/ppermute | solution.py:28
  26.8 6.8 %collective-permute-start.5 = (bf16[32,1024]{1,0:T(8,128)(2,1)S(1)}, bf16[32,1024]{1,0:T(8,128)(2,1)S(1)}, u32[]{:S(2)}, u32[]{:S(2)}) collective-permute-start(bf16[32,1024]{1,0:T(8,128)(2,1)S(1)} %get-tuple-element.44), channel_id=1, source_target_pairs={{0,8},{4,12},{8,0},{12,4},{1,9},{5,13},{9,1},{13,5},{2,10},{6,14},... | collective-permute-start | bytes 196616 | tf_op jit(solution)/shard_map/ppermute | solution.py:28
  28.5 6.2 %collective-permute-start.6 = (bf16[32,1024]{1,0:T(8,128)(2,1)S(1)}, bf16[32,1024]{1,0:T(8,128)(2,1)S(1)}, u32[]{:S(2)}, u32[]{:S(2)}) collective-permute-start(bf16[32,1024]{1,0:T(8,128)(2,1)S(1)} %get-tuple-element.45), channel_id=1, source_target_pairs={{0,12},{4,8},{8,4},{12,0},{1,13},{5,9},{9,5},{13,1},{2,14},{6,10},... | collective-permute-start | bytes 196616 | tf_op jit(solution)/shard_map/ppermute | solution.py:28
  34.7 3.7 %collective-permute-start.7 = (bf16[32,256]{1,0:T(8,128)(2,1)S(1)}, bf16[32,256]{1,0:T(8,128)(2,1)S(1)}, u32[]{:S(2)}, u32[]{:S(2)}) collective-permute-start(bf16[32,256]{1,0:T(8,128)(2,1)S(1)} %get-tuple-element.47), channel_id=1, source_target_pairs={{0,1},{1,0},{2,3},{3,2},{4,5},{5,4},{6,7},{7,6},{8,9},{9,8},{10,11... | collective-permute-start | bytes 49160 | tf_op jit(solution)/shard_map/ppermute | solution.py:28
  34.8 3.8 %collective-permute-start.8 = (bf16[32,256]{1,0:T(8,128)(2,1)S(1)}, bf16[32,256]{1,0:T(8,128)(2,1)S(1)}, u32[]{:S(2)}, u32[]{:S(2)}) collective-permute-start(bf16[32,256]{1,0:T(8,128)(2,1)S(1)} %get-tuple-element.48), channel_id=1, source_target_pairs={{0,2},{1,3},{2,0},{3,1},{4,6},{5,7},{6,4},{7,5},{8,10},{9,11},{10,... | collective-permute-start | bytes 49160 | tf_op jit(solution)/shard_map/ppermute | solution.py:28
  36.3 3.2 %collective-permute-start.9 = (bf16[32,256]{1,0:T(8,128)(2,1)S(1)}, bf16[32,256]{1,0:T(8,128)(2,1)S(1)}, u32[]{:S(2)}, u32[]{:S(2)}) collective-permute-start(bf16[32,256]{1,0:T(8,128)(2,1)S(1)} %get-tuple-element.49), channel_id=1, source_target_pairs={{0,3},{1,2},{2,1},{3,0},{4,7},{5,6},{6,5},{7,4},{8,11},{9,10},{10,... | collective-permute-start | bytes 49160 | tf_op jit(solution)/shard_map/ppermute | solution.py:28

commit v3 on v2

--- a/solution.py
+++ b/solution.py
@@ -86,13 +86,19 @@
     return out
 
 
-def split_kernel(n_x, per, raw, taps_in, tile_in, *refs):
-    outs = refs[:n_x]
-    marked, held, taps, tile, lines, sent = refs[n_x:]
+def split_kernel(n_x, n_fixed, per, raw, taps_in, tile_in, first_in, *refs):
+    fixed, refs = refs[:n_fixed], refs[n_fixed:]
+    outs, refs = refs[:n_x], refs[n_x:]
+    marked, first = refs[:2]
+    brought, refs = refs[2 : n_fixed + 2], refs[n_fixed + 2 :]
+    held, taps, tile, lines, sent = refs
     my_x = lax.axis_index("range")
     copies = [pltpu.make_async_copy(raw.at[c], held.at[c], sent.at[c]) for c in range(2)]
     copies.append(pltpu.make_async_copy(taps_in, taps, sent.at[2]))
     copies.append(pltpu.make_async_copy(tile_in, tile, sent.at[3]))
+    copies.append(pltpu.make_async_copy(first_in.at[my_x], first, sent.at[4]))
+    for i in range(n_fixed):
+        copies.append(pltpu.make_async_copy(fixed[i], brought[i], sent.at[i + 5]))
     for copy in copies:
         copy.start()
     shard = raw.shape[1]
@@ -123,25 +129,7 @@
                 outs[k][c * tiles : (c + 1) * tiles, p * LANES : (p + 1) * LANES] = lines[
                     c, pl.ds((my_x ^ k) * per + p, tiles, stride=shard), :
                 ].astype(BF16)
-
-
-def ready_kernel(n_fixed, own, first, *refs):
-    fixed = refs[:n_fixed]
-    part, rest = refs[n_fixed : n_fixed + 2]
-    brought = refs[n_fixed + 2 : 2 * n_fixed + 2]
-    mine, sent = refs[2 * n_fixed + 2 :]
-    my_x = lax.axis_index("range")
-    copies = [
-        pltpu.make_async_copy(first.at[my_x, 0], mine, sent.at[0]),
-        pltpu.make_async_copy(first.at[my_x, pl.ds(1, rest.shape[0])], rest, sent.at[1]),
-    ]
-    for i in range(n_fixed):
-        copies.append(pltpu.make_async_copy(fixed[i], brought[i], sent.at[i + 2]))
-    for copy in copies:
-        copy.start()
-    copies[0].wait()
-    part[...] = dot(mine[...], own[...])
-    for copy in copies[1:]:
+    for copy in copies[4:]:
         copy.wait()
 
 
@@ -157,13 +145,13 @@
 
 
 def pulse_kernel(n_parts, n_z, per, *refs):
-    parts = refs[: n_parts - 1]
-    mixed, first, turn, second = refs[n_parts - 1 : n_parts + 3]
+    parts = refs[:n_parts]
+    first, turn, second = refs[n_parts : n_parts + 3]
     outs = refs[n_parts + 3 :]
     my_z = lax.axis_index("pulse")
-    mixed = mixed[...]
-    for k, part in enumerate(parts):
-        mixed = mixed + dot(first[k], part[...])
+    mixed = dot(first[0], parts[0][...])
+    for k in range(1, n_parts):
+        mixed = mixed + dot(first[k], parts[k][...])
     half = mixed.shape[0] // 2
     band = LANES // n_z
     picks = []
@@ -401,22 +389,27 @@
     turn3 = table_of(np.stack(phasor(np.arange(low), nt, grid, 1.0)), F32)
 
     piece = pltpu.VMEM((2 * tiles, per * LANES), BF16)
-    *pieces, marked = pl.pallas_call(
-        functools.partial(split_kernel, n_x, per),
-        in_specs=[HELD] * 3,
-        out_specs=[VMEM] * (n_x + 1),
-        out_shape=[piece] * n_x + [pltpu.VMEM((shard, width + LANES), BF16)],
+    fixed = (turn1, second)
+    split = pl.pallas_call(
+        functools.partial(split_kernel, n_x, len(fixed), per),
+        in_specs=[HELD] * (4 + len(fixed)),
+        out_specs=[VMEM] * (n_x + 2 + len(fixed)),
+        out_shape=[piece] * n_x
+        + [pltpu.VMEM((shard, width + LANES), BF16)]
+        + [pltpu.VMEM(first.shape[1:], BF16)]
+        + [pltpu.VMEM(f.shape, f.dtype) for f in fixed],
         scratch_shapes=[
             pltpu.VMEM(raw_echo.shape, BF16),
             pltpu.VMEM(azim_taps.shape, BF16),
             pltpu.SMEM((1, shard), jnp.int32),
             pltpu.VMEM((2, tiles * shard, LANES), F32),
-            pltpu.SemaphoreType.DMA((4,)),
+            pltpu.SemaphoreType.DMA((5 + len(fixed),)),
         ],
         name="split",
         **room,
-    )(*far(raw_echo, azim_taps, tile_col.T))
-    parts = []
+    )(*far(raw_echo, azim_taps, tile_col.T, first, *fixed))
+    pieces, (marked, first, turn1, second) = split[:n_x], split[n_x:]
+    parts = [pieces[0]]
     for k in range(1, n_x):
         parts.append(traded(pieces[k], "range", k))
 
@@ -427,23 +420,6 @@
             everyone = jnp.concatenate([everyone, traded(everyone, axis, k)], axis=0)
             k //= 2
 
-    fixed = (turn1, second)
-    part1, rest, turn1, second = pl.pallas_call(
-        functools.partial(ready_kernel, len(fixed)),
-        in_specs=[VMEM] + [HELD] * (1 + len(fixed)),
-        out_specs=[VMEM] * (2 + len(fixed)),
-        out_shape=[
-            pltpu.VMEM((2 * high, per * LANES), F32),
-            pltpu.VMEM((max(n_x - 1, 1), 2 * high, 2 * tiles), BF16),
-        ]
-        + [pltpu.VMEM(f.shape, f.dtype) for f in fixed],
-        scratch_shapes=[
-            pltpu.VMEM((2 * high, 2 * tiles), BF16),
-            pltpu.SemaphoreType.DMA((2 + len(fixed),)),
-        ],
-        name="ready",
-        **room,
-    )(*near(pieces[0]), *far(first, *fixed))
     fixed = (last, range_taps, table, turn3)
     turn2, last, range_taps, table, turn3 = pl.pallas_call(
         functools.partial(bring_kernel, len(fixed)),
@@ -465,7 +441,7 @@
         out_shape=[chunk] * n_z,
         name="pulse_transform",
         **room,
-    )(*near(*parts, part1, rest, turn1, second))
+    )(*near(*parts, first, turn1, second))
     moved = [chunks[0]]
     for k in range(1, n_z):
         moved.append(traded(chunks[k], "pulse", k))

time: 43.4 us -> 42.4 us (0.977)
  Pallas kernels: 11 us -> 10.1 us
    pallas_call x2 -> x1, Pallas kernels: 2.22 us -> 1.24 us  [program(): pl.pallas_call(functools.partial(split_kernel, n_x, len(fixed), per), in_...]
  transfers between devices with their start and end apart: 13 -> 13, of which waited for: 9 -> 10; matrix products, arithmetic and copies ran while one was open for 0% -> 0% of each run, Pallas kernels for 14% -> 12%
where the time goes in v3:
time: 42.4 us; the launch traced here: 42.2 us
  starting transfers between devices  18 us (42%)
  waiting for transfers between devices  14 us (33%)
  Pallas kernels  10.1 us (24%)
    ppermute x13, starting transfers between devices, traded(): return lax.ppermute(block, axis, [(i, i ^ k) for i in range(count)])  18 us
    ppermute x13, waiting for transfers between devices, traded(): return lax.ppermute(block, axis, [(i, i ^ k) for i in range(count)])  14 us
    pallas_call x1, Pallas kernels, program(): pl.pallas_call(functools.partial(image_kernel, (n_z, n_x, n_c, per), wide...  3.71 us
    pallas_call x1, Pallas kernels, program(): pl.pallas_call(make, in_specs=[VMEM] * 3, out_specs=VMEM, out_shape=pltpu...  1.69 us
    pallas_call x1, Pallas kernels, program(): pl.pallas_call(functools.partial(line_kernel, n_z, per, blocks, quads, to...  1.44 us
    pallas_call x1, Pallas kernels, program(): pl.pallas_call(functools.partial(bring_kernel, len(fixed)), in_specs=[HEL...  1.4 us
    pallas_call x1, Pallas kernels, program(): pl.pallas_call(functools.partial(split_kernel, n_x, len(fixed), per), in_...  1.24 us
  transfers between devices with their start and end apart: 13, of which 10 were waited for; matrix products, arithmetic and copies ran while one was open for 0% of the time, Pallas kernels for 12%

profile of v3, /device:TPU:0, one launch (start us, length us, event | category | flops | bytes accessed | tf_op | source)
XLA Modules:
  0.0 42.2 jit_solution(17316691984509514659)
XLA Ops:
  0.0 1.2 %split.1 = (bf16[128,512]{1,0:T(8,128)(2,1)S(1)}, bf16[128,512]{1,0:T(8,128)(2,1)S(1)}, bf16[8,2176]{1,0:T(8,128)(2,1)S(1)}, bf16[2,256,128]{2,1,0:T(8,128)(2,1)...) custom-call(bf16[2,8,8192]{2,1,0:T(8,128)(2,1)} %raw.1, bf16[8,2048]{1,0:T(8,128)(2,1)} %taps_in.1, ...), custom_call_target="tpu_custom_call" | custom-call | tf_op jit(solution)/shard_map/split/pallas_call | solution.py:393
  1.2 4.1 %collective-permute-start.10 = (bf16[8,2176]{1,0:T(8,128)(2,1)S(1)}, bf16[8,2176]{1,0:T(8,128)(2,1)S(1)}, u32[]{:S(2)}, u32[]{:S(2)}) collective-permute-start(bf16[8,2176]{1,0:T(8,128)(2,1)S(1)} %get-tuple-element.48), channel_id=1, source_target_pairs={{0,8},{4,12},{8,0},{12,4},{1,9},{5,13},{9,1},{13,5},{2,10},{6,14},... | collective-permute-start | bytes 104456 | tf_op jit(solution)/shard_map/ppermute | solution.py:28
  5.4 2.3 %collective-permute-done.10 = bf16[8,2176]{1,0:T(8,128)(2,1)S(1)} collective-permute-done((bf16[8,2176]{1,0:T(8,128)(2,1)S(1)}, bf16[8,2176]{1,0:T(8,128)(2,1)S(1)}, u32[]{:S(2)}, u32[]{:S(2)}) %collective-permute-start.10) | collective-permute-done | bytes 34848 | tf_op jit(solution)/shard_map/ppermute | solution.py:28
  7.7 1.5 %collective-permute-start.11 = (bf16[16,2176]{1,0:T(8,128)(2,1)S(1)}, bf16[16,2176]{1,0:T(8,128)(2,1)S(1)}, u32[]{:S(2)}, u32[]{:S(2)}) collective-permute-start(bf16[16,2176]{1,0:T(8,128)(2,1)S(1)} %pad_maximum_fusion.2), channel_id=1, source_target_pairs={{0,4},{4,0},{8,12},{12,8},{1,5},{5,1},{9,13},{13,9},{2,6},{6,2},{1... | collective-permute-start | bytes 208904 | tf_op jit(solution)/shard_map/ppermute | solution.py:28
  9.2 1.5 %collective-permute-start = (bf16[128,512]{1,0:T(8,128)(2,1)S(1)}, bf16[128,512]{1,0:T(8,128)(2,1)S(1)}, u32[]{:S(2)}, u32[]{:S(2)}) collective-permute-start(bf16[128,512]{1,0:T(8,128)(2,1)S(1)} %get-tuple-element.29), channel_id=1, source_target_pairs={{0,2},{2,0},{1,3},{3,1},{4,6},{6,4},{5,7},{7,5},{8,10},{10,8},{9,1... | collective-permute-start | bytes 393224 | tf_op jit(solution)/shard_map/ppermute | solution.py:28
  10.7 1.3 %collective-permute-done.11 = bf16[16,2176]{1,0:T(8,128)(2,1)S(1)} collective-permute-done((bf16[16,2176]{1,0:T(8,128)(2,1)S(1)}, bf16[16,2176]{1,0:T(8,128)(2,1)S(1)}, u32[]{:S(2)}, u32[]{:S(2)}) %collective-permute-start.11) | collective-permute-done | bytes 69664 | tf_op jit(solution)/shard_map/ppermute | solution.py:28
  12.0 0.1 collective-permute-start.12
  12.1 2.1 %collective-permute-done.refs_1_ = bf16[128,512]{1,0:T(8,128)(2,1)S(1)} collective-permute-done((bf16[128,512]{1,0:T(8,128)(2,1)S(1)}, bf16[128,512]{1,0:T(8,128)(2,1)S(1)}, u32[]{:S(2)}, u32[]{:S(2)}) %collective-permute-start) | collective-permute-done | bytes 131104 | tf_op jit(solution)/shard_map/ppermute | solution.py:28
  14.2 0.6 %pulse_transform.1 = (bf16[64,512]{1,0:T(8,128)(2,1)S(1)}, bf16[64,512]{1,0:T(8,128)(2,1)S(1)}, bf16[64,512]{1,0:T(8,128)(2,1)S(1)}, bf16[64,512]{1,0:T(8,128)(2,1)S(1)}) custom-call(bf16[128,512]{1,0:T(8,128)(2,1)S(1)} %get-tuple-element.28.refs_0_, bf16[128,512]{1,0:T(8,128)(2,1)S(1)} %collective-permute-done.refs_1_, ...), custom_call_target="tpu_custom_call" | custom-call | tf_op jit(solution)/shard_map/pulse_transform/pallas_call | solution.py:437
  14.7 0.6 %collective-permute-start.1 = (bf16[64,512]{1,0:T(8,128)(2,1)S(1)}, bf16[64,512]{1,0:T(8,128)(2,1)S(1)}, u32[]{:S(2)}, u32[]{:S(2)}) collective-permute-start(bf16[64,512]{1,0:T(8,128)(2,1)S(1)} %get-tuple-element.34), channel_id=1, source_target_pairs={{0,4},{4,0},{8,12},{12,8},{1,5},{5,1},{9,13},{13,9},{2,6},{6,2},{1... | collective-permute-start | bytes 196616 | tf_op jit(solution)/shard_map/ppermute | solution.py:28
  15.3 2.6 %collective-permute-start.2 = (bf16[64,512]{1,0:T(8,128)(2,1)S(1)}, bf16[64,512]{1,0:T(8,128)(2,1)S(1)}, u32[]{:S(2)}, u32[]{:S(2)}) collective-permute-start(bf16[64,512]{1,0:T(8,128)(2,1)S(1)} %get-tuple-element.35), channel_id=1, source_target_pairs={{0,8},{4,12},{8,0},{12,4},{1,9},{5,13},{9,1},{13,5},{2,10},{6,14},... | collective-permute-start | bytes 196616 | tf_op jit(solution)/shard_map/ppermute | solution.py:28
  17.9 1.3 %collective-permute-start.3 = (bf16[64,512]{1,0:T(8,128)(2,1)S(1)}, bf16[64,512]{1,0:T(8,128)(2,1)S(1)}, u32[]{:S(2)}, u32[]{:S(2)}) collective-permute-start(bf16[64,512]{1,0:T(8,128)(2,1)S(1)} %get-tuple-element.36), channel_id=1, source_target_pairs={{0,12},{4,8},{8,4},{12,0},{1,13},{5,9},{9,5},{13,1},{2,14},{6,10},... | collective-permute-start | bytes 196616 | tf_op jit(solution)/shard_map/ppermute | solution.py:28
  19.2 1.4 %bring.1 = (f32[2,128,128]{2,1,0:T(8,128)S(1)}, bf16[64,256]{1,0:T(8,128)(2,1)S(1)}, bf16[8,512,128]{2,1,0:T(8,128)(2,1)S(1)}, bf16[256,512]{1,0:T(8,128)(2,1)S(1)}, f32[2,16,256]{2,1,0:T(8,128)S(1)}) custom-call(f32[4,2,128,128]{3,2,1,0:T(8,128)} %constant.17.clone.turn, bf16[64,256]{1,0:T(8,128)(2,1)} %constant.18.clone.refs_0_, ...), custom_call_target="tpu_custom_call" | custom-call | tf_op jit(solution)/shard_map/bring/pallas_call | solution.py:424
  20.6 0.0 collective-permute-done.1.refs_1_
  20.6 0.4 collective-permute-done.2.refs_2_
  21.0 3.1 %collective-permute-done.3.refs_3_ = bf16[64,512]{1,0:T(8,128)(2,1)S(1)} collective-permute-done((bf16[64,512]{1,0:T(8,128)(2,1)S(1)}, bf16[64,512]{1,0:T(8,128)(2,1)S(1)}, u32[]{:S(2)}, u32[]{:S(2)}) %collective-permute-start.3) | collective-permute-done | bytes 65568 | tf_op jit(solution)/shard_map/ppermute | solution.py:28
  24.0 1.4 %line_transform.1 = (bf16[32,1024]{1,0:T(8,128)(2,1)S(1)}, bf16[32,1024]{1,0:T(8,128)(2,1)S(1)}, bf16[32,1024]{1,0:T(8,128)(2,1)S(1)}, bf16[32,1024]{1,0:T(8,128)(2,1)S(1)}) custom-call(bf16[64,512]{1,0:T(8,128)(2,1)S(1)} %get-tuple-element.33.refs_0_, bf16[64,512]{1,0:T(8,128)(2,1)S(1)} %collective-permute-done.1.refs_1_, ...), custom_call_target="tpu_custom_call" | custom-call | tf_op jit(solution)/shard_map/line_transform/pallas_call | solution.py:483
  25.5 0.8 %collective-permute-start.4 = (bf16[32,1024]{1,0:T(8,128)(2,1)S(1)}, bf16[32,1024]{1,0:T(8,128)(2,1)S(1)}, u32[]{:S(2)}, u32[]{:S(2)}) collective-permute-start(bf16[32,1024]{1,0:T(8,128)(2,1)S(1)} %get-tuple-element.41), channel_id=1, source_target_pairs={{0,4},{4,0},{8,12},{12,8},{1,5},{5,1},{9,13},{13,9},{2,6},{6,2},{1... | collective-permute-start | bytes 196616 | tf_op jit(solution)/shard_map/ppermute | solution.py:28
  26.2 1.4 %collective-permute-start.5 = (bf16[32,1024]{1,0:T(8,128)(2,1)S(1)}, bf16[32,1024]{1,0:T(8,128)(2,1)S(1)}, u32[]{:S(2)}, u32[]{:S(2)}) collective-permute-start(bf16[32,1024]{1,0:T(8,128)(2,1)S(1)} %get-tuple-element.42), channel_id=1, source_target_pairs={{0,8},{4,12},{8,0},{12,4},{1,9},{5,13},{9,1},{13,5},{2,10},{6,14},... | collective-permute-start | bytes 196616 | tf_op jit(solution)/shard_map/ppermute | solution.py:28
  27.6 2.3 %collective-permute-start.6 = (bf16[32,1024]{1,0:T(8,128)(2,1)S(1)}, bf16[32,1024]{1,0:T(8,128)(2,1)S(1)}, u32[]{:S(2)}, u32[]{:S(2)}) collective-permute-start(bf16[32,1024]{1,0:T(8,128)(2,1)S(1)} %get-tuple-element.43), channel_id=1, source_target_pairs={{0,12},{4,8},{8,4},{12,0},{1,13},{5,9},{9,5},{13,1},{2,14},{6,10},... | collective-permute-start | bytes 196616 | tf_op jit(solution)/shard_map/ppermute | solution.py:28
  29.9 0.5 %collective-permute-done.4.refs_1_ = bf16[32,1024]{1,0:T(8,128)(2,1)S(1)} collective-permute-done((bf16[32,1024]{1,0:T(8,128)(2,1)S(1)}, bf16[32,1024]{1,0:T(8,128)(2,1)S(1)}, u32[]{:S(2)}, u32[]{:S(2)}) %collective-permute-start.4) | collective-permute-done | bytes 65568 | tf_op jit(solution)/shard_map/ppermute | solution.py:28
  30.4 1.0 %collective-permute-done.5.refs_2_ = bf16[32,1024]{1,0:T(8,128)(2,1)S(1)} collective-permute-done((bf16[32,1024]{1,0:T(8,128)(2,1)S(1)}, bf16[32,1024]{1,0:T(8,128)(2,1)S(1)}, u32[]{:S(2)}, u32[]{:S(2)}) %collective-permute-start.5) | collective-permute-done | bytes 65568 | tf_op jit(solution)/shard_map/ppermute | solution.py:28
  31.4 2.3 %collective-permute-done.6.refs_3_ = bf16[32,1024]{1,0:T(8,128)(2,1)S(1)} collective-permute-done((bf16[32,1024]{1,0:T(8,128)(2,1)S(1)}, bf16[32,1024]{1,0:T(8,128)(2,1)S(1)}, u32[]{:S(2)}, u32[]{:S(2)}) %collective-permute-start.6) | collective-permute-done | bytes 65568 | tf_op jit(solution)/shard_map/ppermute | solution.py:28
  33.7 0.1 fold.1
  33.7 0.1 collective-permute-start.7
  33.8 1.6 %collective-permute-start.8 = (bf16[32,256]{1,0:T(8,128)(2,1)S(1)}, bf16[32,256]{1,0:T(8,128)(2,1)S(1)}, u32[]{:S(2)}, u32[]{:S(2)}) collective-permute-start(bf16[32,256]{1,0:T(8,128)(2,1)S(1)} %get-tuple-element.46), channel_id=1, source_target_pairs={{0,2},{1,3},{2,0},{3,1},{4,6},{5,7},{6,4},{7,5},{8,10},{9,11},{10,... | collective-permute-start | bytes 49160 | tf_op jit(solution)/shard_map/ppermute | solution.py:28
  35.4 0.3 collective-permute-start.9
  35.6 0.0 collective-permute-done.12
  35.7 1.7 %column_transform.1.refs_4_ = bf16[4096,128]{1,0:T(8,128)(2,1)S(1)} custom-call(bf16[64,2176]{1,0:T(8,128)(2,1)S(1)} %pad_maximum_fusion.taps, bf16[256,512]{1,0:T(8,128)(2,1)S(1)} %get-tuple-element.49.table, f32[2,16,256]{2,1,0:T(8,128)S(1)} %get-tuple-element.50.turn), custom_call_target="tpu_custom_call" | custom-call | tf_op jit(solution)/shard_map/column_transform/pallas_call | solution.py:458
  37.4 0.2 collective-permute-done.8.refs_2_
  37.6 0.9 %collective-permute-done.9.refs_3_ = bf16[32,256]{1,0:T(8,128)(2,1)S(1)} collective-permute-done((bf16[32,256]{1,0:T(8,128)(2,1)S(1)}, bf16[32,256]{1,0:T(8,128)(2,1)S(1)}, u32[]{:S(2)}, u32[]{:S(2)}) %collective-permute-start.9) | collective-permute-done | bytes 16416 | tf_op jit(solution)/shard_map/ppermute | solution.py:28
  38.5 3.7 %image.1 = f32[2,256,4096]{2,1,0:T(8,128)} custom-call(bf16[32,256]{1,0:T(8,128)(2,1)S(1)} %get-tuple-element.44.refs_0_, bf16[32,256]{1,0:T(8,128)(2,1)S(1)} %collective-permute-done.7.refs_1_, bf16[32,256]{1,0:T(8,128)(2,1)S(1)} %collective-permute-done.8.refs_2_, bf16[32,256]{1,0:T(8,128)(2,1)S(1)} %collective-permute-done.9.refs_3_, ...), custom_call_target="tpu_custom_call" | custom-call | tf_op jit(solution)/shard_map/image/pallas_call | solution.py:524
  (4 shorter events, 0.0 us)
Async XLA Ops:
  1.2 6.4 %collective-permute-start.10 = (bf16[8,2176]{1,0:T(8,128)(2,1)S(1)}, bf16[8,2176]{1,0:T(8,128)(2,1)S(1)}, u32[]{:S(2)}, u32[]{:S(2)}) collective-permute-start(bf16[8,2176]{1,0:T(8,128)(2,1)S(1)} %get-tuple-element.48), channel_id=1, source_target_pairs={{0,8},{4,12},{8,0},{12,4},{1,9},{5,13},{9,1},{13,5},{2,10},{6,14},... | collective-permute-start | bytes 104456 | tf_op jit(solution)/shard_map/ppermute | solution.py:28
  7.7 4.3 %collective-permute-start.11 = (bf16[16,2176]{1,0:T(8,128)(2,1)S(1)}, bf16[16,2176]{1,0:T(8,128)(2,1)S(1)}, u32[]{:S(2)}, u32[]{:S(2)}) collective-permute-start(bf16[16,2176]{1,0:T(8,128)(2,1)S(1)} %pad_maximum_fusion.2), channel_id=1, source_target_pairs={{0,4},{4,0},{8,12},{12,8},{1,5},{5,1},{9,13},{13,9},{2,6},{6,2},{1... | collective-permute-start | bytes 208904 | tf_op jit(solution)/shard_map/ppermute | solution.py:28
  9.2 5.0 %collective-permute-start = (bf16[128,512]{1,0:T(8,128)(2,1)S(1)}, bf16[128,512]{1,0:T(8,128)(2,1)S(1)}, u32[]{:S(2)}, u32[]{:S(2)}) collective-permute-start(bf16[128,512]{1,0:T(8,128)(2,1)S(1)} %get-tuple-element.29), channel_id=1, source_target_pairs={{0,2},{2,0},{1,3},{3,1},{4,6},{6,4},{5,7},{7,5},{8,10},{10,8},{9,1... | collective-permute-start | bytes 393224 | tf_op jit(solution)/shard_map/ppermute | solution.py:28
  12.0 23.6 %collective-permute-start.12 = (bf16[32,2176]{1,0:T(8,128)(2,1)S(1)}, bf16[32,2176]{1,0:T(8,128)(2,1)S(1)}, u32[]{:S(2)}, u32[]{:S(2)}) collective-permute-start(bf16[32,2176]{1,0:T(8,128)(2,1)S(1)} %pad_maximum_fusion.1), channel_id=1, source_target_pairs={{0,1},{1,0},{2,3},{3,2},{4,5},{5,4},{6,7},{7,6},{8,9},{9,8},{10,11... | collective-permute-start | bytes 417800 | tf_op jit(solution)/shard_map/ppermute | solution.py:28
  14.7 5.9 %collective-permute-start.1 = (bf16[64,512]{1,0:T(8,128)(2,1)S(1)}, bf16[64,512]{1,0:T(8,128)(2,1)S(1)}, u32[]{:S(2)}, u32[]{:S(2)}) collective-permute-start(bf16[64,512]{1,0:T(8,128)(2,1)S(1)} %get-tuple-element.34), channel_id=1, source_target_pairs={{0,4},{4,0},{8,12},{12,8},{1,5},{5,1},{9,13},{13,9},{2,6},{6,2},{1... | collective-permute-start | bytes 196616 | tf_op jit(solution)/shard_map/ppermute | solution.py:28
  15.3 5.7 %collective-permute-start.2 = (bf16[64,512]{1,0:T(8,128)(2,1)S(1)}, bf16[64,512]{1,0:T(8,128)(2,1)S(1)}, u32[]{:S(2)}, u32[]{:S(2)}) collective-permute-start(bf16[64,512]{1,0:T(8,128)(2,1)S(1)} %get-tuple-element.35), channel_id=1, source_target_pairs={{0,8},{4,12},{8,0},{12,4},{1,9},{5,13},{9,1},{13,5},{2,10},{6,14},... | collective-permute-start | bytes 196616 | tf_op jit(solution)/shard_map/ppermute | solution.py:28
  17.9 6.2 %collective-permute-start.3 = (bf16[64,512]{1,0:T(8,128)(2,1)S(1)}, bf16[64,512]{1,0:T(8,128)(2,1)S(1)}, u32[]{:S(2)}, u32[]{:S(2)}) collective-permute-start(bf16[64,512]{1,0:T(8,128)(2,1)S(1)} %get-tuple-element.36), channel_id=1, source_target_pairs={{0,12},{4,8},{8,4},{12,0},{1,13},{5,9},{9,5},{13,1},{2,14},{6,10},... | collective-permute-start | bytes 196616 | tf_op jit(solution)/shard_map/ppermute | solution.py:28
  25.5 4.9 %collective-permute-start.4 = (bf16[32,1024]{1,0:T(8,128)(2,1)S(1)}, bf16[32,1024]{1,0:T(8,128)(2,1)S(1)}, u32[]{:S(2)}, u32[]{:S(2)}) collective-permute-start(bf16[32,1024]{1,0:T(8,128)(2,1)S(1)} %get-tuple-element.41), channel_id=1, source_target_pairs={{0,4},{4,0},{8,12},{12,8},{1,5},{5,1},{9,13},{13,9},{2,6},{6,2},{1... | collective-permute-start | bytes 196616 | tf_op jit(solution)/shard_map/ppermute | solution.py:28
  26.2 5.2 %collective-permute-start.5 = (bf16[32,1024]{1,0:T(8,128)(2,1)S(1)}, bf16[32,1024]{1,0:T(8,128)(2,1)S(1)}, u32[]{:S(2)}, u32[]{:S(2)}) collective-permute-start(bf16[32,1024]{1,0:T(8,128)(2,1)S(1)} %get-tuple-element.42), channel_id=1, source_target_pairs={{0,8},{4,12},{8,0},{12,4},{1,9},{5,13},{9,1},{13,5},{2,10},{6,14},... | collective-permute-start | bytes 196616 | tf_op jit(solution)/shard_map/ppermute | solution.py:28
  27.6 6.1 %collective-permute-start.6 = (bf16[32,1024]{1,0:T(8,128)(2,1)S(1)}, bf16[32,1024]{1,0:T(8,128)(2,1)S(1)}, u32[]{:S(2)}, u32[]{:S(2)}) collective-permute-start(bf16[32,1024]{1,0:T(8,128)(2,1)S(1)} %get-tuple-element.43), channel_id=1, source_target_pairs={{0,12},{4,8},{8,4},{12,0},{1,13},{5,9},{9,5},{13,1},{2,14},{6,10},... | collective-permute-start | bytes 196616 | tf_op jit(solution)/shard_map/ppermute | solution.py:28
  33.7 3.7 %collective-permute-start.7 = (bf16[32,256]{1,0:T(8,128)(2,1)S(1)}, bf16[32,256]{1,0:T(8,128)(2,1)S(1)}, u32[]{:S(2)}, u32[]{:S(2)}) collective-permute-start(bf16[32,256]{1,0:T(8,128)(2,1)S(1)} %get-tuple-element.45), channel_id=1, source_target_pairs={{0,1},{1,0},{2,3},{3,2},{4,5},{5,4},{6,7},{7,6},{8,9},{9,8},{10,11... | collective-permute-start | bytes 49160 | tf_op jit(solution)/shard_map/ppermute | solution.py:28
  33.8 3.8 %collective-permute-start.8 = (bf16[32,256]{1,0:T(8,128)(2,1)S(1)}, bf16[32,256]{1,0:T(8,128)(2,1)S(1)}, u32[]{:S(2)}, u32[]{:S(2)}) collective-permute-start(bf16[32,256]{1,0:T(8,128)(2,1)S(1)} %get-tuple-element.46), channel_id=1, source_target_pairs={{0,2},{1,3},{2,0},{3,1},{4,6},{5,7},{6,4},{7,5},{8,10},{9,11},{10,... | collective-permute-start | bytes 49160 | tf_op jit(solution)/shard_map/ppermute | solution.py:28
  35.4 3.2 %collective-permute-start.9 = (bf16[32,256]{1,0:T(8,128)(2,1)S(1)}, bf16[32,256]{1,0:T(8,128)(2,1)S(1)}, u32[]{:S(2)}, u32[]{:S(2)}) collective-permute-start(bf16[32,256]{1,0:T(8,128)(2,1)S(1)} %get-tuple-element.47), channel_id=1, source_target_pairs={{0,3},{1,2},{2,1},{3,0},{4,7},{5,6},{6,5},{7,4},{8,11},{9,10},{10,... | collective-permute-start | bytes 49160 | tf_op jit(solution)/shard_map/ppermute | solution.py:28

commit v4 on v2

--- a/solution.py
+++ b/solution.py
@@ -182,7 +182,7 @@
             outs[k][:, p * half : (p + 1) * half] = done[2 * band * k : 2 * band * (k + 1), :]
 
 
-def line_kernel(n_z, per, blocks, quads, total_blocks, *refs):
+def line_plain(n_z, per, blocks, quads, total_blocks, *refs):
     chunks = refs[:n_z]
     taps, turn, last = refs[n_z : n_z + 3]
     outs = refs[n_z + 3 : 2 * n_z + 3]
@@ -254,6 +254,115 @@
             outs[k][:, s * LANES : (s + 1) * LANES] = jnp.concatenate(blocks_of, axis=0).astype(BF16)
 
 
+def swapped_rows(values):
+    row = lax.broadcasted_iota(jnp.int32, values[0].shape, 0)
+    for d in (4, 2, 1):
+        lower = (row & d) == 0
+        out = list(values)
+        for i in range(8):
+            if i & d == 0:
+                a, b = values[i], values[i + d]
+                out[i] = jnp.where(lower, a, pltpu.roll(b, d, 0))
+                out[i + d] = jnp.where(lower, pltpu.roll(a, 8 - d, 0), b)
+        values = out
+    return values
+
+
+def line_kernel(n_z, per, blocks, quads, total_blocks, *refs):
+    chunks = refs[:n_z]
+    taps, turn, last = refs[n_z : n_z + 3]
+    outs = refs[n_z + 3 : 2 * n_z + 3]
+    sums, spun, rows = refs[2 * n_z + 3 :]
+    my_z = lax.axis_index("pulse")
+    band = blocks * quads
+    pulses = n_z * per
+    ky = []
+    for t in range(0, band, 16):
+        groups = []
+        for c in range(2):
+            for g in range(0, pulses, 8):
+                tiles = []
+                for k, p in (divmod(m, per) for m in range(g, g + 8)):
+                    tiles.append(
+                        chunks[k][
+                            c * band + t : c * band + t + 16, p * LANES : (p + 1) * LANES
+                        ].astype(F32)
+                    )
+                groups.append(
+                    swapped_rows([v[:8] for v in tiles]) + swapped_rows([v[8:] for v in tiles])
+                )
+        for b in range(16 // quads):
+            lhs = jnp.concatenate(
+                [
+                    jnp.concatenate([g[b * quads + q] for g in groups], axis=0).astype(BF16)
+                    for q in range(quads)
+                ],
+                axis=1,
+            )
+            line = dot(lhs, taps[t // quads + b])
+            ky.append((line[:pulses], line[pulses:]))
+    quarter = total_blocks // 4
+    for y in range(quarter):
+        classes = []
+        for m in range(4):
+            acc = None
+            for b in range(m, blocks, 4):
+                re, im = ky[b]
+                angle = 2.0 * math.pi * (b * y % total_blocks) / total_blocks
+                co, si = math.cos(angle), math.sin(angle)
+                if b * y == 0:
+                    term = (re, im)
+                else:
+                    term = (re * co - im * si, re * si + im * co)
+                acc = term if acc is None else (acc[0] + term[0], acc[1] + term[1])
+            classes.append(acc)
+        for r, (re, im) in enumerate(fourier(classes, 1)):
+            at = (y + r * quarter) * pulses
+            sums[0, at : at + pulses, :] = re
+            sums[1, at : at + pulses, :] = im
+    fold = LANES // total_blocks
+    for g in range(0, pulses, 8):
+        for y in range(0, total_blocks, 16):
+            parts = []
+            for c in range(2):
+                halves = [
+                    swapped_rows(
+                        [sums[c, u * pulses + g : u * pulses + g + 8, :] for u in range(h, h + 8)]
+                    )
+                    for h in (y, y + 8)
+                ]
+                parts.append([jnp.concatenate(pair, axis=0) for pair in zip(*halves)])
+            for f in range(fold):
+                at = slice(f * total_blocks + y, f * total_blocks + y + 16)
+                tc, ts = turn[0, at, :], turn[1, at, :]
+                for i in range(8):
+                    re, im = parts[0][i], parts[1][i]
+                    spun[g + i, at, :LANES] = (re * tc - im * ts).astype(BF16)
+                    spun[g + i, at, LANES:] = (re * ts + im * tc).astype(BF16)
+    tops = last.shape[0] // 2
+    for m in range(pulses):
+        done = dot(last[...], spun[m], NT)
+        for c in range(2):
+            at = (c * pulses + m) * tops
+            rows[at : at + tops, :] = done[c * tops : (c + 1) * tops, :]
+    share = tops // n_z
+    for k in range(n_z):
+        for s in range(0, share, 8):
+            for c in range(2):
+                groups = []
+                for g in range(0, pulses, 8):
+                    tiles = []
+                    for z, p in (divmod(m, per) for m in range(g, g + 8)):
+                        at = (c * pulses + (z ^ k) * per + p) * tops + s
+                        at = pl.multiple_of(at + (my_z ^ k) * share, 8)
+                        tiles.append(rows[pl.ds(at, 8), :])
+                    groups.append(swapped_rows(tiles))
+                for i in range(8):
+                    outs[k][
+                        c * pulses : (c + 1) * pulses, (s + i) * LANES : (s + i + 1) * LANES
+                    ] = jnp.concatenate([g[i] for g in groups], axis=0).astype(BF16)
+
+
 def fold_kernel(n_z, n_c, *refs):
     parts, outs, total = refs[:n_z], refs[n_z:-1], refs[-1]
     acc = parts[0][...].astype(F32)
@@ -504,16 +613,22 @@
         )(everyone, table, turn3)
 
     quads = block_bins // LANES
+    paired = blocks >= 4 and blocks * quads % 16 == 0 and tops // n_z % 8 == 0 and pulses % 16 == 0
+    if paired:
+        line_make, first_scratch = line_kernel, []
+        spun = [pltpu.VMEM((pulses, LANES, 2 * LANES), BF16)]
+    else:
+        line_make, spun = line_plain, []
+        first_scratch = [pltpu.VMEM((2 * pulses * blocks * quads, LANES), F32)]
     lines = pl.pallas_call(
-        functools.partial(line_kernel, n_z, per, blocks, quads, total_blocks),
+        functools.partial(line_make, n_z, per, blocks, quads, total_blocks),
         in_specs=[VMEM] * (n_z + 3),
         out_specs=[VMEM] * n_z,
         out_shape=[pltpu.VMEM((2 * pulses, grid // n_z), BF16)] * n_z,
-        scratch_shapes=[
-            pltpu.VMEM((2 * pulses * blocks * quads, LANES), F32),
-            pltpu.VMEM((2, total_blocks * pulses, LANES), F32),
-            pltpu.VMEM((2 * pulses * tops, LANES), F32),
-        ],
+        scratch_shapes=first_scratch
+        + [pltpu.VMEM((2, total_blocks * pulses, LANES), F32)]
+        + spun
+        + [pltpu.VMEM((2 * pulses * tops, LANES), F32)],
         name="line_transform",
         **room,
     )(*near(*moved, range_taps, turn2, last))

time: 43.4 us -> 43.1 us (level)
  no operation moved by 1% of the time
where the time goes in v4:
time: 43.1 us; the launch traced here: 43 us
  starting transfers between devices  18 us (42%)
  waiting for transfers between devices  14 us (32%)
  Pallas kernels  10.7 us (25%)
    ppermute x13, starting transfers between devices, traded(): return lax.ppermute(block, axis, [(i, i ^ k) for i in range(count)])  18 us
    ppermute x13, waiting for transfers between devices, traded(): return lax.ppermute(block, axis, [(i, i ^ k) for i in range(count)])  14 us
    pallas_call x1, Pallas kernels, program(): pl.pallas_call(functools.partial(image_kernel, (n_z, n_x, n_c, per), wide...  3.71 us
    pallas_call x1, Pallas kernels, program(): pl.pallas_call(make, in_specs=[VMEM] * 3, out_specs=VMEM, out_shape=pltpu...  1.69 us
    pallas_call x1, Pallas kernels, program(): pl.pallas_call(functools.partial(bring_kernel, len(fixed)), in_specs=[HEL...  1.4 us
    pallas_call x1, Pallas kernels, program(): pl.pallas_call(functools.partial(line_make, n_z, per, blocks, quads, tota...  1.17 us
    pallas_call x1, Pallas kernels, program(): pl.pallas_call(functools.partial(ready_kernel, len(fixed)), in_specs=[VME...  1.11 us
    pallas_call x1, Pallas kernels, program(): pl.pallas_call(functools.partial(split_kernel, n_x, per), in_specs=[HELD]...  1.11 us
  transfers between devices with their start and end apart: 13, of which 9 were waited for; matrix products, arithmetic and copies ran while one was open for 0% of the time, Pallas kernels for 14%

profile of v4, /device:TPU:0, one launch (start us, length us, event | category | flops | bytes accessed | tf_op | source)
XLA Modules:
  0.0 43.0 jit_solution(16318995150996463071)
XLA Ops:
  0.0 1.1 %split.1 = (bf16[128,512]{1,0:T(8,128)(2,1)S(1)}, bf16[128,512]{1,0:T(8,128)(2,1)S(1)}, bf16[8,2176]{1,0:T(8,128)(2,1)S(1)}) custom-call(bf16[2,8,8192]{2,1,0:T(8,128)(2,1)} %raw.1, bf16[8,2048]{1,0:T(8,128)(2,1)} %taps_in.1, s32[1,8]{1,0:T(1,128)} %bitcast.1), custom_call_target="tpu_custom_call" | custom-call | tf_op jit(solution)/shard_map/split/pallas_call | solution.py:513
  1.1 4.1 %collective-permute-start.10 = (bf16[8,2176]{1,0:T(8,128)(2,1)S(1)}, bf16[8,2176]{1,0:T(8,128)(2,1)S(1)}, u32[]{:S(2)}, u32[]{:S(2)}) collective-permute-start(bf16[8,2176]{1,0:T(8,128)(2,1)S(1)} %get-tuple-element.50), channel_id=1, source_target_pairs={{0,8},{4,12},{8,0},{12,4},{1,9},{5,13},{9,1},{13,5},{2,10},{6,14},... | collective-permute-start | bytes 104456 | tf_op jit(solution)/shard_map/ppermute | solution.py:28
  5.2 2.3 %collective-permute-done.10 = bf16[8,2176]{1,0:T(8,128)(2,1)S(1)} collective-permute-done((bf16[8,2176]{1,0:T(8,128)(2,1)S(1)}, bf16[8,2176]{1,0:T(8,128)(2,1)S(1)}, u32[]{:S(2)}, u32[]{:S(2)}) %collective-permute-start.10) | collective-permute-done | bytes 34848 | tf_op jit(solution)/shard_map/ppermute | solution.py:28
  7.5 1.5 %collective-permute-start.11 = (bf16[16,2176]{1,0:T(8,128)(2,1)S(1)}, bf16[16,2176]{1,0:T(8,128)(2,1)S(1)}, u32[]{:S(2)}, u32[]{:S(2)}) collective-permute-start(bf16[16,2176]{1,0:T(8,128)(2,1)S(1)} %pad_maximum_fusion.2), channel_id=1, source_target_pairs={{0,4},{4,0},{8,12},{12,8},{1,5},{5,1},{9,13},{13,9},{2,6},{6,2},{1... | collective-permute-start | bytes 208904 | tf_op jit(solution)/shard_map/ppermute | solution.py:28
  9.1 1.5 %collective-permute-start = (bf16[128,512]{1,0:T(8,128)(2,1)S(1)}, bf16[128,512]{1,0:T(8,128)(2,1)S(1)}, u32[]{:S(2)}, u32[]{:S(2)}) collective-permute-start(bf16[128,512]{1,0:T(8,128)(2,1)S(1)} %get-tuple-element.29), channel_id=1, source_target_pairs={{0,2},{2,0},{1,3},{3,1},{4,6},{6,4},{5,7},{7,5},{8,10},{10,8},{9,1... | collective-permute-start | bytes 393224 | tf_op jit(solution)/shard_map/ppermute | solution.py:28
  10.6 1.3 %collective-permute-done.11 = bf16[16,2176]{1,0:T(8,128)(2,1)S(1)} collective-permute-done((bf16[16,2176]{1,0:T(8,128)(2,1)S(1)}, bf16[16,2176]{1,0:T(8,128)(2,1)S(1)}, u32[]{:S(2)}, u32[]{:S(2)}) %collective-permute-start.11) | collective-permute-done | bytes 69664 | tf_op jit(solution)/shard_map/ppermute | solution.py:28
  11.9 0.1 collective-permute-start.12
  11.9 1.1 %ready.1 = (f32[256,512]{1,0:T(8,128)S(1)}, bf16[1,256,128]{2,1,0:T(8,128)(2,1)S(1)}, f32[2,128,128]{2,1,0:T(8,128)S(1)}, bf16[256,256]{1,0:T(8,128)(2,1)S(1)}) custom-call(bf16[128,512]{1,0:T(8,128)(2,1)S(1)} %get-tuple-element.30.own, bf16[2,2,256,128]{3,2,1,0:T(8,128)(2,1)} %constant.14.clone.first, f32[2,128,128]{2,1,0:T(8,128)} %constant.15.clone.refs_0_, ...), custom_call_target="tpu_custom_call" | custom-call | tf_op jit(solution)/shard_map/ready/pallas_call | solution.py:540
  13.1 1.0 %collective-permute-done.refs_0_ = bf16[128,512]{1,0:T(8,128)(2,1)S(1)} collective-permute-done((bf16[128,512]{1,0:T(8,128)(2,1)S(1)}, bf16[128,512]{1,0:T(8,128)(2,1)S(1)}, u32[]{:S(2)}, u32[]{:S(2)}) %collective-permute-start) | collective-permute-done | bytes 131104 | tf_op jit(solution)/shard_map/ppermute | solution.py:28
  14.0 0.5 %pulse_transform.1 = (bf16[64,512]{1,0:T(8,128)(2,1)S(1)}, bf16[64,512]{1,0:T(8,128)(2,1)S(1)}, bf16[64,512]{1,0:T(8,128)(2,1)S(1)}, bf16[64,512]{1,0:T(8,128)(2,1)S(1)}) custom-call(bf16[128,512]{1,0:T(8,128)(2,1)S(1)} %collective-permute-done.refs_0_, f32[256,512]{1,0:T(8,128)S(1)} %get-tuple-element.31.refs_1_, ...), custom_call_target="tpu_custom_call" | custom-call | tf_op jit(solution)/shard_map/pulse_transform/pallas_call | solution.py:570
  14.5 0.6 %collective-permute-start.1 = (bf16[64,512]{1,0:T(8,128)(2,1)S(1)}, bf16[64,512]{1,0:T(8,128)(2,1)S(1)}, u32[]{:S(2)}, u32[]{:S(2)}) collective-permute-start(bf16[64,512]{1,0:T(8,128)(2,1)S(1)} %get-tuple-element.36), channel_id=1, source_target_pairs={{0,4},{4,0},{8,12},{12,8},{1,5},{5,1},{9,13},{13,9},{2,6},{6,2},{1... | collective-permute-start | bytes 196616 | tf_op jit(solution)/shard_map/ppermute | solution.py:28
  15.2 2.8 %collective-permute-start.2 = (bf16[64,512]{1,0:T(8,128)(2,1)S(1)}, bf16[64,512]{1,0:T(8,128)(2,1)S(1)}, u32[]{:S(2)}, u32[]{:S(2)}) collective-permute-start(bf16[64,512]{1,0:T(8,128)(2,1)S(1)} %get-tuple-element.37), channel_id=1, source_target_pairs={{0,8},{4,12},{8,0},{12,4},{1,9},{5,13},{9,1},{13,5},{2,10},{6,14},... | collective-permute-start | bytes 196616 | tf_op jit(solution)/shard_map/ppermute | solution.py:28
  18.0 1.0 %collective-permute-start.3 = (bf16[64,512]{1,0:T(8,128)(2,1)S(1)}, bf16[64,512]{1,0:T(8,128)(2,1)S(1)}, u32[]{:S(2)}, u32[]{:S(2)}) collective-permute-start(bf16[64,512]{1,0:T(8,128)(2,1)S(1)} %get-tuple-element.38), channel_id=1, source_target_pairs={{0,12},{4,8},{8,4},{12,0},{1,13},{5,9},{9,5},{13,1},{2,14},{6,10},... | collective-permute-start | bytes 196616 | tf_op jit(solution)/shard_map/ppermute | solution.py:28
  19.0 1.4 %bring.1 = (f32[2,128,128]{2,1,0:T(8,128)S(1)}, bf16[64,256]{1,0:T(8,128)(2,1)S(1)}, bf16[8,512,128]{2,1,0:T(8,128)(2,1)S(1)}, bf16[256,512]{1,0:T(8,128)(2,1)S(1)}, f32[2,16,256]{2,1,0:T(8,128)S(1)}) custom-call(f32[4,2,128,128]{3,2,1,0:T(8,128)} %constant.17.clone.turn, bf16[64,256]{1,0:T(8,128)(2,1)} %constant.18.clone.refs_0_, ...), custom_call_target="tpu_custom_call" | custom-call | tf_op jit(solution)/shard_map/bring/pallas_call | solution.py:557
  20.4 0.0 collective-permute-done.1.refs_1_
  20.4 2.7 %collective-permute-done.2.refs_2_ = bf16[64,512]{1,0:T(8,128)(2,1)S(1)} collective-permute-done((bf16[64,512]{1,0:T(8,128)(2,1)S(1)}, bf16[64,512]{1,0:T(8,128)(2,1)S(1)}, u32[]{:S(2)}, u32[]{:S(2)}) %collective-permute-start.2) | collective-permute-done | bytes 65568 | tf_op jit(solution)/shard_map/ppermute | solution.py:28
  23.1 1.0 %collective-permute-done.3.refs_3_ = bf16[64,512]{1,0:T(8,128)(2,1)S(1)} collective-permute-done((bf16[64,512]{1,0:T(8,128)(2,1)S(1)}, bf16[64,512]{1,0:T(8,128)(2,1)S(1)}, u32[]{:S(2)}, u32[]{:S(2)}) %collective-permute-start.3) | collective-permute-done | bytes 65568 | tf_op jit(solution)/shard_map/ppermute | solution.py:28
  24.1 1.2 %line_transform.1 = (bf16[32,1024]{1,0:T(8,128)(2,1)S(1)}, bf16[32,1024]{1,0:T(8,128)(2,1)S(1)}, bf16[32,1024]{1,0:T(8,128)(2,1)S(1)}, bf16[32,1024]{1,0:T(8,128)(2,1)S(1)}) custom-call(bf16[64,512]{1,0:T(8,128)(2,1)S(1)} %get-tuple-element.35.refs_0_, bf16[64,512]{1,0:T(8,128)(2,1)S(1)} %collective-permute-done.1.refs_1_, ...), custom_call_target="tpu_custom_call" | custom-call | tf_op jit(solution)/shard_map/line_transform/pallas_call | solution.py:623
  25.3 1.2 %collective-permute-start.4 = (bf16[32,1024]{1,0:T(8,128)(2,1)S(1)}, bf16[32,1024]{1,0:T(8,128)(2,1)S(1)}, u32[]{:S(2)}, u32[]{:S(2)}) collective-permute-start(bf16[32,1024]{1,0:T(8,128)(2,1)S(1)} %get-tuple-element.43), channel_id=1, source_target_pairs={{0,4},{4,0},{8,12},{12,8},{1,5},{5,1},{9,13},{13,9},{2,6},{6,2},{1... | collective-permute-start | bytes 196616 | tf_op jit(solution)/shard_map/ppermute | solution.py:28
  26.5 1.7 %collective-permute-start.5 = (bf16[32,1024]{1,0:T(8,128)(2,1)S(1)}, bf16[32,1024]{1,0:T(8,128)(2,1)S(1)}, u32[]{:S(2)}, u32[]{:S(2)}) collective-permute-start(bf16[32,1024]{1,0:T(8,128)(2,1)S(1)} %get-tuple-element.44), channel_id=1, source_target_pairs={{0,8},{4,12},{8,0},{12,4},{1,9},{5,13},{9,1},{13,5},{2,10},{6,14},... | collective-permute-start | bytes 196616 | tf_op jit(solution)/shard_map/ppermute | solution.py:28
  28.2 1.5 %collective-permute-start.6 = (bf16[32,1024]{1,0:T(8,128)(2,1)S(1)}, bf16[32,1024]{1,0:T(8,128)(2,1)S(1)}, u32[]{:S(2)}, u32[]{:S(2)}) collective-permute-start(bf16[32,1024]{1,0:T(8,128)(2,1)S(1)} %get-tuple-element.45), channel_id=1, source_target_pairs={{0,12},{4,8},{8,4},{12,0},{1,13},{5,9},{9,5},{13,1},{2,14},{6,10},... | collective-permute-start | bytes 196616 | tf_op jit(solution)/shard_map/ppermute | solution.py:28
  29.7 0.0 collective-permute-done.4.refs_1_
  29.7 3.6 %collective-permute-done.5.refs_2_ = bf16[32,1024]{1,0:T(8,128)(2,1)S(1)} collective-permute-done((bf16[32,1024]{1,0:T(8,128)(2,1)S(1)}, bf16[32,1024]{1,0:T(8,128)(2,1)S(1)}, u32[]{:S(2)}, u32[]{:S(2)}) %collective-permute-start.5) | collective-permute-done | bytes 65568 | tf_op jit(solution)/shard_map/ppermute | solution.py:28
  33.3 1.1 %collective-permute-done.6.refs_3_ = bf16[32,1024]{1,0:T(8,128)(2,1)S(1)} collective-permute-done((bf16[32,1024]{1,0:T(8,128)(2,1)S(1)}, bf16[32,1024]{1,0:T(8,128)(2,1)S(1)}, u32[]{:S(2)}, u32[]{:S(2)}) %collective-permute-start.6) | collective-permute-done | bytes 65568 | tf_op jit(solution)/shard_map/ppermute | solution.py:28
  34.4 0.1 fold.1
  34.5 0.1 collective-permute-start.7
  34.5 1.6 %collective-permute-start.8 = (bf16[32,256]{1,0:T(8,128)(2,1)S(1)}, bf16[32,256]{1,0:T(8,128)(2,1)S(1)}, u32[]{:S(2)}, u32[]{:S(2)}) collective-permute-start(bf16[32,256]{1,0:T(8,128)(2,1)S(1)} %get-tuple-element.48), channel_id=1, source_target_pairs={{0,2},{1,3},{2,0},{3,1},{4,6},{5,7},{6,4},{7,5},{8,10},{9,11},{10,... | collective-permute-start | bytes 49160 | tf_op jit(solution)/shard_map/ppermute | solution.py:28
  36.1 0.3 collective-permute-start.9
  36.4 1.7 %column_transform.1.refs_4_ = bf16[4096,128]{1,0:T(8,128)(2,1)S(1)} custom-call(bf16[64,2176]{1,0:T(8,128)(2,1)S(1)} %pad_maximum_fusion.taps, bf16[256,512]{1,0:T(8,128)(2,1)S(1)} %get-tuple-element.51.table, f32[2,16,256]{2,1,0:T(8,128)S(1)} %get-tuple-element.52.turn), custom_call_target="tpu_custom_call" | custom-call | tf_op jit(solution)/shard_map/column_transform/pallas_call | solution.py:591
  38.1 0.2 collective-permute-done.8.refs_2_
  38.3 0.9 %collective-permute-done.9.refs_3_ = bf16[32,256]{1,0:T(8,128)(2,1)S(1)} collective-permute-done((bf16[32,256]{1,0:T(8,128)(2,1)S(1)}, bf16[32,256]{1,0:T(8,128)(2,1)S(1)}, u32[]{:S(2)}, u32[]{:S(2)}) %collective-permute-start.9) | collective-permute-done | bytes 16416 | tf_op jit(solution)/shard_map/ppermute | solution.py:28
  39.3 3.7 %image.1 = f32[2,256,4096]{2,1,0:T(8,128)} custom-call(bf16[32,256]{1,0:T(8,128)(2,1)S(1)} %get-tuple-element.46.refs_0_, bf16[32,256]{1,0:T(8,128)(2,1)S(1)} %collective-permute-done.7.refs_1_, bf16[32,256]{1,0:T(8,128)(2,1)S(1)} %collective-permute-done.8.refs_2_, bf16[32,256]{1,0:T(8,128)(2,1)S(1)} %collective-permute-done.9.refs_3_, ...), custom_call_target="tpu_custom_call" | custom-call | tf_op jit(solution)/shard_map/image/pallas_call | solution.py:663
  (5 shorter events, 0.0 us)
Async XLA Ops:
  1.1 6.4 %collective-permute-start.10 = (bf16[8,2176]{1,0:T(8,128)(2,1)S(1)}, bf16[8,2176]{1,0:T(8,128)(2,1)S(1)}, u32[]{:S(2)}, u32[]{:S(2)}) collective-permute-start(bf16[8,2176]{1,0:T(8,128)(2,1)S(1)} %get-tuple-element.50), channel_id=1, source_target_pairs={{0,8},{4,12},{8,0},{12,4},{1,9},{5,13},{9,1},{13,5},{2,10},{6,14},... | collective-permute-start | bytes 104456 | tf_op jit(solution)/shard_map/ppermute | solution.py:28
  7.5 4.3 %collective-permute-start.11 = (bf16[16,2176]{1,0:T(8,128)(2,1)S(1)}, bf16[16,2176]{1,0:T(8,128)(2,1)S(1)}, u32[]{:S(2)}, u32[]{:S(2)}) collective-permute-start(bf16[16,2176]{1,0:T(8,128)(2,1)S(1)} %pad_maximum_fusion.2), channel_id=1, source_target_pairs={{0,4},{4,0},{8,12},{12,8},{1,5},{5,1},{9,13},{13,9},{2,6},{6,2},{1... | collective-permute-start | bytes 208904 | tf_op jit(solution)/shard_map/ppermute | solution.py:28
  9.1 5.0 %collective-permute-start = (bf16[128,512]{1,0:T(8,128)(2,1)S(1)}, bf16[128,512]{1,0:T(8,128)(2,1)S(1)}, u32[]{:S(2)}, u32[]{:S(2)}) collective-permute-start(bf16[128,512]{1,0:T(8,128)(2,1)S(1)} %get-tuple-element.29), channel_id=1, source_target_pairs={{0,2},{2,0},{1,3},{3,1},{4,6},{6,4},{5,7},{7,5},{8,10},{10,8},{9,1... | collective-permute-start | bytes 393224 | tf_op jit(solution)/shard_map/ppermute | solution.py:28
  11.9 24.5 %collective-permute-start.12 = (bf16[32,2176]{1,0:T(8,128)(2,1)S(1)}, bf16[32,2176]{1,0:T(8,128)(2,1)S(1)}, u32[]{:S(2)}, u32[]{:S(2)}) collective-permute-start(bf16[32,2176]{1,0:T(8,128)(2,1)S(1)} %pad_maximum_fusion.1), channel_id=1, source_target_pairs={{0,1},{1,0},{2,3},{3,2},{4,5},{5,4},{6,7},{7,6},{8,9},{9,8},{10,11... | collective-permute-start | bytes 417800 | tf_op jit(solution)/shard_map/ppermute | solution.py:28
  14.5 5.9 %collective-permute-start.1 = (bf16[64,512]{1,0:T(8,128)(2,1)S(1)}, bf16[64,512]{1,0:T(8,128)(2,1)S(1)}, u32[]{:S(2)}, u32[]{:S(2)}) collective-permute-start(bf16[64,512]{1,0:T(8,128)(2,1)S(1)} %get-tuple-element.36), channel_id=1, source_target_pairs={{0,4},{4,0},{8,12},{12,8},{1,5},{5,1},{9,13},{13,9},{2,6},{6,2},{1... | collective-permute-start | bytes 196616 | tf_op jit(solution)/shard_map/ppermute | solution.py:28
  15.2 7.9 %collective-permute-start.2 = (bf16[64,512]{1,0:T(8,128)(2,1)S(1)}, bf16[64,512]{1,0:T(8,128)(2,1)S(1)}, u32[]{:S(2)}, u32[]{:S(2)}) collective-permute-start(bf16[64,512]{1,0:T(8,128)(2,1)S(1)} %get-tuple-element.37), channel_id=1, source_target_pairs={{0,8},{4,12},{8,0},{12,4},{1,9},{5,13},{9,1},{13,5},{2,10},{6,14},... | collective-permute-start | bytes 196616 | tf_op jit(solution)/shard_map/ppermute | solution.py:28
  18.0 6.1 %collective-permute-start.3 = (bf16[64,512]{1,0:T(8,128)(2,1)S(1)}, bf16[64,512]{1,0:T(8,128)(2,1)S(1)}, u32[]{:S(2)}, u32[]{:S(2)}) collective-permute-start(bf16[64,512]{1,0:T(8,128)(2,1)S(1)} %get-tuple-element.38), channel_id=1, source_target_pairs={{0,12},{4,8},{8,4},{12,0},{1,13},{5,9},{9,5},{13,1},{2,14},{6,10},... | collective-permute-start | bytes 196616 | tf_op jit(solution)/shard_map/ppermute | solution.py:28
  25.3 4.5 %collective-permute-start.4 = (bf16[32,1024]{1,0:T(8,128)(2,1)S(1)}, bf16[32,1024]{1,0:T(8,128)(2,1)S(1)}, u32[]{:S(2)}, u32[]{:S(2)}) collective-permute-start(bf16[32,1024]{1,0:T(8,128)(2,1)S(1)} %get-tuple-element.43), channel_id=1, source_target_pairs={{0,4},{4,0},{8,12},{12,8},{1,5},{5,1},{9,13},{13,9},{2,6},{6,2},{1... | collective-permute-start | bytes 196616 | tf_op jit(solution)/shard_map/ppermute | solution.py:28
  26.5 6.8 %collective-permute-start.5 = (bf16[32,1024]{1,0:T(8,128)(2,1)S(1)}, bf16[32,1024]{1,0:T(8,128)(2,1)S(1)}, u32[]{:S(2)}, u32[]{:S(2)}) collective-permute-start(bf16[32,1024]{1,0:T(8,128)(2,1)S(1)} %get-tuple-element.44), channel_id=1, source_target_pairs={{0,8},{4,12},{8,0},{12,4},{1,9},{5,13},{9,1},{13,5},{2,10},{6,14},... | collective-permute-start | bytes 196616 | tf_op jit(solution)/shard_map/ppermute | solution.py:28
  28.2 6.2 %collective-permute-start.6 = (bf16[32,1024]{1,0:T(8,128)(2,1)S(1)}, bf16[32,1024]{1,0:T(8,128)(2,1)S(1)}, u32[]{:S(2)}, u32[]{:S(2)}) collective-permute-start(bf16[32,1024]{1,0:T(8,128)(2,1)S(1)} %get-tuple-element.45), channel_id=1, source_target_pairs={{0,12},{4,8},{8,4},{12,0},{1,13},{5,9},{9,5},{13,1},{2,14},{6,10},... | collective-permute-start | bytes 196616 | tf_op jit(solution)/shard_map/ppermute | solution.py:28
  34.5 3.7 %collective-permute-start.7 = (bf16[32,256]{1,0:T(8,128)(2,1)S(1)}, bf16[32,256]{1,0:T(8,128)(2,1)S(1)}, u32[]{:S(2)}, u32[]{:S(2)}) collective-permute-start(bf16[32,256]{1,0:T(8,128)(2,1)S(1)} %get-tuple-element.47), channel_id=1, source_target_pairs={{0,1},{1,0},{2,3},{3,2},{4,5},{5,4},{6,7},{7,6},{8,9},{9,8},{10,11... | collective-permute-start | bytes 49160 | tf_op jit(solution)/shard_map/ppermute | solution.py:28
  34.5 3.8 %collective-permute-start.8 = (bf16[32,256]{1,0:T(8,128)(2,1)S(1)}, bf16[32,256]{1,0:T(8,128)(2,1)S(1)}, u32[]{:S(2)}, u32[]{:S(2)}) collective-permute-start(bf16[32,256]{1,0:T(8,128)(2,1)S(1)} %get-tuple-element.48), channel_id=1, source_target_pairs={{0,2},{1,3},{2,0},{3,1},{4,6},{5,7},{6,4},{7,5},{8,10},{9,11},{10,... | collective-permute-start | bytes 49160 | tf_op jit(solution)/shard_map/ppermute | solution.py:28
  36.1 3.2 %collective-permute-start.9 = (bf16[32,256]{1,0:T(8,128)(2,1)S(1)}, bf16[32,256]{1,0:T(8,128)(2,1)S(1)}, u32[]{:S(2)}, u32[]{:S(2)}) collective-permute-start(bf16[32,256]{1,0:T(8,128)(2,1)S(1)} %get-tuple-element.49), channel_id=1, source_target_pairs={{0,3},{1,2},{2,1},{3,0},{4,7},{5,6},{6,5},{7,4},{8,11},{9,10},{10,... | collective-permute-start | bytes 49160 | tf_op jit(solution)/shard_map/ppermute | solution.py:28

commit v5 on v4

--- a/solution.py
+++ b/solution.py
@@ -268,29 +268,21 @@
     return values
 
 
-def line_kernel(n_z, per, blocks, quads, total_blocks, *refs):
-    chunks = refs[:n_z]
-    taps, turn, last = refs[n_z : n_z + 3]
-    outs = refs[n_z + 3 : 2 * n_z + 3]
-    sums, spun, rows = refs[2 * n_z + 3 :]
-    my_z = lax.axis_index("pulse")
+def line_rows(chunks, per, blocks, quads, total_blocks, taps, turn, last, rows, sums, spun):
     band = blocks * quads
-    pulses = n_z * per
+    pulses = len(chunks) * per
     ky = []
     for t in range(0, band, 16):
         groups = []
         for c in range(2):
-            for g in range(0, pulses, 8):
-                tiles = []
-                for k, p in (divmod(m, per) for m in range(g, g + 8)):
-                    tiles.append(
-                        chunks[k][
-                            c * band + t : c * band + t + 16, p * LANES : (p + 1) * LANES
-                        ].astype(F32)
-                    )
-                groups.append(
-                    swapped_rows([v[:8] for v in tiles]) + swapped_rows([v[8:] for v in tiles])
-                )
+            tiles = [
+                chunk[c * band + t : c * band + t + 16, p * LANES : (p + 1) * LANES].astype(F32)
+                for chunk in chunks
+                for p in range(per)
+            ]
+            groups.append(
+                swapped_rows([v[:8] for v in tiles]) + swapped_rows([v[8:] for v in tiles])
+            )
         for b in range(16 // quads):
             lhs = jnp.concatenate(
                 [
@@ -320,47 +312,70 @@
             at = (y + r * quarter) * pulses
             sums[0, at : at + pulses, :] = re
             sums[1, at : at + pulses, :] = im
-    fold = LANES // total_blocks
-    for g in range(0, pulses, 8):
-        for y in range(0, total_blocks, 16):
-            parts = []
-            for c in range(2):
-                halves = [
-                    swapped_rows(
-                        [sums[c, u * pulses + g : u * pulses + g + 8, :] for u in range(h, h + 8)]
-                    )
-                    for h in (y, y + 8)
-                ]
-                parts.append([jnp.concatenate(pair, axis=0) for pair in zip(*halves)])
-            for f in range(fold):
-                at = slice(f * total_blocks + y, f * total_blocks + y + 16)
-                tc, ts = turn[0, at, :], turn[1, at, :]
-                for i in range(8):
-                    re, im = parts[0][i], parts[1][i]
-                    spun[g + i, at, :LANES] = (re * tc - im * ts).astype(BF16)
-                    spun[g + i, at, LANES:] = (re * ts + im * tc).astype(BF16)
+    for y in range(0, total_blocks, 16):
+        parts = []
+        for c in range(2):
+            halves = [
+                swapped_rows([sums[c, u * pulses : (u + 1) * pulses, :] for u in range(h, h + 8)])
+                for h in (y, y + 8)
+            ]
+            parts.append([jnp.concatenate(pair, axis=0) for pair in zip(*halves)])
+        for f in range(LANES // total_blocks):
+            at = slice(f * total_blocks + y, f * total_blocks + y + 16)
+            tc, ts = turn[0, at, :], turn[1, at, :]
+            for i in range(pulses):
+                re, im = parts[0][i], parts[1][i]
+                spun[i, at, :LANES] = (re * tc - im * ts).astype(BF16)
+                spun[i, at, LANES:] = (re * ts + im * tc).astype(BF16)
     tops = last.shape[0] // 2
     for m in range(pulses):
         done = dot(last[...], spun[m], NT)
         for c in range(2):
             at = (c * pulses + m) * tops
             rows[at : at + tops, :] = done[c * tops : (c + 1) * tops, :]
+
+
+def cut_rows(n_z, per, tops, place, rows, k, group, c):
+    half = len(place) * per
     share = tops // n_z
+    base = (lax.axis_index("pulse") ^ k) * share
+    lanes = []
+    for s in range(0, share, 8):
+        tiles = []
+        for z in group:
+            for p in range(per):
+                at = (c * half + place.index(z ^ k) * per + p) * tops + s
+                tiles.append(rows[pl.ds(pl.multiple_of(at + base, 8), 8), :])
+        lanes += swapped_rows(tiles)
+    return jnp.concatenate(lanes, axis=1).astype(BF16)
+
+
+def line_head_kernel(n_z, dims, head, tail, one, two, taps, turn, last, early, sums, spun, rows):
+    line_rows((one, two), *dims, taps, turn, last, rows, sums, spun)
+    tops = last.shape[0] // 2
     for k in range(n_z):
-        for s in range(0, share, 8):
-            for c in range(2):
-                groups = []
-                for g in range(0, pulses, 8):
-                    tiles = []
-                    for z, p in (divmod(m, per) for m in range(g, g + 8)):
-                        at = (c * pulses + (z ^ k) * per + p) * tops + s
-                        at = pl.multiple_of(at + (my_z ^ k) * share, 8)
-                        tiles.append(rows[pl.ds(at, 8), :])
-                    groups.append(swapped_rows(tiles))
-                for i in range(8):
-                    outs[k][
-                        c * pulses : (c + 1) * pulses, (s + i) * LANES : (s + i + 1) * LANES
-                    ] = jnp.concatenate([g[i] for g in groups], axis=0).astype(BF16)
+        group = head if k in head else tail
+        for c in range(2):
+            early[k, c * 8 : (c + 1) * 8, :] = cut_rows(
+                n_z, dims[0], tops, head, rows, k, group, c
+            )
+
+
+def line_tail_kernel(n_z, dims, head, tail, *refs):
+    chunks, refs = refs[: len(tail)], refs[len(tail) :]
+    taps, turn, last, early = refs[:4]
+    outs = refs[4 : 4 + n_z]
+    sums, spun, rows = refs[4 + n_z :]
+    line_rows(chunks, *dims, taps, turn, last, rows, sums, spun)
+    tops = last.shape[0] // 2
+    for k in range(n_z):
+        first = 0 if k in head else 8
+        group = tail if k in head else head
+        for c in range(2):
+            at = c * 16 + first
+            outs[k][at : at + 8, :] = early[k, c * 8 : (c + 1) * 8, :]
+            at = c * 16 + 8 - first
+            outs[k][at : at + 8, :] = cut_rows(n_z, dims[0], tops, tail, rows, k, group, c)
 
 
 def fold_kernel(n_z, n_c, *refs):
@@ -417,24 +432,25 @@
     return order
 
 
-def factor(parts, n_z, n_x, n_c, per):
+def factor(parts, order, n_x, n_c, per):
+    n_z = len(order)
     pulses = n_z * per
     out = []
     for comp in range(2):
         for c in turned(n_c):
             for z in turned(n_z):
                 for x in range(n_x):
-                    at = comp * pulses + z * per
+                    at = comp * pulses + order.index(z) * per
                     out.append(parts[x * n_c + c][at : at + per, :])
     return jnp.concatenate(out, axis=0)
 
 
 def image_kernel(dims, step, *refs):
-    n_z, n_x, n_c, per = dims
+    order, n_x, n_c, per = dims
     count = n_x * n_c
     parts = [ref[...].astype(F32) for ref in refs[:count]]
     cols, out, held, sent = refs[count:]
-    lines = factor(parts, n_z, n_x, n_c, per).T
+    lines = factor(parts, order, n_x, n_c, per).T
     half = lines.shape[1] // 2
     re, im = lines[:, :half], lines[:, half:]
     rows = lines.shape[0]
@@ -613,25 +629,50 @@
         )(everyone, table, turn3)
 
     quads = block_bins // LANES
-    paired = blocks >= 4 and blocks * quads % 16 == 0 and tops // n_z % 8 == 0 and pulses % 16 == 0
+    paired = n_z == 4 and per == 4 and blocks >= 4 and blocks * quads % 16 == 0 and tops % 32 == 0
+    out_lines = [pltpu.VMEM((2 * pulses, grid // n_z), BF16)] * n_z
+    order = tuple(range(n_z))
     if paired:
-        line_make, first_scratch = line_kernel, []
-        spun = [pltpu.VMEM((pulses, LANES, 2 * LANES), BF16)]
+        head, tail = (0, 2), (1, 3)
+        order = head + tail
+        dims = (per, blocks, quads, total_blocks)
+        scratch = [
+            pltpu.VMEM((2, total_blocks * pulses // 2, LANES), F32),
+            pltpu.VMEM((pulses // 2, LANES, 2 * LANES), BF16),
+            pltpu.VMEM((pulses * tops, LANES), F32),
+        ]
+        early_rows = pl.pallas_call(
+            functools.partial(line_head_kernel, n_z, dims, head, tail),
+            in_specs=[VMEM] * 5,
+            out_specs=VMEM,
+            out_shape=pltpu.VMEM((n_z, pulses, grid // n_z), BF16),
+            scratch_shapes=scratch,
+            name="line_head",
+            **room,
+        )(*near(*(moved[k] for k in head), range_taps, turn2, last))
+        lines = pl.pallas_call(
+            functools.partial(line_tail_kernel, n_z, dims, head, tail),
+            in_specs=[VMEM] * 6,
+            out_specs=[VMEM] * n_z,
+            out_shape=out_lines,
+            scratch_shapes=scratch,
+            name="line_tail",
+            **room,
+        )(*near(*(moved[k] for k in tail), range_taps, turn2, last, early_rows))
     else:
-        line_make, spun = line_plain, []
-        first_scratch = [pltpu.VMEM((2 * pulses * blocks * quads, LANES), F32)]
-    lines = pl.pallas_call(
-        functools.partial(line_make, n_z, per, blocks, quads, total_blocks),
-        in_specs=[VMEM] * (n_z + 3),
-        out_specs=[VMEM] * n_z,
-        out_shape=[pltpu.VMEM((2 * pulses, grid // n_z), BF16)] * n_z,
-        scratch_shapes=first_scratch
-        + [pltpu.VMEM((2, total_blocks * pulses, LANES), F32)]
-        + spun
-        + [pltpu.VMEM((2 * pulses * tops, LANES), F32)],
-        name="line_transform",
-        **room,
-    )(*near(*moved, range_taps, turn2, last))
+        lines = pl.pallas_call(
+            functools.partial(line_plain, n_z, per, blocks, quads, total_blocks),
+            in_specs=[VMEM] * (n_z + 3),
+            out_specs=[VMEM] * n_z,
+            out_shape=out_lines,
+            scratch_shapes=[
+                pltpu.VMEM((2 * pulses * blocks * quads, LANES), F32),
+                pltpu.VMEM((2, total_blocks * pulses, LANES), F32),
+                pltpu.VMEM((2 * pulses * tops, LANES), F32),
+            ],
+            name="line_transform",
+            **room,
+        )(*near(*moved, range_taps, turn2, last))
     moved = [lines[0]]
     for k in range(1, n_z):
         moved.append(traded(lines[k], "pulse", k))
@@ -661,7 +702,7 @@
     out_shape = jax.ShapeDtypeStruct((2, out_rows, grid), F32)
     if cuts == 1 and wide:
         return pl.pallas_call(
-            functools.partial(image_kernel, (n_z, n_x, n_c, per), wide_x),
+            functools.partial(image_kernel, (order, n_x, n_c, per), wide_x),
             in_specs=[VMEM] * (quad + 1),
             out_specs=HELD,
             out_shape=out_shape,
@@ -672,7 +713,7 @@
             name="image",
             **room,
         )(*near(*parts, cols))
-    lines = factor([p.astype(F32) for p in parts], n_z, n_x, n_c, per).T
+    lines = factor([p.astype(F32) for p in parts], order, n_x, n_c, per).T
     re = lines[:, :all_pulses].reshape(out_rows, cuts, 1, group)
     im = lines[:, all_pulses:].reshape(out_rows, cuts, 1, group)
     lhs = jnp.stack(

time: 43.1 us -> 42.6 us (0.988)
  waiting for transfers between devices: 14 us -> 13.1 us
    ppermute x13, waiting for transfers between devices: 14 us -> 13.1 us  [traded(): return lax.ppermute(block, axis, [(i, i ^ k) for i in range(count)])]
    pallas_call x2 -> x3, Pallas kernels: 4.88 us -> 5.25 us  [the longest x1 3.71 us: program(): pl.pallas_call(functools.partial(image_kernel, (order, n_x, n_c, per), wi...]
  transfers between devices with their start and end apart: 13 -> 13, of which waited for: 9 -> 8; matrix products, arithmetic and copies ran while one was open for 0% -> 0% of each run, Pallas kernels for 14% -> 15%
where the time goes in v5:
time: 42.6 us; the launch traced here: 42.4 us
  starting transfers between devices  18 us (42%)
  waiting for transfers between devices  13.1 us (31%)
  Pallas kernels  11.1 us (26%)
    ppermute x13, starting transfers between devices, traded(): return lax.ppermute(block, axis, [(i, i ^ k) for i in range(count)])  18 us
    ppermute x13, waiting for transfers between devices, traded(): return lax.ppermute(block, axis, [(i, i ^ k) for i in range(count)])  13.1 us
    pallas_call x1, Pallas kernels, program(): pl.pallas_call(functools.partial(image_kernel, (order, n_x, n_c, per), wi...  3.71 us
    pallas_call x1, Pallas kernels, program(): pl.pallas_call(make, in_specs=[VMEM] * 3, out_specs=VMEM, out_shape=pltpu...  1.69 us
    pallas_call x1, Pallas kernels, program(): pl.pallas_call(functools.partial(bring_kernel, len(fixed)), in_specs=[HEL...  1.4 us
    pallas_call x1, Pallas kernels, program(): pl.pallas_call(functools.partial(ready_kernel, len(fixed)), in_specs=[VME...  1.11 us
    pallas_call x1, Pallas kernels, program(): pl.pallas_call(functools.partial(split_kernel, n_x, per), in_specs=[HELD]...  1.11 us
  transfers between devices with their start and end apart: 13, of which 8 were waited for; matrix products, arithmetic and copies ran while one was open for 0% of the time, Pallas kernels for 15%

profile of v5, /device:TPU:0, one launch (start us, length us, event | category | flops | bytes accessed | tf_op | source)
XLA Modules:
  0.0 42.4 jit_solution(15978035915305457792)
XLA Ops:
  0.0 1.1 %split.1 = (bf16[128,512]{1,0:T(8,128)(2,1)S(1)}, bf16[128,512]{1,0:T(8,128)(2,1)S(1)}, bf16[8,2176]{1,0:T(8,128)(2,1)S(1)}) custom-call(bf16[2,8,8192]{2,1,0:T(8,128)(2,1)} %raw.1, bf16[8,2048]{1,0:T(8,128)(2,1)} %taps_in.1, s32[1,8]{1,0:T(1,128)} %bitcast.1), custom_call_target="tpu_custom_call" | custom-call | tf_op jit(solution)/shard_map/split/pallas_call | solution.py:529
  1.1 4.1 %collective-permute-start.10 = (bf16[8,2176]{1,0:T(8,128)(2,1)S(1)}, bf16[8,2176]{1,0:T(8,128)(2,1)S(1)}, u32[]{:S(2)}, u32[]{:S(2)}) collective-permute-start(bf16[8,2176]{1,0:T(8,128)(2,1)S(1)} %get-tuple-element.50), channel_id=1, source_target_pairs={{0,8},{4,12},{8,0},{12,4},{1,9},{5,13},{9,1},{13,5},{2,10},{6,14},... | collective-permute-start | bytes 104456 | tf_op jit(solution)/shard_map/ppermute | solution.py:28
  5.2 2.3 %collective-permute-done.10 = bf16[8,2176]{1,0:T(8,128)(2,1)S(1)} collective-permute-done((bf16[8,2176]{1,0:T(8,128)(2,1)S(1)}, bf16[8,2176]{1,0:T(8,128)(2,1)S(1)}, u32[]{:S(2)}, u32[]{:S(2)}) %collective-permute-start.10) | collective-permute-done | bytes 34848 | tf_op jit(solution)/shard_map/ppermute | solution.py:28
  7.5 1.5 %collective-permute-start.11 = (bf16[16,2176]{1,0:T(8,128)(2,1)S(1)}, bf16[16,2176]{1,0:T(8,128)(2,1)S(1)}, u32[]{:S(2)}, u32[]{:S(2)}) collective-permute-start(bf16[16,2176]{1,0:T(8,128)(2,1)S(1)} %pad_maximum_fusion.2), channel_id=1, source_target_pairs={{0,4},{4,0},{8,12},{12,8},{1,5},{5,1},{9,13},{13,9},{2,6},{6,2},{1... | collective-permute-start | bytes 208904 | tf_op jit(solution)/shard_map/ppermute | solution.py:28
  9.1 1.5 %collective-permute-start = (bf16[128,512]{1,0:T(8,128)(2,1)S(1)}, bf16[128,512]{1,0:T(8,128)(2,1)S(1)}, u32[]{:S(2)}, u32[]{:S(2)}) collective-permute-start(bf16[128,512]{1,0:T(8,128)(2,1)S(1)} %get-tuple-element.29), channel_id=1, source_target_pairs={{0,2},{2,0},{1,3},{3,1},{4,6},{6,4},{5,7},{7,5},{8,10},{10,8},{9,1... | collective-permute-start | bytes 393224 | tf_op jit(solution)/shard_map/ppermute | solution.py:28
  10.6 1.3 %collective-permute-done.11 = bf16[16,2176]{1,0:T(8,128)(2,1)S(1)} collective-permute-done((bf16[16,2176]{1,0:T(8,128)(2,1)S(1)}, bf16[16,2176]{1,0:T(8,128)(2,1)S(1)}, u32[]{:S(2)}, u32[]{:S(2)}) %collective-permute-start.11) | collective-permute-done | bytes 69664 | tf_op jit(solution)/shard_map/ppermute | solution.py:28
  11.9 0.1 collective-permute-start.12
  11.9 1.1 %ready.1 = (f32[256,512]{1,0:T(8,128)S(1)}, bf16[1,256,128]{2,1,0:T(8,128)(2,1)S(1)}, f32[2,128,128]{2,1,0:T(8,128)S(1)}, bf16[256,256]{1,0:T(8,128)(2,1)S(1)}) custom-call(bf16[128,512]{1,0:T(8,128)(2,1)S(1)} %get-tuple-element.30.own, bf16[2,2,256,128]{3,2,1,0:T(8,128)(2,1)} %constant.14.clone.first, f32[2,128,128]{2,1,0:T(8,128)} %constant.15.clone.refs_0_, ...), custom_call_target="tpu_custom_call" | custom-call | tf_op jit(solution)/shard_map/ready/pallas_call | solution.py:556
  13.1 1.0 %collective-permute-done.refs_0_ = bf16[128,512]{1,0:T(8,128)(2,1)S(1)} collective-permute-done((bf16[128,512]{1,0:T(8,128)(2,1)S(1)}, bf16[128,512]{1,0:T(8,128)(2,1)S(1)}, u32[]{:S(2)}, u32[]{:S(2)}) %collective-permute-start) | collective-permute-done | bytes 131104 | tf_op jit(solution)/shard_map/ppermute | solution.py:28
  14.0 0.5 %pulse_transform.1 = (bf16[64,512]{1,0:T(8,128)(2,1)S(1)}, bf16[64,512]{1,0:T(8,128)(2,1)S(1)}, bf16[64,512]{1,0:T(8,128)(2,1)S(1)}, bf16[64,512]{1,0:T(8,128)(2,1)S(1)}) custom-call(bf16[128,512]{1,0:T(8,128)(2,1)S(1)} %collective-permute-done.refs_0_, f32[256,512]{1,0:T(8,128)S(1)} %get-tuple-element.31.refs_1_, ...), custom_call_target="tpu_custom_call" | custom-call | tf_op jit(solution)/shard_map/pulse_transform/pallas_call | solution.py:586
  14.5 2.9 %collective-permute-start.3 = (bf16[64,512]{1,0:T(8,128)(2,1)S(1)}, bf16[64,512]{1,0:T(8,128)(2,1)S(1)}, u32[]{:S(2)}, u32[]{:S(2)}) collective-permute-start(bf16[64,512]{1,0:T(8,128)(2,1)S(1)} %get-tuple-element.41), channel_id=1, source_target_pairs={{0,8},{4,12},{8,0},{12,4},{1,9},{5,13},{9,1},{13,5},{2,10},{6,14},... | collective-permute-start | bytes 196616 | tf_op jit(solution)/shard_map/ppermute | solution.py:28
  17.4 0.6 %collective-permute-start.1 = (bf16[64,512]{1,0:T(8,128)(2,1)S(1)}, bf16[64,512]{1,0:T(8,128)(2,1)S(1)}, u32[]{:S(2)}, u32[]{:S(2)}) collective-permute-start(bf16[64,512]{1,0:T(8,128)(2,1)S(1)} %get-tuple-element.35), channel_id=1, source_target_pairs={{0,4},{4,0},{8,12},{12,8},{1,5},{5,1},{9,13},{13,9},{2,6},{6,2},{1... | collective-permute-start | bytes 196616 | tf_op jit(solution)/shard_map/ppermute | solution.py:28
  18.0 1.0 %collective-permute-start.2 = (bf16[64,512]{1,0:T(8,128)(2,1)S(1)}, bf16[64,512]{1,0:T(8,128)(2,1)S(1)}, u32[]{:S(2)}, u32[]{:S(2)}) collective-permute-start(bf16[64,512]{1,0:T(8,128)(2,1)S(1)} %get-tuple-element.36), channel_id=1, source_target_pairs={{0,12},{4,8},{8,4},{12,0},{1,13},{5,9},{9,5},{13,1},{2,14},{6,10},... | collective-permute-start | bytes 196616 | tf_op jit(solution)/shard_map/ppermute | solution.py:28
  19.0 1.4 %bring.1 = (f32[2,128,128]{2,1,0:T(8,128)S(1)}, bf16[64,256]{1,0:T(8,128)(2,1)S(1)}, bf16[8,512,128]{2,1,0:T(8,128)(2,1)S(1)}, bf16[256,512]{1,0:T(8,128)(2,1)S(1)}, f32[2,16,256]{2,1,0:T(8,128)S(1)}) custom-call(f32[4,2,128,128]{3,2,1,0:T(8,128)} %constant.17.clone.turn, bf16[64,256]{1,0:T(8,128)(2,1)} %constant.18.clone.refs_0_, ...), custom_call_target="tpu_custom_call" | custom-call | tf_op jit(solution)/shard_map/bring/pallas_call | solution.py:573
  20.4 1.0 %collective-permute-done.3.two = bf16[64,512]{1,0:T(8,128)(2,1)S(1)} collective-permute-done((bf16[64,512]{1,0:T(8,128)(2,1)S(1)}, bf16[64,512]{1,0:T(8,128)(2,1)S(1)}, u32[]{:S(2)}, u32[]{:S(2)}) %collective-permute-start.3) | collective-permute-done | bytes 65568 | tf_op jit(solution)/shard_map/ppermute | solution.py:28
  21.4 0.8 %line_head.1.refs_5_ = bf16[4,16,1024]{2,1,0:T(8,128)(2,1)S(1)} custom-call(bf16[64,512]{1,0:T(8,128)(2,1)S(1)} %get-tuple-element.40.one, bf16[64,512]{1,0:T(8,128)(2,1)S(1)} %collective-permute-done.3.two, bf16[8,512,128]{2,1,0:T(8,128)(2,1)S(1)} %get-tuple-element.37.taps.refs_2_, f32[2,128,128]{2,1,0:T(8,128)S(1)} %get-tuple-element.38.turn.refs_3_, ...), custom_call_target="tpu_custom_call" | custom-call | tf_op jit(solution)/shard_map/line_head/pallas_call | solution.py:644
  22.2 1.9 %collective-permute-done.2.refs_1_ = bf16[64,512]{1,0:T(8,128)(2,1)S(1)} collective-permute-done((bf16[64,512]{1,0:T(8,128)(2,1)S(1)}, bf16[64,512]{1,0:T(8,128)(2,1)S(1)}, u32[]{:S(2)}, u32[]{:S(2)}) %collective-permute-start.2) | collective-permute-done | bytes 65568 | tf_op jit(solution)/shard_map/ppermute | solution.py:28
  24.1 0.8 %line_tail.1 = (bf16[32,1024]{1,0:T(8,128)(2,1)S(1)}, bf16[32,1024]{1,0:T(8,128)(2,1)S(1)}, bf16[32,1024]{1,0:T(8,128)(2,1)S(1)}, bf16[32,1024]{1,0:T(8,128)(2,1)S(1)}) custom-call(bf16[64,512]{1,0:T(8,128)(2,1)S(1)} %collective-permute-done.1.refs_0_, bf16[64,512]{1,0:T(8,128)(2,1)S(1)} %collective-permute-done.2.refs_1_, ...), custom_call_target="tpu_custom_call" | custom-call | tf_op jit(solution)/shard_map/line_tail/pallas_call | solution.py:653
  24.9 1.0 %collective-permute-start.4 = (bf16[32,1024]{1,0:T(8,128)(2,1)S(1)}, bf16[32,1024]{1,0:T(8,128)(2,1)S(1)}, u32[]{:S(2)}, u32[]{:S(2)}) collective-permute-start(bf16[32,1024]{1,0:T(8,128)(2,1)S(1)} %get-tuple-element.43), channel_id=1, source_target_pairs={{0,4},{4,0},{8,12},{12,8},{1,5},{5,1},{9,13},{13,9},{2,6},{6,2},{1... | collective-permute-start | bytes 196616 | tf_op jit(solution)/shard_map/ppermute | solution.py:28
  25.8 1.7 %collective-permute-start.5 = (bf16[32,1024]{1,0:T(8,128)(2,1)S(1)}, bf16[32,1024]{1,0:T(8,128)(2,1)S(1)}, u32[]{:S(2)}, u32[]{:S(2)}) collective-permute-start(bf16[32,1024]{1,0:T(8,128)(2,1)S(1)} %get-tuple-element.44), channel_id=1, source_target_pairs={{0,8},{4,12},{8,0},{12,4},{1,9},{5,13},{9,1},{13,5},{2,10},{6,14},... | collective-permute-start | bytes 196616 | tf_op jit(solution)/shard_map/ppermute | solution.py:28
  27.5 1.8 %collective-permute-start.6 = (bf16[32,1024]{1,0:T(8,128)(2,1)S(1)}, bf16[32,1024]{1,0:T(8,128)(2,1)S(1)}, u32[]{:S(2)}, u32[]{:S(2)}) collective-permute-start(bf16[32,1024]{1,0:T(8,128)(2,1)S(1)} %get-tuple-element.45), channel_id=1, source_target_pairs={{0,12},{4,8},{8,4},{12,0},{1,13},{5,9},{9,5},{13,1},{2,14},{6,10},... | collective-permute-start | bytes 196616 | tf_op jit(solution)/shard_map/ppermute | solution.py:28
  29.3 4.5 %collective-permute-done.5.refs_2_ = bf16[32,1024]{1,0:T(8,128)(2,1)S(1)} collective-permute-done((bf16[32,1024]{1,0:T(8,128)(2,1)S(1)}, bf16[32,1024]{1,0:T(8,128)(2,1)S(1)}, u32[]{:S(2)}, u32[]{:S(2)}) %collective-permute-start.5) | collective-permute-done | bytes 65568 | tf_op jit(solution)/shard_map/ppermute | solution.py:28
  33.8 0.0 collective-permute-done.6.refs_3_
  33.8 0.1 fold.1
  33.9 0.1 collective-permute-start.7
  34.0 1.6 %collective-permute-start.8 = (bf16[32,256]{1,0:T(8,128)(2,1)S(1)}, bf16[32,256]{1,0:T(8,128)(2,1)S(1)}, u32[]{:S(2)}, u32[]{:S(2)}) collective-permute-start(bf16[32,256]{1,0:T(8,128)(2,1)S(1)} %get-tuple-element.48), channel_id=1, source_target_pairs={{0,2},{1,3},{2,0},{3,1},{4,6},{5,7},{6,4},{7,5},{8,10},{9,11},{10,... | collective-permute-start | bytes 49160 | tf_op jit(solution)/shard_map/ppermute | solution.py:28
  35.6 0.2 collective-permute-start.9
  35.8 0.0 collective-permute-done.12
  35.8 1.7 %column_transform.1.refs_4_ = bf16[4096,128]{1,0:T(8,128)(2,1)S(1)} custom-call(bf16[64,2176]{1,0:T(8,128)(2,1)S(1)} %pad_maximum_fusion.taps, bf16[256,512]{1,0:T(8,128)(2,1)S(1)} %get-tuple-element.51.table, f32[2,16,256]{2,1,0:T(8,128)S(1)} %get-tuple-element.52.turn), custom_call_target="tpu_custom_call" | custom-call | tf_op jit(solution)/shard_map/column_transform/pallas_call | solution.py:607
  37.5 0.2 collective-permute-done.8.refs_2_
  37.8 1.0 %collective-permute-done.9.refs_3_ = bf16[32,256]{1,0:T(8,128)(2,1)S(1)} collective-permute-done((bf16[32,256]{1,0:T(8,128)(2,1)S(1)}, bf16[32,256]{1,0:T(8,128)(2,1)S(1)}, u32[]{:S(2)}, u32[]{:S(2)}) %collective-permute-start.9) | collective-permute-done | bytes 16416 | tf_op jit(solution)/shard_map/ppermute | solution.py:28
  38.7 3.7 %image.1 = f32[2,256,4096]{2,1,0:T(8,128)} custom-call(bf16[32,256]{1,0:T(8,128)(2,1)S(1)} %get-tuple-element.46.refs_0_, bf16[32,256]{1,0:T(8,128)(2,1)S(1)} %collective-permute-done.7.refs_1_, bf16[32,256]{1,0:T(8,128)(2,1)S(1)} %collective-permute-done.8.refs_2_, bf16[32,256]{1,0:T(8,128)(2,1)S(1)} %collective-permute-done.9.refs_3_, ...), custom_call_target="tpu_custom_call" | custom-call | tf_op jit(solution)/shard_map/image/pallas_call | solution.py:704
  (6 shorter events, 0.1 us)
Async XLA Ops:
  1.1 6.4 %collective-permute-start.10 = (bf16[8,2176]{1,0:T(8,128)(2,1)S(1)}, bf16[8,2176]{1,0:T(8,128)(2,1)S(1)}, u32[]{:S(2)}, u32[]{:S(2)}) collective-permute-start(bf16[8,2176]{1,0:T(8,128)(2,1)S(1)} %get-tuple-element.50), channel_id=1, source_target_pairs={{0,8},{4,12},{8,0},{12,4},{1,9},{5,13},{9,1},{13,5},{2,10},{6,14},... | collective-permute-start | bytes 104456 | tf_op jit(solution)/shard_map/ppermute | solution.py:28
  7.5 4.3 %collective-permute-start.11 = (bf16[16,2176]{1,0:T(8,128)(2,1)S(1)}, bf16[16,2176]{1,0:T(8,128)(2,1)S(1)}, u32[]{:S(2)}, u32[]{:S(2)}) collective-permute-start(bf16[16,2176]{1,0:T(8,128)(2,1)S(1)} %pad_maximum_fusion.2), channel_id=1, source_target_pairs={{0,4},{4,0},{8,12},{12,8},{1,5},{5,1},{9,13},{13,9},{2,6},{6,2},{1... | collective-permute-start | bytes 208904 | tf_op jit(solution)/shard_map/ppermute | solution.py:28
  9.1 5.0 %collective-permute-start = (bf16[128,512]{1,0:T(8,128)(2,1)S(1)}, bf16[128,512]{1,0:T(8,128)(2,1)S(1)}, u32[]{:S(2)}, u32[]{:S(2)}) collective-permute-start(bf16[128,512]{1,0:T(8,128)(2,1)S(1)} %get-tuple-element.29), channel_id=1, source_target_pairs={{0,2},{2,0},{1,3},{3,1},{4,6},{6,4},{5,7},{7,5},{8,10},{10,8},{9,1... | collective-permute-start | bytes 393224 | tf_op jit(solution)/shard_map/ppermute | solution.py:28
  11.9 23.9 %collective-permute-start.12 = (bf16[32,2176]{1,0:T(8,128)(2,1)S(1)}, bf16[32,2176]{1,0:T(8,128)(2,1)S(1)}, u32[]{:S(2)}, u32[]{:S(2)}) collective-permute-start(bf16[32,2176]{1,0:T(8,128)(2,1)S(1)} %pad_maximum_fusion.1), channel_id=1, source_target_pairs={{0,1},{1,0},{2,3},{3,2},{4,5},{5,4},{6,7},{7,6},{8,9},{9,8},{10,11... | collective-permute-start | bytes 417800 | tf_op jit(solution)/shard_map/ppermute | solution.py:28
  14.5 6.9 %collective-permute-start.3 = (bf16[64,512]{1,0:T(8,128)(2,1)S(1)}, bf16[64,512]{1,0:T(8,128)(2,1)S(1)}, u32[]{:S(2)}, u32[]{:S(2)}) collective-permute-start(bf16[64,512]{1,0:T(8,128)(2,1)S(1)} %get-tuple-element.41), channel_id=1, source_target_pairs={{0,8},{4,12},{8,0},{12,4},{1,9},{5,13},{9,1},{13,5},{2,10},{6,14},... | collective-permute-start | bytes 196616 | tf_op jit(solution)/shard_map/ppermute | solution.py:28
  17.4 4.8 %collective-permute-start.1 = (bf16[64,512]{1,0:T(8,128)(2,1)S(1)}, bf16[64,512]{1,0:T(8,128)(2,1)S(1)}, u32[]{:S(2)}, u32[]{:S(2)}) collective-permute-start(bf16[64,512]{1,0:T(8,128)(2,1)S(1)} %get-tuple-element.35), channel_id=1, source_target_pairs={{0,4},{4,0},{8,12},{12,8},{1,5},{5,1},{9,13},{13,9},{2,6},{6,2},{1... | collective-permute-start | bytes 196616 | tf_op jit(solution)/shard_map/ppermute | solution.py:28
  18.0 6.1 %collective-permute-start.2 = (bf16[64,512]{1,0:T(8,128)(2,1)S(1)}, bf16[64,512]{1,0:T(8,128)(2,1)S(1)}, u32[]{:S(2)}, u32[]{:S(2)}) collective-permute-start(bf16[64,512]{1,0:T(8,128)(2,1)S(1)} %get-tuple-element.36), channel_id=1, source_target_pairs={{0,12},{4,8},{8,4},{12,0},{1,13},{5,9},{9,5},{13,1},{2,14},{6,10},... | collective-permute-start | bytes 196616 | tf_op jit(solution)/shard_map/ppermute | solution.py:28
  24.9 4.5 %collective-permute-start.4 = (bf16[32,1024]{1,0:T(8,128)(2,1)S(1)}, bf16[32,1024]{1,0:T(8,128)(2,1)S(1)}, u32[]{:S(2)}, u32[]{:S(2)}) collective-permute-start(bf16[32,1024]{1,0:T(8,128)(2,1)S(1)} %get-tuple-element.43), channel_id=1, source_target_pairs={{0,4},{4,0},{8,12},{12,8},{1,5},{5,1},{9,13},{13,9},{2,6},{6,2},{1... | collective-permute-start | bytes 196616 | tf_op jit(solution)/shard_map/ppermute | solution.py:28
  25.8 8.0 %collective-permute-start.5 = (bf16[32,1024]{1,0:T(8,128)(2,1)S(1)}, bf16[32,1024]{1,0:T(8,128)(2,1)S(1)}, u32[]{:S(2)}, u32[]{:S(2)}) collective-permute-start(bf16[32,1024]{1,0:T(8,128)(2,1)S(1)} %get-tuple-element.44), channel_id=1, source_target_pairs={{0,8},{4,12},{8,0},{12,4},{1,9},{5,13},{9,1},{13,5},{2,10},{6,14},... | collective-permute-start | bytes 196616 | tf_op jit(solution)/shard_map/ppermute | solution.py:28
  27.5 6.3 %collective-permute-start.6 = (bf16[32,1024]{1,0:T(8,128)(2,1)S(1)}, bf16[32,1024]{1,0:T(8,128)(2,1)S(1)}, u32[]{:S(2)}, u32[]{:S(2)}) collective-permute-start(bf16[32,1024]{1,0:T(8,128)(2,1)S(1)} %get-tuple-element.45), channel_id=1, source_target_pairs={{0,12},{4,8},{8,4},{12,0},{1,13},{5,9},{9,5},{13,1},{2,14},{6,10},... | collective-permute-start | bytes 196616 | tf_op jit(solution)/shard_map/ppermute | solution.py:28
  33.9 3.7 %collective-permute-start.7 = (bf16[32,256]{1,0:T(8,128)(2,1)S(1)}, bf16[32,256]{1,0:T(8,128)(2,1)S(1)}, u32[]{:S(2)}, u32[]{:S(2)}) collective-permute-start(bf16[32,256]{1,0:T(8,128)(2,1)S(1)} %get-tuple-element.47), channel_id=1, source_target_pairs={{0,1},{1,0},{2,3},{3,2},{4,5},{5,4},{6,7},{7,6},{8,9},{9,8},{10,11... | collective-permute-start | bytes 49160 | tf_op jit(solution)/shard_map/ppermute | solution.py:28
  34.0 3.8 %collective-permute-start.8 = (bf16[32,256]{1,0:T(8,128)(2,1)S(1)}, bf16[32,256]{1,0:T(8,128)(2,1)S(1)}, u32[]{:S(2)}, u32[]{:S(2)}) collective-permute-start(bf16[32,256]{1,0:T(8,128)(2,1)S(1)} %get-tuple-element.48), channel_id=1, source_target_pairs={{0,2},{1,3},{2,0},{3,1},{4,6},{5,7},{6,4},{7,5},{8,10},{9,11},{10,... | collective-permute-start | bytes 49160 | tf_op jit(solution)/shard_map/ppermute | solution.py:28
  35.6 3.2 %collective-permute-start.9 = (bf16[32,256]{1,0:T(8,128)(2,1)S(1)}, bf16[32,256]{1,0:T(8,128)(2,1)S(1)}, u32[]{:S(2)}, u32[]{:S(2)}) collective-permute-start(bf16[32,256]{1,0:T(8,128)(2,1)S(1)} %get-tuple-element.49), channel_id=1, source_target_pairs={{0,3},{1,2},{2,1},{3,0},{4,7},{5,6},{6,5},{7,4},{8,11},{9,10},{10,... | collective-permute-start | bytes 49160 | tf_op jit(solution)/shard_map/ppermute | solution.py:28

commit v6 on v5

--- a/solution.py
+++ b/solution.py
@@ -335,30 +335,8 @@
             rows[at : at + tops, :] = done[c * tops : (c + 1) * tops, :]
 
 
-def cut_rows(n_z, per, tops, place, rows, k, group, c):
-    half = len(place) * per
-    share = tops // n_z
-    base = (lax.axis_index("pulse") ^ k) * share
-    lanes = []
-    for s in range(0, share, 8):
-        tiles = []
-        for z in group:
-            for p in range(per):
-                at = (c * half + place.index(z ^ k) * per + p) * tops + s
-                tiles.append(rows[pl.ds(pl.multiple_of(at + base, 8), 8), :])
-        lanes += swapped_rows(tiles)
-    return jnp.concatenate(lanes, axis=1).astype(BF16)
-
-
-def line_head_kernel(n_z, dims, head, tail, one, two, taps, turn, last, early, sums, spun, rows):
+def line_head_kernel(dims, one, two, taps, turn, last, rows, sums, spun):
     line_rows((one, two), *dims, taps, turn, last, rows, sums, spun)
-    tops = last.shape[0] // 2
-    for k in range(n_z):
-        group = head if k in head else tail
-        for c in range(2):
-            early[k, c * 8 : (c + 1) * 8, :] = cut_rows(
-                n_z, dims[0], tops, head, rows, k, group, c
-            )
 
 
 def line_tail_kernel(n_z, dims, head, tail, *refs):
@@ -367,15 +345,27 @@
     outs = refs[4 : 4 + n_z]
     sums, spun, rows = refs[4 + n_z :]
     line_rows(chunks, *dims, taps, turn, last, rows, sums, spun)
+    my_z = lax.axis_index("pulse")
+    per = dims[0]
     tops = last.shape[0] // 2
+    half, pulses = len(tail) * per, n_z * per
+    share = tops // n_z
     for k in range(n_z):
-        first = 0 if k in head else 8
-        group = tail if k in head else head
-        for c in range(2):
-            at = c * 16 + first
-            outs[k][at : at + 8, :] = early[k, c * 8 : (c + 1) * 8, :]
-            at = c * 16 + 8 - first
-            outs[k][at : at + 8, :] = cut_rows(n_z, dims[0], tops, tail, rows, k, group, c)
+        for s in range(0, share, 8):
+            for c in range(2):
+                groups = []
+                for g in range(0, pulses, 8):
+                    tiles = []
+                    for z, p in (divmod(m, per) for m in range(g, g + 8)):
+                        source, place = (early, head) if z ^ k in head else (rows, tail)
+                        at = (c * half + place.index(z ^ k) * per + p) * tops + s
+                        at = pl.multiple_of(at + (my_z ^ k) * share, 8)
+                        tiles.append(source[pl.ds(at, 8), :])
+                    groups.append(swapped_rows(tiles))
+                for i in range(8):
+                    outs[k][
+                        c * pulses : (c + 1) * pulses, (s + i) * LANES : (s + i + 1) * LANES
+                    ] = jnp.concatenate([g[i] for g in groups], axis=0).astype(BF16)
 
 
 def fold_kernel(n_z, n_c, *refs):
@@ -432,25 +422,24 @@
     return order
 
 
-def factor(parts, order, n_x, n_c, per):
-    n_z = len(order)
+def factor(parts, n_z, n_x, n_c, per):
     pulses = n_z * per
     out = []
     for comp in range(2):
         for c in turned(n_c):
             for z in turned(n_z):
                 for x in range(n_x):
-                    at = comp * pulses + order.index(z) * per
+                    at = comp * pulses + z * per
                     out.append(parts[x * n_c + c][at : at + per, :])
     return jnp.concatenate(out, axis=0)
 
 
 def image_kernel(dims, step, *refs):
-    order, n_x, n_c, per = dims
+    n_z, n_x, n_c, per = dims
     count = n_x * n_c
     parts = [ref[...].astype(F32) for ref in refs[:count]]
     cols, out, held, sent = refs[count:]
-    lines = factor(parts, order, n_x, n_c, per).T
+    lines = factor(parts, n_z, n_x, n_c, per).T
     half = lines.shape[1] // 2
     re, im = lines[:, :half], lines[:, half:]
     rows = lines.shape[0]
@@ -631,21 +620,19 @@
     quads = block_bins // LANES
     paired = n_z == 4 and per == 4 and blocks >= 4 and blocks * quads % 16 == 0 and tops % 32 == 0
     out_lines = [pltpu.VMEM((2 * pulses, grid // n_z), BF16)] * n_z
-    order = tuple(range(n_z))
     if paired:
         head, tail = (0, 2), (1, 3)
-        order = head + tail
         dims = (per, blocks, quads, total_blocks)
+        early = pltpu.VMEM((pulses * tops, LANES), F32)
         scratch = [
             pltpu.VMEM((2, total_blocks * pulses // 2, LANES), F32),
             pltpu.VMEM((pulses // 2, LANES, 2 * LANES), BF16),
-            pltpu.VMEM((pulses * tops, LANES), F32),
         ]
         early_rows = pl.pallas_call(
-            functools.partial(line_head_kernel, n_z, dims, head, tail),
+            functools.partial(line_head_kernel, dims),
             in_specs=[VMEM] * 5,
             out_specs=VMEM,
-            out_shape=pltpu.VMEM((n_z, pulses, grid // n_z), BF16),
+            out_shape=early,
             scratch_shapes=scratch,
             name="line_head",
             **room,
@@ -655,7 +642,7 @@
             in_specs=[VMEM] * 6,
             out_specs=[VMEM] * n_z,
             out_shape=out_lines,
-            scratch_shapes=scratch,
+            scratch_shapes=scratch + [early],
             name="line_tail",
             **room,
         )(*near(*(moved[k] for k in tail), range_taps, turn2, last, early_rows))
@@ -697,12 +684,12 @@
     for k in range(1, quad):
         parts.append(traded(pieces[k], ("range", "sub"), k))
 
-    wide_x = 512
+    wide_x = 256
     depth = 2 * all_pulses
     out_shape = jax.ShapeDtypeStruct((2, out_rows, grid), F32)
     if cuts == 1 and wide:
         return pl.pallas_call(
-            functools.partial(image_kernel, (order, n_x, n_c, per), wide_x),
+            functools.partial(image_kernel, (n_z, n_x, n_c, per), wide_x),
             in_specs=[VMEM] * (quad + 1),
             out_specs=HELD,
             out_shape=out_shape,
@@ -713,7 +700,7 @@
             name="image",
             **room,
         )(*near(*parts, cols))
-    lines = factor([p.astype(F32) for p in parts], order, n_x, n_c, per).T
+    lines = factor([p.astype(F32) for p in parts], n_z, n_x, n_c, per).T
     re = lines[:, :all_pulses].reshape(out_rows, cuts, 1, group)
     im = lines[:, all_pulses:].reshape(out_rows, cuts, 1, group)
     lhs = jnp.stack(

time: 42.6 us -> 42.7 us (level)
  no operation moved by 1% of the time
where the time goes in v6:
time: 42.7 us; the launch traced here: 42.5 us
  starting transfers between devices  18 us (42%)
  waiting for transfers between devices  13.2 us (31%)
  Pallas kernels  11.1 us (26%)
    ppermute x13, starting transfers between devices, traded(): return lax.ppermute(block, axis, [(i, i ^ k) for i in range(count)])  18 us
    ppermute x13, waiting for transfers between devices, traded(): return lax.ppermute(block, axis, [(i, i ^ k) for i in range(count)])  13.2 us
    pallas_call x1, Pallas kernels, program(): pl.pallas_call(functools.partial(image_kernel, (n_z, n_x, n_c, per), wide...  3.76 us
    pallas_call x1, Pallas kernels, program(): pl.pallas_call(make, in_specs=[VMEM] * 3, out_specs=VMEM, out_shape=pltpu...  1.69 us
    pallas_call x1, Pallas kernels, program(): pl.pallas_call(functools.partial(bring_kernel, len(fixed)), in_specs=[HEL...  1.4 us
    pallas_call x1, Pallas kernels, program(): pl.pallas_call(functools.partial(ready_kernel, len(fixed)), in_specs=[VME...  1.11 us
    pallas_call x1, Pallas kernels, program(): pl.pallas_call(functools.partial(split_kernel, n_x, per), in_specs=[HELD]...  1.11 us
  transfers between devices with their start and end apart: 13, of which 8 were waited for; matrix products, arithmetic and copies ran while one was open for 0% of the time, Pallas kernels for 15%

profile of v6, /device:TPU:0, one launch (start us, length us, event | category | flops | bytes accessed | tf_op | source)
XLA Modules:
  0.0 42.5 jit_solution(6353293285704184157)
XLA Ops:
  0.0 1.1 %split.1 = (bf16[128,512]{1,0:T(8,128)(2,1)S(1)}, bf16[128,512]{1,0:T(8,128)(2,1)S(1)}, bf16[8,2176]{1,0:T(8,128)(2,1)S(1)}) custom-call(bf16[2,8,8192]{2,1,0:T(8,128)(2,1)} %raw.1, bf16[8,2048]{1,0:T(8,128)(2,1)} %taps_in.1, s32[1,8]{1,0:T(1,128)} %bitcast.1), custom_call_target="tpu_custom_call" | custom-call | tf_op jit(solution)/shard_map/split/pallas_call | solution.py:518
  1.1 4.1 %collective-permute-start.10 = (bf16[8,2176]{1,0:T(8,128)(2,1)S(1)}, bf16[8,2176]{1,0:T(8,128)(2,1)S(1)}, u32[]{:S(2)}, u32[]{:S(2)}) collective-permute-start(bf16[8,2176]{1,0:T(8,128)(2,1)S(1)} %get-tuple-element.50), channel_id=1, source_target_pairs={{0,8},{4,12},{8,0},{12,4},{1,9},{5,13},{9,1},{13,5},{2,10},{6,14},... | collective-permute-start | bytes 104456 | tf_op jit(solution)/shard_map/ppermute | solution.py:28
  5.2 2.3 %collective-permute-done.10 = bf16[8,2176]{1,0:T(8,128)(2,1)S(1)} collective-permute-done((bf16[8,2176]{1,0:T(8,128)(2,1)S(1)}, bf16[8,2176]{1,0:T(8,128)(2,1)S(1)}, u32[]{:S(2)}, u32[]{:S(2)}) %collective-permute-start.10) | collective-permute-done | bytes 34848 | tf_op jit(solution)/shard_map/ppermute | solution.py:28
  7.5 1.5 %collective-permute-start.11 = (bf16[16,2176]{1,0:T(8,128)(2,1)S(1)}, bf16[16,2176]{1,0:T(8,128)(2,1)S(1)}, u32[]{:S(2)}, u32[]{:S(2)}) collective-permute-start(bf16[16,2176]{1,0:T(8,128)(2,1)S(1)} %pad_maximum_fusion.2), channel_id=1, source_target_pairs={{0,4},{4,0},{8,12},{12,8},{1,5},{5,1},{9,13},{13,9},{2,6},{6,2},{1... | collective-permute-start | bytes 208904 | tf_op jit(solution)/shard_map/ppermute | solution.py:28
  9.1 1.5 %collective-permute-start = (bf16[128,512]{1,0:T(8,128)(2,1)S(1)}, bf16[128,512]{1,0:T(8,128)(2,1)S(1)}, u32[]{:S(2)}, u32[]{:S(2)}) collective-permute-start(bf16[128,512]{1,0:T(8,128)(2,1)S(1)} %get-tuple-element.29), channel_id=1, source_target_pairs={{0,2},{2,0},{1,3},{3,1},{4,6},{6,4},{5,7},{7,5},{8,10},{10,8},{9,1... | collective-permute-start | bytes 393224 | tf_op jit(solution)/shard_map/ppermute | solution.py:28
  10.6 1.3 %collective-permute-done.11 = bf16[16,2176]{1,0:T(8,128)(2,1)S(1)} collective-permute-done((bf16[16,2176]{1,0:T(8,128)(2,1)S(1)}, bf16[16,2176]{1,0:T(8,128)(2,1)S(1)}, u32[]{:S(2)}, u32[]{:S(2)}) %collective-permute-start.11) | collective-permute-done | bytes 69664 | tf_op jit(solution)/shard_map/ppermute | solution.py:28
  11.9 0.1 collective-permute-start.12
  11.9 1.1 %ready.1 = (f32[256,512]{1,0:T(8,128)S(1)}, bf16[1,256,128]{2,1,0:T(8,128)(2,1)S(1)}, f32[2,128,128]{2,1,0:T(8,128)S(1)}, bf16[256,256]{1,0:T(8,128)(2,1)S(1)}) custom-call(bf16[128,512]{1,0:T(8,128)(2,1)S(1)} %get-tuple-element.30.own, bf16[2,2,256,128]{3,2,1,0:T(8,128)(2,1)} %constant.14.clone.first, f32[2,128,128]{2,1,0:T(8,128)} %constant.15.clone.refs_0_, ...), custom_call_target="tpu_custom_call" | custom-call | tf_op jit(solution)/shard_map/ready/pallas_call | solution.py:545
  13.1 1.0 %collective-permute-done.refs_0_ = bf16[128,512]{1,0:T(8,128)(2,1)S(1)} collective-permute-done((bf16[128,512]{1,0:T(8,128)(2,1)S(1)}, bf16[128,512]{1,0:T(8,128)(2,1)S(1)}, u32[]{:S(2)}, u32[]{:S(2)}) %collective-permute-start) | collective-permute-done | bytes 131104 | tf_op jit(solution)/shard_map/ppermute | solution.py:28
  14.0 0.5 %pulse_transform.1 = (bf16[64,512]{1,0:T(8,128)(2,1)S(1)}, bf16[64,512]{1,0:T(8,128)(2,1)S(1)}, bf16[64,512]{1,0:T(8,128)(2,1)S(1)}, bf16[64,512]{1,0:T(8,128)(2,1)S(1)}) custom-call(bf16[128,512]{1,0:T(8,128)(2,1)S(1)} %collective-permute-done.refs_0_, f32[256,512]{1,0:T(8,128)S(1)} %get-tuple-element.31.refs_1_, ...), custom_call_target="tpu_custom_call" | custom-call | tf_op jit(solution)/shard_map/pulse_transform/pallas_call | solution.py:575
  14.5 2.9 %collective-permute-start.3 = (bf16[64,512]{1,0:T(8,128)(2,1)S(1)}, bf16[64,512]{1,0:T(8,128)(2,1)S(1)}, u32[]{:S(2)}, u32[]{:S(2)}) collective-permute-start(bf16[64,512]{1,0:T(8,128)(2,1)S(1)} %get-tuple-element.41), channel_id=1, source_target_pairs={{0,8},{4,12},{8,0},{12,4},{1,9},{5,13},{9,1},{13,5},{2,10},{6,14},... | collective-permute-start | bytes 196616 | tf_op jit(solution)/shard_map/ppermute | solution.py:28
  17.4 0.6 %collective-permute-start.1 = (bf16[64,512]{1,0:T(8,128)(2,1)S(1)}, bf16[64,512]{1,0:T(8,128)(2,1)S(1)}, u32[]{:S(2)}, u32[]{:S(2)}) collective-permute-start(bf16[64,512]{1,0:T(8,128)(2,1)S(1)} %get-tuple-element.35), channel_id=1, source_target_pairs={{0,4},{4,0},{8,12},{12,8},{1,5},{5,1},{9,13},{13,9},{2,6},{6,2},{1... | collective-permute-start | bytes 196616 | tf_op jit(solution)/shard_map/ppermute | solution.py:28
  18.0 1.0 %collective-permute-start.2 = (bf16[64,512]{1,0:T(8,128)(2,1)S(1)}, bf16[64,512]{1,0:T(8,128)(2,1)S(1)}, u32[]{:S(2)}, u32[]{:S(2)}) collective-permute-start(bf16[64,512]{1,0:T(8,128)(2,1)S(1)} %get-tuple-element.36), channel_id=1, source_target_pairs={{0,12},{4,8},{8,4},{12,0},{1,13},{5,9},{9,5},{13,1},{2,14},{6,10},... | collective-permute-start | bytes 196616 | tf_op jit(solution)/shard_map/ppermute | solution.py:28
  19.0 1.4 %bring.1 = (f32[2,128,128]{2,1,0:T(8,128)S(1)}, bf16[64,256]{1,0:T(8,128)(2,1)S(1)}, bf16[8,512,128]{2,1,0:T(8,128)(2,1)S(1)}, bf16[256,512]{1,0:T(8,128)(2,1)S(1)}, f32[2,16,256]{2,1,0:T(8,128)S(1)}) custom-call(f32[4,2,128,128]{3,2,1,0:T(8,128)} %constant.17.clone.turn, bf16[64,256]{1,0:T(8,128)(2,1)} %constant.18.clone.refs_0_, ...), custom_call_target="tpu_custom_call" | custom-call | tf_op jit(solution)/shard_map/bring/pallas_call | solution.py:562
  20.4 1.0 %collective-permute-done.3.two = bf16[64,512]{1,0:T(8,128)(2,1)S(1)} collective-permute-done((bf16[64,512]{1,0:T(8,128)(2,1)S(1)}, bf16[64,512]{1,0:T(8,128)(2,1)S(1)}, u32[]{:S(2)}, u32[]{:S(2)}) %collective-permute-start.3) | collective-permute-done | bytes 65568 | tf_op jit(solution)/shard_map/ppermute | solution.py:28
  21.4 0.7 %line_head.1.refs_5_ = f32[512,128]{1,0:T(8,128)S(1)} custom-call(bf16[64,512]{1,0:T(8,128)(2,1)S(1)} %get-tuple-element.40.one, bf16[64,512]{1,0:T(8,128)(2,1)S(1)} %collective-permute-done.3.two, bf16[8,512,128]{2,1,0:T(8,128)(2,1)S(1)} %get-tuple-element.37.taps.refs_2_, f32[2,128,128]{2,1,0:T(8,128)S(1)} %get-tuple-element.38.turn.refs_3_, ...), custom_call_target="tpu_custom_call" | custom-call | tf_op jit(solution)/shard_map/line_head/pallas_call | solution.py:631
  22.1 0.0 collective-permute-done.1.refs_0_
  22.1 1.9 %collective-permute-done.2.refs_1_ = bf16[64,512]{1,0:T(8,128)(2,1)S(1)} collective-permute-done((bf16[64,512]{1,0:T(8,128)(2,1)S(1)}, bf16[64,512]{1,0:T(8,128)(2,1)S(1)}, u32[]{:S(2)}, u32[]{:S(2)}) %collective-permute-start.2) | collective-permute-done | bytes 65568 | tf_op jit(solution)/shard_map/ppermute | solution.py:28
  24.1 0.8 %line_tail.1 = (bf16[32,1024]{1,0:T(8,128)(2,1)S(1)}, bf16[32,1024]{1,0:T(8,128)(2,1)S(1)}, bf16[32,1024]{1,0:T(8,128)(2,1)S(1)}, bf16[32,1024]{1,0:T(8,128)(2,1)S(1)}) custom-call(bf16[64,512]{1,0:T(8,128)(2,1)S(1)} %collective-permute-done.1.refs_0_, bf16[64,512]{1,0:T(8,128)(2,1)S(1)} %collective-permute-done.2.refs_1_, ...), custom_call_target="tpu_custom_call" | custom-call | tf_op jit(solution)/shard_map/line_tail/pallas_call | solution.py:640
  24.9 1.0 %collective-permute-start.4 = (bf16[32,1024]{1,0:T(8,128)(2,1)S(1)}, bf16[32,1024]{1,0:T(8,128)(2,1)S(1)}, u32[]{:S(2)}, u32[]{:S(2)}) collective-permute-start(bf16[32,1024]{1,0:T(8,128)(2,1)S(1)} %get-tuple-element.43), channel_id=1, source_target_pairs={{0,4},{4,0},{8,12},{12,8},{1,5},{5,1},{9,13},{13,9},{2,6},{6,2},{1... | collective-permute-start | bytes 196616 | tf_op jit(solution)/shard_map/ppermute | solution.py:28
  25.9 1.7 %collective-permute-start.5 = (bf16[32,1024]{1,0:T(8,128)(2,1)S(1)}, bf16[32,1024]{1,0:T(8,128)(2,1)S(1)}, u32[]{:S(2)}, u32[]{:S(2)}) collective-permute-start(bf16[32,1024]{1,0:T(8,128)(2,1)S(1)} %get-tuple-element.44), channel_id=1, source_target_pairs={{0,8},{4,12},{8,0},{12,4},{1,9},{5,13},{9,1},{13,5},{2,10},{6,14},... | collective-permute-start | bytes 196616 | tf_op jit(solution)/shard_map/ppermute | solution.py:28
  27.6 1.8 %collective-permute-start.6 = (bf16[32,1024]{1,0:T(8,128)(2,1)S(1)}, bf16[32,1024]{1,0:T(8,128)(2,1)S(1)}, u32[]{:S(2)}, u32[]{:S(2)}) collective-permute-start(bf16[32,1024]{1,0:T(8,128)(2,1)S(1)} %get-tuple-element.45), channel_id=1, source_target_pairs={{0,12},{4,8},{8,4},{12,0},{1,13},{5,9},{9,5},{13,1},{2,14},{6,10},... | collective-permute-start | bytes 196616 | tf_op jit(solution)/shard_map/ppermute | solution.py:28
  29.3 0.0 collective-permute-done.4.refs_1_
  29.3 4.5 %collective-permute-done.5.refs_2_ = bf16[32,1024]{1,0:T(8,128)(2,1)S(1)} collective-permute-done((bf16[32,1024]{1,0:T(8,128)(2,1)S(1)}, bf16[32,1024]{1,0:T(8,128)(2,1)S(1)}, u32[]{:S(2)}, u32[]{:S(2)}) %collective-permute-start.5) | collective-permute-done | bytes 65568 | tf_op jit(solution)/shard_map/ppermute | solution.py:28
  33.9 0.1 fold.1
  33.9 0.1 collective-permute-start.7
  34.0 1.6 %collective-permute-start.8 = (bf16[32,256]{1,0:T(8,128)(2,1)S(1)}, bf16[32,256]{1,0:T(8,128)(2,1)S(1)}, u32[]{:S(2)}, u32[]{:S(2)}) collective-permute-start(bf16[32,256]{1,0:T(8,128)(2,1)S(1)} %get-tuple-element.48), channel_id=1, source_target_pairs={{0,2},{1,3},{2,0},{3,1},{4,6},{5,7},{6,4},{7,5},{8,10},{9,11},{10,... | collective-permute-start | bytes 49160 | tf_op jit(solution)/shard_map/ppermute | solution.py:28
  35.6 0.2 collective-permute-start.9
  35.9 1.7 %column_transform.1.refs_4_ = bf16[4096,128]{1,0:T(8,128)(2,1)S(1)} custom-call(bf16[64,2176]{1,0:T(8,128)(2,1)S(1)} %pad_maximum_fusion.taps, bf16[256,512]{1,0:T(8,128)(2,1)S(1)} %get-tuple-element.51.table, f32[2,16,256]{2,1,0:T(8,128)S(1)} %get-tuple-element.52.turn), custom_call_target="tpu_custom_call" | custom-call | tf_op jit(solution)/shard_map/column_transform/pallas_call | solution.py:596
  37.6 0.2 collective-permute-done.8.refs_2_
  37.8 1.0 %collective-permute-done.9.refs_3_ = bf16[32,256]{1,0:T(8,128)(2,1)S(1)} collective-permute-done((bf16[32,256]{1,0:T(8,128)(2,1)S(1)}, bf16[32,256]{1,0:T(8,128)(2,1)S(1)}, u32[]{:S(2)}, u32[]{:S(2)}) %collective-permute-start.9) | collective-permute-done | bytes 16416 | tf_op jit(solution)/shard_map/ppermute | solution.py:28
  38.8 3.8 %image.1 = f32[2,256,4096]{2,1,0:T(8,128)} custom-call(bf16[32,256]{1,0:T(8,128)(2,1)S(1)} %get-tuple-element.46.refs_0_, bf16[32,256]{1,0:T(8,128)(2,1)S(1)} %collective-permute-done.7.refs_1_, bf16[32,256]{1,0:T(8,128)(2,1)S(1)} %collective-permute-done.8.refs_2_, bf16[32,256]{1,0:T(8,128)(2,1)S(1)} %collective-permute-done.9.refs_3_, ...), custom_call_target="tpu_custom_call" | custom-call | tf_op jit(solution)/shard_map/image/pallas_call | solution.py:691
  (6 shorter events, 0.1 us)
Async XLA Ops:
  1.1 6.4 %collective-permute-start.10 = (bf16[8,2176]{1,0:T(8,128)(2,1)S(1)}, bf16[8,2176]{1,0:T(8,128)(2,1)S(1)}, u32[]{:S(2)}, u32[]{:S(2)}) collective-permute-start(bf16[8,2176]{1,0:T(8,128)(2,1)S(1)} %get-tuple-element.50), channel_id=1, source_target_pairs={{0,8},{4,12},{8,0},{12,4},{1,9},{5,13},{9,1},{13,5},{2,10},{6,14},... | collective-permute-start | bytes 104456 | tf_op jit(solution)/shard_map/ppermute | solution.py:28
  7.5 4.3 %collective-permute-start.11 = (bf16[16,2176]{1,0:T(8,128)(2,1)S(1)}, bf16[16,2176]{1,0:T(8,128)(2,1)S(1)}, u32[]{:S(2)}, u32[]{:S(2)}) collective-permute-start(bf16[16,2176]{1,0:T(8,128)(2,1)S(1)} %pad_maximum_fusion.2), channel_id=1, source_target_pairs={{0,4},{4,0},{8,12},{12,8},{1,5},{5,1},{9,13},{13,9},{2,6},{6,2},{1... | collective-permute-start | bytes 208904 | tf_op jit(solution)/shard_map/ppermute | solution.py:28
  9.1 5.0 %collective-permute-start = (bf16[128,512]{1,0:T(8,128)(2,1)S(1)}, bf16[128,512]{1,0:T(8,128)(2,1)S(1)}, u32[]{:S(2)}, u32[]{:S(2)}) collective-permute-start(bf16[128,512]{1,0:T(8,128)(2,1)S(1)} %get-tuple-element.29), channel_id=1, source_target_pairs={{0,2},{2,0},{1,3},{3,1},{4,6},{6,4},{5,7},{7,5},{8,10},{10,8},{9,1... | collective-permute-start | bytes 393224 | tf_op jit(solution)/shard_map/ppermute | solution.py:28
  11.9 24.0 %collective-permute-start.12 = (bf16[32,2176]{1,0:T(8,128)(2,1)S(1)}, bf16[32,2176]{1,0:T(8,128)(2,1)S(1)}, u32[]{:S(2)}, u32[]{:S(2)}) collective-permute-start(bf16[32,2176]{1,0:T(8,128)(2,1)S(1)} %pad_maximum_fusion.1), channel_id=1, source_target_pairs={{0,1},{1,0},{2,3},{3,2},{4,5},{5,4},{6,7},{7,6},{8,9},{9,8},{10,11... | collective-permute-start | bytes 417800 | tf_op jit(solution)/shard_map/ppermute | solution.py:28
  14.5 6.9 %collective-permute-start.3 = (bf16[64,512]{1,0:T(8,128)(2,1)S(1)}, bf16[64,512]{1,0:T(8,128)(2,1)S(1)}, u32[]{:S(2)}, u32[]{:S(2)}) collective-permute-start(bf16[64,512]{1,0:T(8,128)(2,1)S(1)} %get-tuple-element.41), channel_id=1, source_target_pairs={{0,8},{4,12},{8,0},{12,4},{1,9},{5,13},{9,1},{13,5},{2,10},{6,14},... | collective-permute-start | bytes 196616 | tf_op jit(solution)/shard_map/ppermute | solution.py:28
  17.4 4.7 %collective-permute-start.1 = (bf16[64,512]{1,0:T(8,128)(2,1)S(1)}, bf16[64,512]{1,0:T(8,128)(2,1)S(1)}, u32[]{:S(2)}, u32[]{:S(2)}) collective-permute-start(bf16[64,512]{1,0:T(8,128)(2,1)S(1)} %get-tuple-element.35), channel_id=1, source_target_pairs={{0,4},{4,0},{8,12},{12,8},{1,5},{5,1},{9,13},{13,9},{2,6},{6,2},{1... | collective-permute-start | bytes 196616 | tf_op jit(solution)/shard_map/ppermute | solution.py:28
  18.0 6.1 %collective-permute-start.2 = (bf16[64,512]{1,0:T(8,128)(2,1)S(1)}, bf16[64,512]{1,0:T(8,128)(2,1)S(1)}, u32[]{:S(2)}, u32[]{:S(2)}) collective-permute-start(bf16[64,512]{1,0:T(8,128)(2,1)S(1)} %get-tuple-element.36), channel_id=1, source_target_pairs={{0,12},{4,8},{8,4},{12,0},{1,13},{5,9},{9,5},{13,1},{2,14},{6,10},... | collective-permute-start | bytes 196616 | tf_op jit(solution)/shard_map/ppermute | solution.py:28
  24.9 4.5 %collective-permute-start.4 = (bf16[32,1024]{1,0:T(8,128)(2,1)S(1)}, bf16[32,1024]{1,0:T(8,128)(2,1)S(1)}, u32[]{:S(2)}, u32[]{:S(2)}) collective-permute-start(bf16[32,1024]{1,0:T(8,128)(2,1)S(1)} %get-tuple-element.43), channel_id=1, source_target_pairs={{0,4},{4,0},{8,12},{12,8},{1,5},{5,1},{9,13},{13,9},{2,6},{6,2},{1... | collective-permute-start | bytes 196616 | tf_op jit(solution)/shard_map/ppermute | solution.py:28
  25.9 8.0 %collective-permute-start.5 = (bf16[32,1024]{1,0:T(8,128)(2,1)S(1)}, bf16[32,1024]{1,0:T(8,128)(2,1)S(1)}, u32[]{:S(2)}, u32[]{:S(2)}) collective-permute-start(bf16[32,1024]{1,0:T(8,128)(2,1)S(1)} %get-tuple-element.44), channel_id=1, source_target_pairs={{0,8},{4,12},{8,0},{12,4},{1,9},{5,13},{9,1},{13,5},{2,10},{6,14},... | collective-permute-start | bytes 196616 | tf_op jit(solution)/shard_map/ppermute | solution.py:28
  27.6 6.3 %collective-permute-start.6 = (bf16[32,1024]{1,0:T(8,128)(2,1)S(1)}, bf16[32,1024]{1,0:T(8,128)(2,1)S(1)}, u32[]{:S(2)}, u32[]{:S(2)}) collective-permute-start(bf16[32,1024]{1,0:T(8,128)(2,1)S(1)} %get-tuple-element.45), channel_id=1, source_target_pairs={{0,12},{4,8},{8,4},{12,0},{1,13},{5,9},{9,5},{13,1},{2,14},{6,10},... | collective-permute-start | bytes 196616 | tf_op jit(solution)/shard_map/ppermute | solution.py:28
  33.9 3.7 %collective-permute-start.7 = (bf16[32,256]{1,0:T(8,128)(2,1)S(1)}, bf16[32,256]{1,0:T(8,128)(2,1)S(1)}, u32[]{:S(2)}, u32[]{:S(2)}) collective-permute-start(bf16[32,256]{1,0:T(8,128)(2,1)S(1)} %get-tuple-element.47), channel_id=1, source_target_pairs={{0,1},{1,0},{2,3},{3,2},{4,5},{5,4},{6,7},{7,6},{8,9},{9,8},{10,11... | collective-permute-start | bytes 49160 | tf_op jit(solution)/shard_map/ppermute | solution.py:28
  34.0 3.8 %collective-permute-start.8 = (bf16[32,256]{1,0:T(8,128)(2,1)S(1)}, bf16[32,256]{1,0:T(8,128)(2,1)S(1)}, u32[]{:S(2)}, u32[]{:S(2)}) collective-permute-start(bf16[32,256]{1,0:T(8,128)(2,1)S(1)} %get-tuple-element.48), channel_id=1, source_target_pairs={{0,2},{1,3},{2,0},{3,1},{4,6},{5,7},{6,4},{7,5},{8,10},{9,11},{10,... | collective-permute-start | bytes 49160 | tf_op jit(solution)/shard_map/ppermute | solution.py:28
  35.6 3.2 %collective-permute-start.9 = (bf16[32,256]{1,0:T(8,128)(2,1)S(1)}, bf16[32,256]{1,0:T(8,128)(2,1)S(1)}, u32[]{:S(2)}, u32[]{:S(2)}) collective-permute-start(bf16[32,256]{1,0:T(8,128)(2,1)S(1)} %get-tuple-element.49), channel_id=1, source_target_pairs={{0,3},{1,2},{2,1},{3,0},{4,7},{5,6},{6,5},{7,4},{8,11},{9,10},{10,... | collective-permute-start | bytes 49160 | tf_op jit(solution)/shard_map/ppermute | solution.py:28
